TPU v7x, 32 devices: a whole 2x2x4 slice. The times are simulated.
32 devices in a mesh: case: 2 (over y), phase: 4 (over x, core), slab: 4 (over z).
Axes of the slice: x: 2, y: 2, z: 4, core: 2. Of those that a mesh axis runs over, the one named last changes fastest.
Arguments:
- fine_images: float32 [8, 64, 128, 512], P(('case', 'phase'), 'slab'), parts along dimension 0, may hold values from -6 to 6
- offsets: int32 [8, 3, 32, 64, 256], P(('case', 'phase'), None, 'slab'), parts along dimension 0, may hold values from -4 to 4
- velocity_init: float32 [8, 3, 32, 64, 256], P(('case', 'phase'), None, 'slab'), parts along dimension 0, may hold values from -3 to 3
Outputs:
- velocity: float32 [8, 3, 32, 64, 256], P(('case', 'phase'), None, 'slab'), parts along dimension 0
There are 2 independent parts, one for each index of `case`. A program takes and returns all parts, laid end to end along the dimension named above; each array names one. Nothing has to cross between parts.
All inputs are finite; a program needn't handle non-finite values.
Results may differ from a plain program's by a relative error of at most 0.000076.
Values sent between devices are 32-bit elements; how exact they have to be, the bound alone decides.
No kernel may reach another device: no remote copies, remote signals or barrier semaphores. Data moves between devices by JAX's collectives and lax.ppermute only.
A program may use at most 64 MiB of HBM per device.

v0:
```python
import jax
import jax.numpy as jnp
from jax import lax
from jax.sharding import PartitionSpec as P

ITERS = 2


highest = lax.Precision.HIGHEST


def extended(cells, sides, width):
    for axis, dim in sides:
        count = lax.axis_size(axis)
        ends = count - 1
        head = lax.slice_in_dim(cells, 0, width, axis=dim)
        tail = lax.slice_in_dim(cells, cells.shape[dim] - width, cells.shape[dim], axis=dim)
        cells = jnp.concatenate(
            [
                lax.ppermute(tail, axis, [(i, (i + 1) % count) for i in range(ends)]),
                cells,
                lax.ppermute(head, axis, [((i + 1) % count, i) for i in range(ends)]),
            ],
            axis=dim,
        )
    return cells


def passed_along(block, axis, distance):
    devices = range(lax.axis_size(axis))
    route = [((i - distance) % len(devices), i) for i in devices]
    return lax.ppermute(block, axis, route)


def pad_axis(values, dimension, width):
    widths = [(0, 0)] * values.ndim
    widths[dimension] = (width, width)
    return jnp.pad(values, widths)


def halve_matrix(length):
    fine_index = lax.broadcasted_iota(jnp.int32, (length, length // 2), 0)
    coarse_index = lax.broadcasted_iota(jnp.int32, (length, length // 2), 1)
    outer = (fine_index == 2 * coarse_index - 1) | (fine_index == 2 * coarse_index + 2)
    inner = (fine_index == 2 * coarse_index) | (fine_index == 2 * coarse_index + 1)
    return jnp.where(inner, 0.375, jnp.where(outer, 0.125, 0.0)).astype(jnp.float32)


def smooth_matrix(length):
    source = lax.broadcasted_iota(jnp.int32, (length, length), 0)
    result = lax.broadcasted_iota(jnp.int32, (length, length), 1)
    return jnp.where(
        source == result, 0.5, jnp.where(jnp.abs(source - result) == 1, 0.25, 0.0)
    ).astype(jnp.float32)


def gradient_matrix(length):
    source = lax.broadcasted_iota(jnp.int32, (length, length), 0)
    result = lax.broadcasted_iota(jnp.int32, (length, length), 1)
    return jnp.where(source == result + 1, 0.5, jnp.where(source == result - 1, -0.5, 0.0)).astype(
        jnp.float32
    )


def along_last(values, matrix):
    return jnp.einsum("...j,jk->...k", values, matrix, precision=highest)


def along_rows(values, matrix):
    return jnp.einsum("...jx,jk->...kx", values, matrix, precision=highest)


def halve_depth(values):
    count, depth = (values.shape[0], values.shape[1])
    pairs = values.reshape((count, depth // 2, 2) + values.shape[2:])
    even = pairs[:, :, 0]
    odd = pairs[:, :, 1]
    return (even[:, :-1] + 3.0 * odd[:, :-1] + 3.0 * even[:, 1:] + odd[:, 1:]) * 0.125


def depth_gradient(values):
    length = values.shape[1] - 2
    return (values[:, 2 : 2 + length] - values[:, 0:length]) * 0.5


def depth_smooth(values):
    length = values.shape[2] - 2
    return (
        values[:, :, 0:length] + 2.0 * values[:, :, 1 : 1 + length] + values[:, :, 2 : 2 + length]
    ) * 0.25


def axis_weights(offsets):
    return [
        jnp.where(
            2 * displace == offsets, 1.0, jnp.where(jnp.abs(2 * displace - offsets) == 1, 0.5, 0.0)
        ).astype(jnp.float32)
        for displace in range(-2, 3)
    ]


def warp_moving(moving_rows, offsets):
    layers, height, breadth = (offsets.shape[2], offsets.shape[3], offsets.shape[4])
    weights_z = axis_weights(offsets[:, 0])
    weights_y = axis_weights(offsets[:, 1])
    weights_x = axis_weights(offsets[:, 2])
    shape = offsets[:, 0].shape
    rows_padded = pad_axis(moving_rows, 2, 2)
    wide = pad_axis(rows_padded, 3, 2)
    shifted = [wide[..., index_x : index_x + breadth] for index_x in range(5)]
    warped = jnp.zeros(shape, jnp.float32)
    for index_z in range(5):
        plane_sum = jnp.zeros(shape, jnp.float32)
        for index_y in range(5):
            line_sum = jnp.zeros(shape, jnp.float32)
            for index_x in range(5):
                window = shifted[index_x][:, index_z : index_z + layers, index_y : index_y + height]
                line_sum = line_sum + weights_x[index_x] * window
            plane_sum = plane_sum + weights_y[index_y] * line_sum
        warped = warped + weights_z[index_z] * plane_sum
    return warped


def shards(fine_images, offsets, velocity_init):
    fine_height, fine_breadth = (fine_images.shape[2], fine_images.shape[3])
    rimmed_fine = extended(fine_images, (("slab", 1),), 1)
    coarse = halve_depth(rimmed_fine)
    coarse = along_rows(coarse, halve_matrix(fine_height))
    coarse = along_last(coarse, halve_matrix(fine_breadth))
    target = passed_along(coarse, "phase", -1)
    height, breadth = (coarse.shape[2], coarse.shape[3])
    moving_rows = extended(coarse, (("slab", 1),), 2)
    target_rows = extended(target, (("slab", 1),), 1)
    grad_z = depth_gradient(target_rows)
    grad_y = along_rows(target, gradient_matrix(height))
    grad_x = along_last(target, gradient_matrix(breadth))
    gradients = jnp.stack([grad_z, grad_y, grad_x], axis=1)
    norm_squared = grad_z * grad_z + grad_y * grad_y + grad_x * grad_x
    warped_base = warp_moving(moving_rows, offsets)
    smooth_rows = smooth_matrix(height)
    smooth_columns = smooth_matrix(breadth)
    velocity = velocity_init
    for iteration in range(ITERS):
        warped = (
            warped_base
            + velocity[:, 0] * grad_z
            + velocity[:, 1] * grad_y
            + velocity[:, 2] * grad_x
        )
        mismatch = warped - target
        denominator = norm_squared + mismatch * mismatch + 1.0
        velocity = velocity - (mismatch / denominator)[:, None] * gradients
        rimmed = extended(velocity, (("slab", 2),), 1)
        velocity = depth_smooth(rimmed)
        velocity = along_rows(velocity, smooth_rows)
        velocity = along_last(velocity, smooth_columns)
        earlier = passed_along(velocity, "phase", 1)
        later = passed_along(velocity, "phase", -1)
        velocity = (earlier + 2.0 * velocity + later) * 0.25
    return velocity


def solution(mesh):
    placed = (
        P(("case", "phase"), "slab", None, None),
        P(("case", "phase"), None, "slab", None, None),
        P(("case", "phase"), None, "slab", None, None),
    )
    return jax.shard_map(
        shards,
        mesh=mesh,
        in_specs=placed,
        out_specs=P(("case", "phase"), None, "slab", None, None),
        check_vma=False,
    )
```

profile of v0, /device:TPU:0, one launch (start us, length us, event | category | flops | bytes accessed | tf_op | source)
XLA Modules:
  0.0 166.3 jit_solution(1200865793441317581)
XLA Ops:
  0.0 1.1 fusion.437
  1.1 5.0 %collective-permute-start = (f32[1,1,128,512]{3,2,1,0:T(8,128)S(1)}, f32[1,1,128,512]{3,2,1,0:T(8,128)S(1)}, u32[]{:S(2)}, u32[]{:S(2)}) collective-permute-start(f32[1,1,128,512]{3,2,1,0:T(8,128)S(1)} %get-tuple-element.9), channel_id=1, source_target_pairs={{0,1},{1,2},{2,3},{4,5},{5,6},{6,7},{8,9},{9,10},{10,11},{12,13},{... | collective-permute-start | bytes 786440 | tf_op jit(solution)/shard_map/ppermute | solution.py:20
  6.0 1.3 collective-permute-start.1
  7.4 4.2 %collective-permute-done = f32[1,1,128,512]{3,2,1,0:T(8,128)S(1)} collective-permute-done((f32[1,1,128,512]{3,2,1,0:T(8,128)S(1)}, f32[1,1,128,512]{3,2,1,0:T(8,128)S(1)}, u32[]{:S(2)}, u32[]{:S(2)}) %collective-permute-start) | collective-permute-done | bytes 262176 | tf_op jit(solution)/shard_map/ppermute | solution.py:20
  11.6 4.1 %collective-permute-done.1 = f32[1,1,128,512]{3,2,1,0:T(8,128)S(1)} collective-permute-done((f32[1,1,128,512]{3,2,1,0:T(8,128)S(1)}, f32[1,1,128,512]{3,2,1,0:T(8,128)S(1)}, u32[]{:S(2)}, u32[]{:S(2)}) %collective-permute-start.1) | collective-permute-done | bytes 262176 | tf_op jit(solution)/shard_map/ppermute | solution.py:22
  15.7 2.9 %pad_maximum_fusion = f32[1,18,128,512]{3,2,1,0:T(8,128)S(1)} fusion(f32[1,1,128,512]{3,2,1,0:T(8,128)S(1)} %collective-permute-done.1, f32[1,16,128,512]{3,2,1,0:T(8,128)} %param.3, f32[1,1,128,512]{3,2,1,0:T(8,128)S(1)} %collective-permute-done), kind=kLoop, calls=%fused_computation.100 | loop fusion | flops 2359296 | bytes 9437184 | tf_op jit(solution)/shard_map/concatenate | solution.py:18
  18.6 0.7 slice_bitcast_fusion.1
  19.3 1.7 %fusion.37 = f32[8,64,512]{2,1,0:T(8,128)S(1)} fusion(f32[1,9,128,512]{3,2,1,0:T(8,128)S(1)} %get-tuple-element.8, f32[1,9,128,512]{3,2,1,0:T(8,128)S(1)} %get-tuple-element.7, s32[64]{0:T(128)S(1)} %get-tuple-element.22, s32[64]{0:T(128)S(1)} %get-tuple-element.20, s32[64]{0:T(128)S(1)} %get-tuple-element.21, s32[64]{0:T(128)S(1)} %get-tuple-element.19), kind=kOutput, calls=%fused_computation.145 | convolution fusion | flops 405864448 | bytes 9439232 | tf_op jit(solution)/shard_map/...jx,jk->...kx/dot_general | solution.py:70
  21.0 1.1 fusion.326
  22.1 0.1 collective-permute-start.4
  22.2 3.5 %collective-permute-start.2 = (f32[1,2,64,256]{3,2,1,0:T(8,128)S(1)}, f32[1,2,64,256]{3,2,1,0:T(8,128)S(1)}, u32[]{:S(2)}, u32[]{:S(2)}) collective-permute-start(f32[1,2,64,256]{3,2,1,0:T(8,128)S(1)} %get-tuple-element.15), channel_id=1, source_target_pairs={{0,1},{1,2},{2,3},{4,5},{5,6},{6,7},{8,9},{9,10},{10,11},{12,13},{... | collective-permute-start | bytes 393224 | tf_op jit(solution)/shard_map/ppermute | solution.py:20
  25.6 1.3 collective-permute-start.3
  27.0 2.1 %collective-permute-done.2 = f32[1,2,64,256]{3,2,1,0:T(8,128)S(1)} collective-permute-done((f32[1,2,64,256]{3,2,1,0:T(8,128)S(1)}, f32[1,2,64,256]{3,2,1,0:T(8,128)S(1)}, u32[]{:S(2)}, u32[]{:S(2)}) %collective-permute-start.2) | collective-permute-done | bytes 131104 | tf_op jit(solution)/shard_map/ppermute | solution.py:20
  29.0 0.0 copy-start.5
  29.0 4.1 %collective-permute-done.3 = f32[1,2,64,256]{3,2,1,0:T(8,128)S(1)} collective-permute-done((f32[1,2,64,256]{3,2,1,0:T(8,128)S(1)}, f32[1,2,64,256]{3,2,1,0:T(8,128)S(1)}, u32[]{:S(2)}, u32[]{:S(2)}) %collective-permute-start.3) | collective-permute-done | bytes 131104 | tf_op jit(solution)/shard_map/ppermute | solution.py:22
  33.1 0.0 copy-start.6
  33.1 0.1 select_maximum_fusion
  33.2 0.0 collective-permute-done.4
  33.3 1.3 collective-permute-start.5
  34.6 4.5 %collective-permute-start.6 = (f32[1,1,64,256]{3,2,1,0:T(8,128)S(1)}, f32[1,1,64,256]{3,2,1,0:T(8,128)S(1)}, u32[]{:S(2)}, u32[]{:S(2)}) collective-permute-start(f32[1,1,64,256]{3,2,1,0:T(8,128)S(1)} %get-tuple-element.18), channel_id=1, source_target_pairs={{0,1},{1,2},{2,3},{4,5},{5,6},{6,7},{8,9},{9,10},{10,11},{12,13},{... | collective-permute-start | bytes 196616 | tf_op jit(solution)/shard_map/ppermute | solution.py:20
  39.1 0.0 copy-done.5
  39.1 0.0 copy-done.6
  39.2 0.6 fusion.321
  39.8 0.6 fusion.323
  40.4 0.0 collective-permute-done.5
  40.4 0.0 copy-start.1
  40.4 0.6 collective-permute-done.6
  41.0 0.0 copy-done.1
  41.0 0.0 copy-start.3
  41.0 0.6 copy-done.3
  41.7 16.4 %divide_bitcast_fusion.1 = (f32[8,64,256]{2,1,0:T(8,128)}, f32[1,8,64,256]{3,2,1,0:T(8,128)}) fusion(f32[1,8,64,256]{3,2,1,0:T(8,128)S(1)} %collective-permute-done.4, f32[8,64,256]{2,1,0:T(8,128)S(1)} %fusion.321, f32[64,8,256]{2,0,1:T(8,128)S(1)} %fusion.323, f32[1,3,8,64,256]{4,3,2,1,0:T(8,128)} %param.5, f32[1,1,64,256]{3,2,1,0:T(8,128)} %copy-done.3, ...), kind=kLoop, calls=%fused_computation.480 | loop fusion | flops 51511296 | bytes 18579456 | tf_op jit(solution)/shard_map/mul | solution.py:152
  58.1 1.8 %multiply_subtract_fusion.1 = f32[1,3,8,64,256]{4,3,2,1,0:T(8,128)S(1)} fusion(f32[1,3,8,64,256]{4,3,2,1,0:T(8,128)} %param.5, f32[1,1,8,64,256]{4,3,2,1,0:T(8,128)S(1)} %bitcast.242, f32[1,1,8,64,256]{4,3,2,1,0:T(8,128)S(1)} %bitcast.244, f32[1,1,8,64,256]{4,3,2,1,0:T(8,128)S(1)} %fusion.334, f32[8,64,256]{2,1,0:T(8,128)} %get-tuple-element.5), kind=kLoop, calls=%fused_computation.144 | loop fusion | flops 1572864 | bytes 5242880 | tf_op jit(solution)/shard_map/sub | solution.py:152
  59.9 4.3 %collective-permute-start.7 = (f32[1,3,1,64,256]{4,3,2,1,0:T(8,128)S(1)}, f32[1,3,1,64,256]{4,3,2,1,0:T(8,128)S(1)}, u32[]{:S(2)}, u32[]{:S(2)}) collective-permute-start(f32[1,3,1,64,256]{4,3,2,1,0:T(8,128)S(1)} %get-tuple-element.13), channel_id=1, source_target_pairs={{0,1},{1,2},{2,3},{4,5},{5,6},{6,7},{8,9},{9,10},{10,11},{12,13},{... | collective-permute-start | bytes 589832 | tf_op jit(solution)/shard_map/ppermute | solution.py:20
  64.2 1.5 collective-permute-start.8
  65.7 1.7 %collective-permute-done.7 = f32[1,3,1,64,256]{4,3,2,1,0:T(8,128)S(1)} collective-permute-done((f32[1,3,1,64,256]{4,3,2,1,0:T(8,128)S(1)}, f32[1,3,1,64,256]{4,3,2,1,0:T(8,128)S(1)}, u32[]{:S(2)}, u32[]{:S(2)}) %collective-permute-start.7) | collective-permute-done | bytes 196640 | tf_op jit(solution)/shard_map/ppermute | solution.py:20
  67.3 4.4 %collective-permute-done.8 = f32[1,3,1,64,256]{4,3,2,1,0:T(8,128)S(1)} collective-permute-done((f32[1,3,1,64,256]{4,3,2,1,0:T(8,128)S(1)}, f32[1,3,1,64,256]{4,3,2,1,0:T(8,128)S(1)}, u32[]{:S(2)}, u32[]{:S(2)}) %collective-permute-start.8) | collective-permute-done | bytes 196640 | tf_op jit(solution)/shard_map/ppermute | solution.py:22
  71.7 1.6 fusion.21
  73.4 1.5 fusion.29
  74.8 0.0 copy-start
  74.8 0.0 copy-start.2
  74.8 0.0 copy-start.4
  74.9 0.1 collective-permute-start.10
  74.9 0.5 collective-permute-start.9
  75.4 33.3 %collective-permute-done.10 = f32[1,3,8,64,256]{4,3,2,1,0:T(8,128)S(1)} collective-permute-done((f32[1,3,8,64,256]{4,3,2,1,0:T(8,128)S(1)}, f32[1,3,8,64,256]{4,3,2,1,0:T(8,128)S(1)}, u32[]{:S(2)}, u32[]{:S(2)}) %collective-permute-start.10) | collective-permute-done | bytes 1572896 | tf_op jit(solution)/shard_map/ppermute | solution.py:32
  108.7 2.9 %collective-permute-done.9 = f32[1,3,8,64,256]{4,3,2,1,0:T(8,128)S(1)} collective-permute-done((f32[1,3,8,64,256]{4,3,2,1,0:T(8,128)S(1)}, f32[1,3,8,64,256]{4,3,2,1,0:T(8,128)S(1)}, u32[]{:S(2)}, u32[]{:S(2)}) %collective-permute-start.9) | collective-permute-done | bytes 1572896 | tf_op jit(solution)/shard_map/ppermute | solution.py:32
  111.7 0.5 fusion.34
  112.2 0.0 copy-done
  112.2 0.0 copy-done.2
  112.2 0.0 copy-done.4
  112.2 0.4 divide_bitcast_fusion
  112.6 0.4 multiply_subtract_fusion
  113.0 3.5 %collective-permute-start.11 = (f32[1,3,1,64,256]{4,3,2,1,0:T(8,128)S(1)}, f32[1,3,1,64,256]{4,3,2,1,0:T(8,128)S(1)}, u32[]{:S(2)}, u32[]{:S(2)}) collective-permute-start(f32[1,3,1,64,256]{4,3,2,1,0:T(8,128)S(1)} %get-tuple-element.11), channel_id=1, source_target_pairs={{0,1},{1,2},{2,3},{4,5},{5,6},{6,7},{8,9},{9,10},{10,11},{12,13},{... | collective-permute-start | bytes 589832 | tf_op jit(solution)/shard_map/ppermute | solution.py:20
  116.5 1.3 collective-permute-start.12
  117.8 3.1 %collective-permute-done.11 = f32[1,3,1,64,256]{4,3,2,1,0:T(8,128)S(1)} collective-permute-done((f32[1,3,1,64,256]{4,3,2,1,0:T(8,128)S(1)}, f32[1,3,1,64,256]{4,3,2,1,0:T(8,128)S(1)}, u32[]{:S(2)}, u32[]{:S(2)}) %collective-permute-start.11) | collective-permute-done | bytes 196640 | tf_op jit(solution)/shard_map/ppermute | solution.py:20
  120.9 4.1 %collective-permute-done.12 = f32[1,3,1,64,256]{4,3,2,1,0:T(8,128)S(1)} collective-permute-done((f32[1,3,1,64,256]{4,3,2,1,0:T(8,128)S(1)}, f32[1,3,1,64,256]{4,3,2,1,0:T(8,128)S(1)}, u32[]{:S(2)}, u32[]{:S(2)}) %collective-permute-start.12) | collective-permute-done | bytes 196640 | tf_op jit(solution)/shard_map/ppermute | solution.py:22
  125.1 1.6 fusion.12
  126.7 1.5 fusion.27
  128.1 0.1 collective-permute-start.13
  128.2 1.7 %collective-permute-start.14 = (f32[1,3,8,64,256]{4,3,2,1,0:T(8,128)S(1)}, f32[1,3,8,64,256]{4,3,2,1,0:T(8,128)S(1)}, u32[]{:S(2)}, u32[]{:S(2)}) collective-permute-start(f32[1,3,8,64,256]{4,3,2,1,0:T(8,128)S(1)} %bitcast.253), channel_id=1, source_target_pairs={{4,0},{8,4},{12,8},{0,12},{5,1},{9,5},{13,9},{1,13},{6,2},{10,6},{... | collective-permute-start | bytes 4718600 | tf_op jit(solution)/shard_map/ppermute | solution.py:32
  129.9 34.8 %collective-permute-done.13 = f32[1,3,8,64,256]{4,3,2,1,0:T(8,128)S(1)} collective-permute-done((f32[1,3,8,64,256]{4,3,2,1,0:T(8,128)S(1)}, f32[1,3,8,64,256]{4,3,2,1,0:T(8,128)S(1)}, u32[]{:S(2)}, u32[]{:S(2)}) %collective-permute-start.13) | collective-permute-done | bytes 1572896 | tf_op jit(solution)/shard_map/ppermute | solution.py:32
  164.7 0.0 collective-permute-done.14
  164.7 1.5 fusion.32
  (11 shorter events, 0.2 us)
Async XLA Ops:
  1.1 10.5 %collective-permute-start = (f32[1,1,128,512]{3,2,1,0:T(8,128)S(1)}, f32[1,1,128,512]{3,2,1,0:T(8,128)S(1)}, u32[]{:S(2)}, u32[]{:S(2)}) collective-permute-start(f32[1,1,128,512]{3,2,1,0:T(8,128)S(1)} %get-tuple-element.9), channel_id=1, source_target_pairs={{0,1},{1,2},{2,3},{4,5},{5,6},{6,7},{8,9},{9,10},{10,11},{12,13},{... | collective-permute-start | bytes 786440 | tf_op jit(solution)/shard_map/ppermute | solution.py:20
  6.0 9.7 %collective-permute-start.1 = (f32[1,1,128,512]{3,2,1,0:T(8,128)S(1)}, f32[1,1,128,512]{3,2,1,0:T(8,128)S(1)}, u32[]{:S(2)}, u32[]{:S(2)}) collective-permute-start(f32[1,1,128,512]{3,2,1,0:T(8,128)S(1)} %get-tuple-element.10), channel_id=1, source_target_pairs={{1,0},{2,1},{3,2},{5,4},{6,5},{7,6},{9,8},{10,9},{11,10},{13,12},{... | collective-permute-start | bytes 786440 | tf_op jit(solution)/shard_map/ppermute | solution.py:22
  22.1 11.2 %collective-permute-start.4 = (f32[1,8,64,256]{3,2,1,0:T(8,128)S(1)}, f32[1,8,64,256]{3,2,1,0:T(8,128)S(1)}, u32[]{:S(2)}, u32[]{:S(2)}) collective-permute-start(f32[1,8,64,256]{3,2,1,0:T(8,128)S(1)} %bitcast.246), channel_id=1, source_target_pairs={{4,0},{8,4},{12,8},{0,12},{5,1},{9,5},{13,9},{1,13},{6,2},{10,6},{... | collective-permute-start | bytes 1572872 | tf_op jit(solution)/shard_map/ppermute | solution.py:32
  22.2 6.9 %collective-permute-start.2 = (f32[1,2,64,256]{3,2,1,0:T(8,128)S(1)}, f32[1,2,64,256]{3,2,1,0:T(8,128)S(1)}, u32[]{:S(2)}, u32[]{:S(2)}) collective-permute-start(f32[1,2,64,256]{3,2,1,0:T(8,128)S(1)} %get-tuple-element.15), channel_id=1, source_target_pairs={{0,1},{1,2},{2,3},{4,5},{5,6},{6,7},{8,9},{9,10},{10,11},{12,13},{... | collective-permute-start | bytes 393224 | tf_op jit(solution)/shard_map/ppermute | solution.py:20
  25.6 7.5 %collective-permute-start.3 = (f32[1,2,64,256]{3,2,1,0:T(8,128)S(1)}, f32[1,2,64,256]{3,2,1,0:T(8,128)S(1)}, u32[]{:S(2)}, u32[]{:S(2)}) collective-permute-start(f32[1,2,64,256]{3,2,1,0:T(8,128)S(1)} %get-tuple-element.16), channel_id=1, source_target_pairs={{1,0},{2,1},{3,2},{5,4},{6,5},{7,6},{9,8},{10,9},{11,10},{13,12},{... | collective-permute-start | bytes 393224 | tf_op jit(solution)/shard_map/ppermute | solution.py:22
  29.0 10.1 %copy-start.5 = (f32[1,2,64,256]{3,2,1,0:T(8,128)}, f32[1,2,64,256]{3,2,1,0:T(8,128)S(1)}, u32[]{:S(2)}) copy-start(f32[1,2,64,256]{3,2,1,0:T(8,128)S(1)} %collective-permute-done.2) | copy-start | bytes 393220
  33.1 6.0 %copy-start.6 = (f32[1,2,64,256]{3,2,1,0:T(8,128)}, f32[1,2,64,256]{3,2,1,0:T(8,128)S(1)}, u32[]{:S(2)}) copy-start(f32[1,2,64,256]{3,2,1,0:T(8,128)S(1)} %collective-permute-done.3) | copy-start | bytes 393220
  33.3 7.1 %collective-permute-start.5 = (f32[1,1,64,256]{3,2,1,0:T(8,128)S(1)}, f32[1,1,64,256]{3,2,1,0:T(8,128)S(1)}, u32[]{:S(2)}, u32[]{:S(2)}) collective-permute-start(f32[1,1,64,256]{3,2,1,0:T(8,128)S(1)} %get-tuple-element.17), channel_id=1, source_target_pairs={{1,0},{2,1},{3,2},{5,4},{6,5},{7,6},{9,8},{10,9},{11,10},{13,12},{... | collective-permute-start | bytes 196616 | tf_op jit(solution)/shard_map/ppermute | solution.py:22
  34.6 6.4 %collective-permute-start.6 = (f32[1,1,64,256]{3,2,1,0:T(8,128)S(1)}, f32[1,1,64,256]{3,2,1,0:T(8,128)S(1)}, u32[]{:S(2)}, u32[]{:S(2)}) collective-permute-start(f32[1,1,64,256]{3,2,1,0:T(8,128)S(1)} %get-tuple-element.18), channel_id=1, source_target_pairs={{0,1},{1,2},{2,3},{4,5},{5,6},{6,7},{8,9},{9,10},{10,11},{12,13},{... | collective-permute-start | bytes 196616 | tf_op jit(solution)/shard_map/ppermute | solution.py:20
  40.4 0.6 copy-start.1
  41.0 0.6 copy-start.3
  59.9 7.4 %collective-permute-start.7 = (f32[1,3,1,64,256]{4,3,2,1,0:T(8,128)S(1)}, f32[1,3,1,64,256]{4,3,2,1,0:T(8,128)S(1)}, u32[]{:S(2)}, u32[]{:S(2)}) collective-permute-start(f32[1,3,1,64,256]{4,3,2,1,0:T(8,128)S(1)} %get-tuple-element.13), channel_id=1, source_target_pairs={{0,1},{1,2},{2,3},{4,5},{5,6},{6,7},{8,9},{9,10},{10,11},{12,13},{... | collective-permute-start | bytes 589832 | tf_op jit(solution)/shard_map/ppermute | solution.py:20
  64.2 7.6 %collective-permute-start.8 = (f32[1,3,1,64,256]{4,3,2,1,0:T(8,128)S(1)}, f32[1,3,1,64,256]{4,3,2,1,0:T(8,128)S(1)}, u32[]{:S(2)}, u32[]{:S(2)}) collective-permute-start(f32[1,3,1,64,256]{4,3,2,1,0:T(8,128)S(1)} %get-tuple-element.14), channel_id=1, source_target_pairs={{1,0},{2,1},{3,2},{5,4},{6,5},{7,6},{9,8},{10,9},{11,10},{13,12},{... | collective-permute-start | bytes 589832 | tf_op jit(solution)/shard_map/ppermute | solution.py:22
  74.8 37.3 %copy-start = (f32[1,8,64,256]{3,2,1,0:T(8,128)S(1)}, f32[1,8,64,256]{3,2,1,0:T(8,128)}, u32[]{:S(2)}) copy-start(f32[1,8,64,256]{3,2,1,0:T(8,128)} %get-tuple-element.6) | copy-start | bytes 1572868
  74.8 37.3 %copy-start.2 = (f32[1,1,64,256]{3,2,1,0:T(8,128)S(1)}, f32[1,1,64,256]{3,2,1,0:T(8,128)}, u32[]{:S(2)}) copy-start(f32[1,1,64,256]{3,2,1,0:T(8,128)} %copy-done.1) | copy-start | bytes 196612
  74.8 37.3 %copy-start.4 = (f32[1,1,64,256]{3,2,1,0:T(8,128)S(1)}, f32[1,1,64,256]{3,2,1,0:T(8,128)}, u32[]{:S(2)}) copy-start(f32[1,1,64,256]{3,2,1,0:T(8,128)} %copy-done.3) | copy-start | bytes 196612
  74.9 33.9 %collective-permute-start.10 = (f32[1,3,8,64,256]{4,3,2,1,0:T(8,128)S(1)}, f32[1,3,8,64,256]{4,3,2,1,0:T(8,128)S(1)}, u32[]{:S(2)}, u32[]{:S(2)}) collective-permute-start(f32[1,3,8,64,256]{4,3,2,1,0:T(8,128)S(1)} %bitcast.250), channel_id=1, source_target_pairs={{4,0},{8,4},{12,8},{0,12},{5,1},{9,5},{13,9},{1,13},{6,2},{10,6},{... | collective-permute-start | bytes 4718600 | tf_op jit(solution)/shard_map/ppermute | solution.py:32
  74.9 36.7 %collective-permute-start.9 = (f32[1,3,8,64,256]{4,3,2,1,0:T(8,128)S(1)}, f32[1,3,8,64,256]{4,3,2,1,0:T(8,128)S(1)}, u32[]{:S(2)}, u32[]{:S(2)}) collective-permute-start(f32[1,3,8,64,256]{4,3,2,1,0:T(8,128)S(1)} %bitcast.251), channel_id=1, source_target_pairs={{12,0},{0,4},{4,8},{8,12},{13,1},{1,5},{5,9},{9,13},{14,2},{2,6},{... | collective-permute-start | bytes 4718600 | tf_op jit(solution)/shard_map/ppermute | solution.py:32
  113.0 7.9 %collective-permute-start.11 = (f32[1,3,1,64,256]{4,3,2,1,0:T(8,128)S(1)}, f32[1,3,1,64,256]{4,3,2,1,0:T(8,128)S(1)}, u32[]{:S(2)}, u32[]{:S(2)}) collective-permute-start(f32[1,3,1,64,256]{4,3,2,1,0:T(8,128)S(1)} %get-tuple-element.11), channel_id=1, source_target_pairs={{0,1},{1,2},{2,3},{4,5},{5,6},{6,7},{8,9},{9,10},{10,11},{12,13},{... | collective-permute-start | bytes 589832 | tf_op jit(solution)/shard_map/ppermute | solution.py:20
  116.5 8.5 %collective-permute-start.12 = (f32[1,3,1,64,256]{4,3,2,1,0:T(8,128)S(1)}, f32[1,3,1,64,256]{4,3,2,1,0:T(8,128)S(1)}, u32[]{:S(2)}, u32[]{:S(2)}) collective-permute-start(f32[1,3,1,64,256]{4,3,2,1,0:T(8,128)S(1)} %get-tuple-element.12), channel_id=1, source_target_pairs={{1,0},{2,1},{3,2},{5,4},{6,5},{7,6},{9,8},{10,9},{11,10},{13,12},{... | collective-permute-start | bytes 589832 | tf_op jit(solution)/shard_map/ppermute | solution.py:22
  128.1 36.6 %collective-permute-start.13 = (f32[1,3,8,64,256]{4,3,2,1,0:T(8,128)S(1)}, f32[1,3,8,64,256]{4,3,2,1,0:T(8,128)S(1)}, u32[]{:S(2)}, u32[]{:S(2)}) collective-permute-start(f32[1,3,8,64,256]{4,3,2,1,0:T(8,128)S(1)} %bitcast.252), channel_id=1, source_target_pairs={{12,0},{0,4},{4,8},{8,12},{13,1},{1,5},{5,9},{9,13},{14,2},{2,6},{... | collective-permute-start | bytes 4718600 | tf_op jit(solution)/shard_map/ppermute | solution.py:32
  128.2 36.5 %collective-permute-start.14 = (f32[1,3,8,64,256]{4,3,2,1,0:T(8,128)S(1)}, f32[1,3,8,64,256]{4,3,2,1,0:T(8,128)S(1)}, u32[]{:S(2)}, u32[]{:S(2)}) collective-permute-start(f32[1,3,8,64,256]{4,3,2,1,0:T(8,128)S(1)} %bitcast.253), channel_id=1, source_target_pairs={{4,0},{8,4},{12,8},{0,12},{5,1},{9,5},{13,9},{1,13},{6,2},{10,6},{... | collective-permute-start | bytes 4718600 | tf_op jit(solution)/shard_map/ppermute | solution.py:32
where the time goes:
time: 167 us; the launch traced here: 166 us
  waiting for transfers between devices  99.5 us (60%)
  starting transfers between devices  29.8 us (18%)
  other arithmetic  24 us (14%)
  matrix products  10.1 us (6%)
  local copies, waits for them, and re-layouts  2.5 us (1%)
    ppermute x5, waiting for transfers between devices, passed_along(): return lax.ppermute(block, axis, route)  71 us
    ppermute x5, starting transfers between devices, extended(): lax.ppermute(tail, axis, [(i, (i + 1) % count) for i in range(ends)])  20.8 us
    mul x2, other arithmetic, shards(): velocity = velocity - (mismatch / denominator)[:, None] * gradients  16.8 us
    ppermute x5, waiting for transfers between devices, extended(): lax.ppermute(head, axis, [((i + 1) % count, i) for i in range(ends)])  16.8 us
    ppermute x5, waiting for transfers between devices, extended(): lax.ppermute(tail, axis, [(i, (i + 1) % count) for i in range(ends)])  11.7 us
    ppermute x5, starting transfers between devices, extended(): lax.ppermute(head, axis, [((i + 1) % count, i) for i in range(ends)])  6.64 us
    dot_general x4, matrix products, along_rows(): return jnp.einsum('...jx,jk->...kx', values, matrix, precision=highest)  5.51 us
    dot_general x4, matrix products, along_last(): return jnp.einsum('...j,jk->...k', values, matrix, precision=highest)  4.57 us
  transfers between devices with their start and end apart: 15, of which 12 were waited for; matrix products, arithmetic and copies ran while one was open for 1% of the time, Pallas kernels for 0%

commit v1 on v0

--- a/solution.py
+++ b/solution.py
@@ -1,9 +1,493 @@
+import functools
+
 import jax
 import jax.numpy as jnp
 from jax import lax
+from jax.experimental import pallas as pl
+from jax.experimental.pallas import tpu as pltpu
 from jax.sharding import PartitionSpec as P
 
 ITERS = 2
+RIM = 8
+F32 = jnp.float32
+BF16 = jnp.bfloat16
+
+
+def launch(body, outs, ins, scratch=(), anys=(), grid=None, in_specs=None, out_specs=None, flops=0):
+    vmem = pl.BlockSpec(memory_space=pltpu.VMEM)
+    anym = pl.BlockSpec(memory_space=pl.ANY)
+    if in_specs is None:
+        in_specs = [anym if i in anys else vmem for i in range(len(ins))]
+    if out_specs is None:
+        out_specs = [vmem for _ in outs]
+    moved = sum(4 * x.size for x in ins) + sum(4 * o.size for o in outs)
+    params = dict(grid=grid) if grid is not None else {}
+    return pl.pallas_call(
+        body,
+        out_shape=outs,
+        in_specs=in_specs,
+        out_specs=out_specs,
+        scratch_shapes=scratch,
+        compiler_params=pltpu.CompilerParams(vmem_limit_bytes=48 * 2**20),
+        cost_estimate=pl.CostEstimate(flops=flops, bytes_accessed=moved, transcendentals=0),
+        **params,
+    )(*ins)
+
+
+def shape(*dims):
+    return jax.ShapeDtypeStruct(dims, F32)
+
+
+def chip_and_core():
+    phase = lax.axis_index("phase")
+    return phase // 2, phase % 2
+
+
+def slab_place():
+    slab = lax.axis_index("slab")
+    last = lax.axis_size("slab") - 1
+    return slab % 2, slab > 0, slab < last
+
+
+def shift_rows(a, up):
+    zero = jnp.zeros((1, a.shape[1]), a.dtype)
+    return jnp.concatenate([a[1:], zero], 0) if up else jnp.concatenate([zero, a[:-1]], 0)
+
+
+def shift_lanes(a, step):
+    width = a.shape[1]
+    lane = lax.broadcasted_iota(jnp.int32, a.shape, 1)
+    moved = pltpu.roll(a, (-step) % width, 1)
+    keep = lane < width - step if step > 0 else lane >= -step
+    return jnp.where(keep, moved, 0.0)
+
+
+def halve_kernel(fine, part, edge, buf_a, buf_b, mat, rows, prev):
+    k = pl.program_id(0)
+    last = pl.num_programs(0) - 1
+    deep, tall, wide = fine.shape
+
+    @pl.when(k == 0)
+    def _():
+        i = lax.broadcasted_iota(jnp.int32, mat.shape, 0)
+        j = lax.broadcasted_iota(jnp.int32, mat.shape, 1)
+        d = i - 2 * j
+        inner = (d == 0) | (d == 1)
+        outer = (d == -1) | (d == 2)
+        mat[...] = jnp.where(inner, 0.375, jnp.where(outer, 0.125, 0.0)).astype(BF16)
+
+    f = fine[...].reshape(deep * tall, wide)
+    hi = f.astype(BF16)
+    lo = (f - hi.astype(F32)).astype(BF16)
+    w = mat[...]
+    got = jnp.dot(hi, w, preferred_element_type=F32) + jnp.dot(lo, w, preferred_element_type=F32)
+    half = tall // 2
+    cut = rows.shape[2]
+    for c in range(rows.shape[0]):
+        rows[c] = got[:, c * cut : (c + 1) * cut]
+    layers = []
+    for z in range(deep):
+        cols = []
+        for c in range(rows.shape[0]):
+            even = rows[c, pl.ds(z * tall, half, 2), :]
+            odd = rows[c, pl.ds(z * tall + 1, half, 2), :]
+            cols.append(
+                (shift_rows(odd, False) + shift_rows(even, True) + 3.0 * (even + odd)) * (1.0 / 64.0)
+            )
+        layers.append(jnp.concatenate(cols, 1))
+    even, odd = layers
+    mid = 3.0 * (even + odd)
+
+    @pl.when(k == 0)
+    def _():
+        edge[0] = even
+        part[0] = mid
+
+    @pl.when(k > 0)
+    def _():
+        part[k] = mid + prev[...]
+        part[k - 1] += even
+
+    prev[...] = odd
+
+    @pl.when(k == last)
+    def _():
+        edge[1] = odd
+        parity, _, _ = slab_place()
+        n = part.shape[0]
+        for i in range(4):
+            above = odd if i == 3 else part[n - 3 + i]
+            below = edge[0] if i == 0 else part[i - 1]
+            buf_a[i] = jnp.where(parity == 0, above, below)
+            buf_b[i] = jnp.where(parity == 0, below, above)
+
+
+def join_kernel(part, edge, got_a, got_b, ext, near, far):
+    n = part.shape[0]
+    parity, has_below, has_above = slab_place()
+    x, _ = chip_and_core()
+    for i in range(3):
+        low = jnp.where(parity == 0, got_b[i], got_a[i])
+        high = jnp.where(parity == 0, got_a[i + 1], got_b[i + 1])
+        if i == 2:
+            low = jnp.where(has_below, low + edge[0], 0.0)
+        if i == 0:
+            high = jnp.where(has_above, high + edge[1], 0.0)
+        ext[i] = low
+        ext[n + 3 + i] = high
+    for i in range(n):
+        v = part[i]
+        if i == 0:
+            v = v + jnp.where(parity == 0, got_b[3], got_a[3])
+        if i == n - 1:
+            v = v + jnp.where(parity == 0, got_a[0], got_b[0])
+        ext[i + 3] = v
+    span = near.shape[1]
+    step = ext.shape[1] - span
+    near[...] = ext[:, pl.ds(pl.multiple_of(x * step, 8), span), :]
+    far[...] = ext[:, pl.ds(pl.multiple_of((1 - x) * step, 8), span), :]
+
+
+def warp_kernel(ext, offs, near, far, wide, full):
+    n, tall = offs.shape[1], ext.shape[1]
+    depth = n + 4
+    columns, lanes = wide.shape[1], wide.shape[4]
+    blank = jnp.zeros((8, lanes), F32)
+
+    def fill(z, carry):
+        v = ext[z + 1]
+        for s in range(5):
+            moved = v if s == 2 else shift_lanes(v, s - 2)
+            for c in range(columns):
+                wide[s, c, z, pl.ds(0, 8), :] = blank
+                wide[s, c, z, pl.ds(8, tall), :] = moved[:, c * lanes : (c + 1) * lanes]
+                wide[s, c, z, pl.ds(8 + tall, 8), :] = blank
+        return carry
+
+    lax.fori_loop(0, depth, fill, 0)
+
+    def weights(comp, z, y, c):
+        h = offs[comp, z, pl.ds(y, 8), pl.ds(c * lanes, lanes)].astype(F32) * 0.5
+        return [jnp.maximum(1.0 - jnp.abs(h - (s - 2.0)), 0.0) for s in range(5)]
+
+    def tile(i, carry):
+        z = i // (tall // 8)
+        y = pl.multiple_of((i % (tall // 8)) * 8, 8)
+        for c in range(columns):
+            wz, wy, wx = (weights(m, z, y, c) for m in range(3))
+            total = None
+            for a in range(5):
+                plane = None
+                for b in range(5):
+                    line = None
+                    for s in range(5):
+                        term = wx[s] * wide[s, c, z + a, pl.ds(y + 6 + b, 8), :]
+                        line = term if line is None else line + term
+                    line = wy[b] * line
+                    plane = line if plane is None else plane + line
+                plane = wz[a] * plane
+                total = plane if total is None else total + plane
+            full[z, pl.ds(y, 8), pl.ds(c * lanes, lanes)] = total
+        return carry
+
+    lax.fori_loop(0, n * (tall // 8), tile, 0)
+    x, _ = chip_and_core()
+    span = near.shape[1]
+    step = tall - span
+    near[...] = full[:, pl.ds(pl.multiple_of(x * step, 8), span), :]
+    far[...] = full[:, pl.ds(pl.multiple_of((1 - x) * step, 8), span), :]
+
+
+def cut_kernel(vel, far, sem):
+    x, _ = chip_and_core()
+    span = far.shape[2]
+    step = vel.shape[2] - span
+    copy = pltpu.make_async_copy(
+        vel.at[:, :, pl.ds(pl.multiple_of((1 - x) * step, 8), span), :], far, sem
+    )
+    copy.start()
+    copy.wait()
+
+
+def rim_velocity_kernel(vel, other, buf_a, buf_b, stage, sem):
+    x, _ = chip_and_core()
+    parity, _, _ = slab_place()
+    n = vel.shape[1]
+    span = other.shape[2]
+    start = pl.multiple_of(x * (vel.shape[2] - span), 8)
+    copies = [
+        pltpu.make_async_copy(vel.at[:, pl.ds(z, 2), pl.ds(start, span), :], stage.at[j], sem.at[j])
+        for j, z in enumerate((0, n - 2))
+    ]
+    for copy in copies:
+        copy.start()
+    for copy in copies:
+        copy.wait()
+    for m in range(2):
+        for comp in range(3):
+            for i in range(2):
+                below = stage[0, comp, i] if m == 0 else other[comp, i]
+                above = stage[1, comp, i] if m == 0 else other[comp, n - 2 + i]
+                buf_a[m, comp, i] = jnp.where(parity == 0, above, below)
+                buf_b[m, comp, i] = jnp.where(parity == 0, below, above)
+
+
+def rim_warp_kernel(near, other, buf_a, buf_b):
+    parity, _, _ = slab_place()
+    n = near.shape[0]
+    for m in range(2):
+        ref = near if m == 0 else other
+        for i in range(2):
+            below, above = ref[i], ref[n - 2 + i]
+            buf_a[m, i] = jnp.where(parity == 0, above, below)
+            buf_b[m, i] = jnp.where(parity == 0, below, above)
+
+
+def pick(parity, got_a, got_b, high):
+    a, b = (got_a, got_b) if high else (got_b, got_a)
+    return jnp.where(parity == 0, a, b)
+
+
+def update(velocity, warped, low, here, high, valid):
+    gz = (high - low) * 0.5
+    gy = (shift_rows(here, True) - shift_rows(here, False)) * 0.5
+    gx = (shift_lanes(here, 1) - shift_lanes(here, -1)) * 0.5
+    mismatch = warped + velocity[0] * gz + velocity[1] * gy + velocity[2] * gx - here
+    denominator = (gz * gz + gy * gy + gx * gx) + mismatch * mismatch + 1.0
+    ratio = mismatch / denominator
+    return [jnp.where(valid, v - ratio * g, 0.0) for v, g in zip(velocity, (gz, gy, gx))]
+
+
+def smooth_plane(v):
+    v = (shift_rows(v, False) + 2.0 * v + shift_rows(v, True)) * 0.25
+    return (shift_lanes(v, -1) + 2.0 * v + shift_lanes(v, 1)) * 0.25
+
+
+def first_kernel(
+    vel, vel_other, vel_a, vel_b, warp, warp_other, warp_a, warp_b, chip, diag,
+    out, out_sum, warps, targets, held, moved, stage, sem,
+):
+    x, core = chip_and_core()
+    parity, has_below, has_above = slab_place()
+    n, span = vel_other.shape[1], vel_other.shape[2]
+    start = pl.multiple_of(x * (vel.shape[2] - span), 8)
+    copy = pltpu.make_async_copy(vel.at[:, :, pl.ds(start, span), :], stage, sem)
+    copy.start()
+    for i in range(n + 6):
+        a, b = chip[i], diag[i]
+        targets[0, i] = jnp.where(core == 0, a, b)
+        targets[1, i] = jnp.where(core == 0, b, a)
+    for m in range(2):
+        ref = warp if m == 0 else warp_other
+        for i in range(2):
+            warps[m, i] = pick(parity, warp_a[m, i], warp_b[m, i], False)
+            warps[m, n + 2 + i] = pick(parity, warp_a[m, i], warp_b[m, i], True)
+        for i in range(n):
+            warps[m, i + 2] = ref[i]
+    copy.wait()
+    for m in range(2):
+        ref = stage if m == 0 else vel_other
+        for comp in range(3):
+            for i in range(2):
+                held[m, comp, i] = pick(parity, vel_a[m, comp, i], vel_b[m, comp, i], False)
+                held[m, comp, n + 2 + i] = pick(parity, vel_a[m, comp, i], vel_b[m, comp, i], True)
+            for i in range(n):
+                held[m, comp, i + 2] = ref[comp, i]
+    deep = n + 4
+
+    def step(j, carry):
+        m, i = j // deep, j % deep
+        valid = (has_below | (i >= 2)) & (has_above | (i < n + 2))
+        v = update(
+            [held[m, comp, i] for comp in range(3)], warps[m, i],
+            targets[m, i], targets[m, i + 1], targets[m, i + 2], valid,
+        )
+        for comp in range(3):
+            moved[m, comp, i] = v[comp]
+        return carry
+
+    lax.fori_loop(0, 2 * deep, step, 0)
+
+    def blur(i, carry):
+        valid = (has_below | (i >= 1)) & (has_above | (i < n + 1))
+        for comp in range(3):
+            total = None
+            for m in range(2):
+                v = (moved[m, comp, i] + 2.0 * moved[m, comp, i + 1] + moved[m, comp, i + 2]) * 0.25
+                v = jnp.where(valid, smooth_plane(v), 0.0)
+                out[m, comp, i] = v
+                total = v if total is None else total + v
+            out_sum[comp, i] = total
+        return carry
+
+    lax.fori_loop(0, n + 2, blur, 0)
+
+
+def second_kernel(vel, beside, warps, targets, out, out_sum, moved):
+    x, _ = chip_and_core()
+    _, has_below, has_above = slab_place()
+    n, half = out.shape[2], out.shape[3]
+    deep = n + 2
+
+    def step(j, carry):
+        m, i = j // deep, j % deep
+        valid = (has_below | (i >= 1)) & (has_above | (i < n + 1))
+        v = update(
+            [(2.0 * vel[m, comp, i] + beside[comp, i]) * 0.25 for comp in range(3)], warps[m, i + 1],
+            targets[m, i + 1], targets[m, i + 2], targets[m, i + 3], valid,
+        )
+        for comp in range(3):
+            moved[m, comp, i] = v[comp]
+        return carry
+
+    lax.fori_loop(0, 2 * deep, step, 0)
+
+    def blur(i, carry):
+        for comp in range(3):
+            total = None
+            for m in range(2):
+                v = (moved[m, comp, i] + 2.0 * moved[m, comp, i + 1] + moved[m, comp, i + 2]) * 0.25
+                v = smooth_plane(v)
+                v = jnp.where(x == 0, v[:half], v[v.shape[0] - half :])
+                out[m, comp, i] = v
+                total = v if total is None else total + v
+            out_sum[comp, i] = total
+        return carry
+
+    lax.fori_loop(0, n, blur, 0)
+
+
+def send_kernel(vel, beside, out):
+    out[...] = (2.0 * vel[1] + beside[...]) * 0.25
+
+
+def close_kernel(vel, beside, other, out, stage, sem):
+    x, _ = chip_and_core()
+    half = stage.shape[2]
+    there = pltpu.make_async_copy(
+        other, out.at[:, :, pl.ds(pl.multiple_of((1 - x) * half, 8), half), :], sem.at[0]
+    )
+    there.start()
+    stage[...] = (2.0 * vel[0] + beside[...]) * 0.25
+    here = pltpu.make_async_copy(
+        stage, out.at[:, :, pl.ds(pl.multiple_of(x * half, 8), half), :], sem.at[1]
+    )
+    here.start()
+    here.wait()
+    there.wait()
+
+
+def swaps(count, first):
+    pairs = []
+    for i in range(first, count - 1, 2):
+        pairs += [(i, i + 1), (i + 1, i)]
+    return pairs
+
+
+def swap_slabs(buf_a, buf_b):
+    count = lax.axis_size("slab")
+    return (
+        lax.ppermute(buf_a, "slab", swaps(count, 0)),
+        lax.ppermute(buf_b, "slab", swaps(count, 1)),
+    )
+
+
+def swap_phases(values, mask):
+    return lax.ppermute(values, "phase", [(i, i ^ mask) for i in range(lax.axis_size("phase"))])
+
+
+def ring_of_four(fine_images, offsets, velocity_init):
+    fine, offs, vel = fine_images[0], offsets[0], velocity_init[0]
+    deep, tall, wide = fine.shape
+    n, rows, cols = offs.shape[1:]
+    half = rows // 2
+    span = half + RIM
+    lanes = 128
+    dma = pltpu.SemaphoreType.DMA
+
+    (vel_far,) = launch(cut_kernel, [shape(3, n, span, cols)], [vel], [dma], anys=(0,))
+    vel_other = swap_phases(vel_far, 2)
+
+    full = lambda *dims: pl.BlockSpec(dims, lambda k: (0,) * len(dims))
+    part, edge, buf_a, buf_b = launch(
+        halve_kernel,
+        [shape(n, rows, cols), shape(2, rows, cols), shape(4, rows, cols), shape(4, rows, cols)],
+        [fine],
+        [
+            pltpu.VMEM((wide, cols), BF16),
+            pltpu.VMEM((cols // lanes, 2 * tall, lanes), F32),
+            pltpu.VMEM((rows, cols), F32),
+        ],
+        grid=(n,),
+        in_specs=[pl.BlockSpec((2, tall, wide), lambda k: (k, 0, 0))],
+        out_specs=[full(n, rows, cols), full(2, rows, cols), full(4, rows, cols), full(4, rows, cols)],
+    )
+    got_a, got_b = swap_slabs(buf_a, buf_b)
+    ext, near, far = launch(
+        join_kernel,
+        [shape(n + 6, rows, cols), shape(n + 6, span, cols), shape(n + 6, span, cols)],
+        [part, edge, got_a, got_b],
+    )
+    chip = swap_phases(near, 1)
+    diag = swap_phases(far, 3)
+
+    warp, warp_far = launch(
+        warp_kernel,
+        [shape(n, span, cols), shape(n, span, cols)],
+        [ext, offs],
+        [
+            pltpu.VMEM((5, cols // lanes, n + 4, rows + 16, lanes), F32),
+            pltpu.VMEM((n, rows, cols), F32),
+        ],
+    )
+    warp_other = swap_phases(warp_far, 2)
+
+    buf_a, buf_b = launch(
+        rim_velocity_kernel,
+        [shape(2, 3, 2, span, cols)] * 2,
+        [vel, vel_other],
+        [pltpu.VMEM((2, 3, 2, span, cols), F32), dma((2,))],
+        anys=(0,),
+    )
+    vel_a, vel_b = swap_slabs(buf_a, buf_b)
+    buf_a, buf_b = launch(rim_warp_kernel, [shape(2, 2, span, cols)] * 2, [warp, warp_other])
+    warp_a, warp_b = swap_slabs(buf_a, buf_b)
+
+    state, own_sum, warps, targets = launch(
+        first_kernel,
+        [
+            shape(2, 3, n + 2, span, cols),
+            shape(3, n + 2, span, cols),
+            shape(2, n + 4, span, cols),
+            shape(2, n + 6, span, cols),
+        ],
+        [vel, vel_other, vel_a, vel_b, warp, warp_other, warp_a, warp_b, chip, diag],
+        [
+            pltpu.VMEM((2, 3, n + 4, span, cols), F32),
+            pltpu.VMEM((2, 3, n + 4, span, cols), F32),
+            pltpu.VMEM((3, n, span, cols), F32),
+            dma,
+        ],
+        anys=(0,),
+    )
+    beside = swap_phases(own_sum, 1)
+    state, own_sum = launch(
+        second_kernel,
+        [shape(2, 3, n, half, cols), shape(3, n, half, cols)],
+        [state, beside, warps, targets],
+        [pltpu.VMEM((2, 3, n + 2, span, cols), F32)],
+    )
+    beside = swap_phases(own_sum, 1)
+    (away,) = launch(send_kernel, [shape(3, n, half, cols)], [state, beside])
+    home = swap_phases(away, 2)
+    (velocity,) = launch(
+        close_kernel,
+        [shape(3, n, rows, cols)],
+        [state, beside, home],
+        [pltpu.VMEM((3, n, half, cols), F32), dma((2,))],
+        out_specs=[pl.BlockSpec(memory_space=pl.ANY)],
+    )
+    return velocity[None]
 
 
 highest = lax.Precision.HIGHEST
@@ -167,7 +651,7 @@
         P(("case", "phase"), None, "slab", None, None),
     )
     return jax.shard_map(
-        shards,
+        ring_of_four if mesh.shape["phase"] == 4 else shards,
         mesh=mesh,
         in_specs=placed,
         out_specs=P(("case", "phase"), None, "slab", None, None),

time: 167 us -> 95.9 us (0.57)
  the two profiles are of different devices: /device:TPU:0 before, /device:TPU:16 now
where the time goes in v1:
time: 95.9 us; the launch traced here: 95.6 us
  waiting for transfers between devices  51.1 us (53%)
  Pallas kernels  28 us (29%)
  starting transfers between devices  12.7 us (13%)
  local copies, waits for them, and re-layouts  3.6 us (4%)
    ppermute x7, waiting for transfers between devices, swap_phases(): lax.ppermute(values, 'phase', [(i, i ^ mask) for i in range(lax.axis_size...  30.3 us
    pallas_call x10, Pallas kernels, launch(): pl.pallas_call(body, out_shape=outs, in_specs=in_specs, out_specs=out_spe...  28 us
    ppermute x3, waiting for transfers between devices, swap_slabs(): lax.ppermute(buf_a, 'slab', swaps(count, 0))  12.6 us
    ppermute x3, waiting for transfers between devices, swap_slabs(): lax.ppermute(buf_b, 'slab', swaps(count, 1))  8.19 us
    ppermute x3, starting transfers between devices, swap_slabs(): lax.ppermute(buf_b, 'slab', swaps(count, 1))  6.3 us
    ppermute x7, starting transfers between devices, swap_phases(): lax.ppermute(values, 'phase', [(i, i ^ mask) for i in range(lax.axis_size...  4.64 us
    unnamed x8, local copies, waits for them, and re-layouts  3.6 us
  transfers between devices with their start and end apart: 13, of which 8 were waited for; matrix products, arithmetic and copies ran while one was open for 0% of the time, Pallas kernels for 13%

profile of v1, /device:TPU:16, one launch (start us, length us, event | category | flops | bytes accessed | tf_op | source)
XLA Modules:
  0.0 95.6 jit_solution(14082279636799928943)
XLA Ops:
  0.0 0.0 copy-start
  0.0 1.4 %copy-done = f32[1,3,8,64,256]{4,3,2,1,0:T(8,128)S(1)} copy-done((f32[1,3,8,64,256]{4,3,2,1,0:T(8,128)S(1)}, f32[1,3,8,64,256]{4,3,2,1,0:T(8,128)}, u32[]{:S(2)}) %copy-start) | copy-done | bytes 1572888
  1.4 0.1 shard_map.37
  1.5 1.6 %collective-permute-start = (f32[3,8,40,256]{3,2,1,0:T(8,128)S(1)}, f32[3,8,40,256]{3,2,1,0:T(8,128)S(1)}, u32[]{:S(2)}, u32[]{:S(2)}) collective-permute-start(f32[3,8,40,256]{3,2,1,0:T(8,128)S(1)} %shard_map.37), channel_id=1, source_target_pairs={{0,8},{4,12},{8,0},{12,4},{1,9},{5,13},{9,1},{13,5},{2,10},{6,14},... | collective-permute-start | bytes 2949128 | tf_op jit(solution)/shard_map/ppermute | solution.py:396
  3.1 0.0 copy-start.2
  3.1 2.2 %copy-done.2 = f32[1,16,128,512]{3,2,1,0:T(8,128)S(1)} copy-done((f32[1,16,128,512]{3,2,1,0:T(8,128)S(1)}, f32[1,16,128,512]{3,2,1,0:T(8,128)}, u32[]{:S(2)}) %copy-start.2) | copy-done | bytes 4194328
  5.2 0.0 copy-start.3
  5.2 3.2 %shard_map.39 = (f32[8,64,256]{2,1,0:T(8,128)S(1)}, f32[2,64,256]{2,1,0:T(8,128)S(1)}, f32[4,64,256]{2,1,0:T(8,128)S(1)}, f32[4,64,256]{2,1,0:T(8,128)S(1)}) custom-call(f32[16,128,512]{2,1,0:T(8,128)S(1)} %bitcast.7), custom_call_target="tpu_custom_call" | custom-call | bytes 5373952 | tf_op jit(solution)/shard_map/pallas_call | solution.py:25
  8.4 1.6 %collective-permute-start.3 = (f32[4,64,256]{2,1,0:T(8,128)S(1)}, f32[4,64,256]{2,1,0:T(8,128)S(1)}, u32[]{:S(2)}, u32[]{:S(2)}) collective-permute-start(f32[4,64,256]{2,1,0:T(8,128)S(1)} %get-tuple-element.28), channel_id=1, source_target_pairs={{0,1},{1,0},{2,3},{3,2},{4,5},{5,4},{6,7},{7,6},{8,9},{9,8},{10,11... | collective-permute-start | bytes 786440 | tf_op jit(solution)/shard_map/ppermute | solution.py:390
  10.1 1.9 %collective-permute-start.4 = (f32[4,64,256]{2,1,0:T(8,128)S(1)}, f32[4,64,256]{2,1,0:T(8,128)S(1)}, u32[]{:S(2)}, u32[]{:S(2)}) collective-permute-start(f32[4,64,256]{2,1,0:T(8,128)S(1)} %get-tuple-element.29), channel_id=1, source_target_pairs={{1,2},{2,1},{5,6},{6,5},{9,10},{10,9},{13,14},{14,13},{17,18},{18,... | collective-permute-start | bytes 786440 | tf_op jit(solution)/shard_map/ppermute | solution.py:391
  12.0 4.3 %collective-permute-done.3.got_a = f32[4,64,256]{2,1,0:T(8,128)S(1)} collective-permute-done((f32[4,64,256]{2,1,0:T(8,128)S(1)}, f32[4,64,256]{2,1,0:T(8,128)S(1)}, u32[]{:S(2)}, u32[]{:S(2)}) %collective-permute-start.3) | collective-permute-done | bytes 262176 | tf_op jit(solution)/shard_map/ppermute | solution.py:390
  16.2 3.2 %collective-permute-done.4.got_b = f32[4,64,256]{2,1,0:T(8,128)S(1)} collective-permute-done((f32[4,64,256]{2,1,0:T(8,128)S(1)}, f32[4,64,256]{2,1,0:T(8,128)S(1)}, u32[]{:S(2)}, u32[]{:S(2)}) %collective-permute-start.4) | collective-permute-done | bytes 262176 | tf_op jit(solution)/shard_map/ppermute | solution.py:391
  19.4 0.0 copy-start.1
  19.4 0.2 shard_map.40
  19.6 0.0 copy-done.3
  19.6 8.5 %shard_map.41 = (f32[8,40,256]{2,1,0:T(8,128)S(1)}, f32[8,40,256]{2,1,0:T(8,128)S(1)}) custom-call(f32[14,64,256]{2,1,0:T(8,128)S(1)} %get-tuple-element.30.ext, s32[3,8,64,256]{3,2,1,0:T(8,128)S(1)} %bitcast.8), custom_call_target="tpu_custom_call" | custom-call | bytes 3145728 | tf_op jit(solution)/shard_map/pallas_call | solution.py:25
  28.1 0.6 collective-permute-start.5
  28.7 0.0 collective-permute-start.8
  28.7 1.6 %collective-permute-start.9 = (f32[14,40,256]{2,1,0:T(8,128)S(1)}, f32[14,40,256]{2,1,0:T(8,128)S(1)}, u32[]{:S(2)}, u32[]{:S(2)}) collective-permute-start(f32[14,40,256]{2,1,0:T(8,128)S(1)} %get-tuple-element.36), channel_id=1, source_target_pairs={{0,12},{4,8},{8,4},{12,0},{1,13},{5,9},{9,5},{13,1},{2,14},{6,10},... | collective-permute-start | bytes 1720328 | tf_op jit(solution)/shard_map/ppermute | solution.py:396
  30.3 0.0 collective-permute-done.other.vel_other
  30.3 0.0 copy-done.1
  30.3 0.2 shard_map.38
  30.5 0.1 collective-permute-start.1
  30.6 2.2 %collective-permute-start.2 = (f32[2,3,2,40,256]{4,3,2,1,0:T(8,128)S(1)}, f32[2,3,2,40,256]{4,3,2,1,0:T(8,128)S(1)}, u32[]{:S(2)}, u32[]{:S(2)}) collective-permute-start(f32[2,3,2,40,256]{4,3,2,1,0:T(8,128)S(1)} %get-tuple-element.25), channel_id=1, source_target_pairs={{1,2},{2,1},{5,6},{6,5},{9,10},{10,9},{13,14},{14,13},{17,18},{18,... | collective-permute-start | bytes 1474568 | tf_op jit(solution)/shard_map/ppermute | solution.py:391
  32.8 5.9 %collective-permute-done.5.other.warp_other = f32[8,40,256]{2,1,0:T(8,128)S(1)} collective-permute-done((f32[8,40,256]{2,1,0:T(8,128)S(1)}, f32[8,40,256]{2,1,0:T(8,128)S(1)}, u32[]{:S(2)}, u32[]{:S(2)}) %collective-permute-start.5) | collective-permute-done | bytes 327712 | tf_op jit(solution)/shard_map/ppermute | solution.py:396
  38.8 0.1 collective-permute-start.6
  38.8 8.4 %collective-permute-done.6.warp_a = f32[2,2,40,256]{3,2,1,0:T(8,128)S(1)} collective-permute-done((f32[2,2,40,256]{3,2,1,0:T(8,128)S(1)}, f32[2,2,40,256]{3,2,1,0:T(8,128)S(1)}, u32[]{:S(2)}, u32[]{:S(2)}) %collective-permute-start.6) | collective-permute-done | bytes 163872 | tf_op jit(solution)/shard_map/ppermute | solution.py:390
  47.2 2.2 %collective-permute-start.7 = (f32[2,2,40,256]{3,2,1,0:T(8,128)S(1)}, f32[2,2,40,256]{3,2,1,0:T(8,128)S(1)}, u32[]{:S(2)}, u32[]{:S(2)}) collective-permute-start(f32[2,2,40,256]{3,2,1,0:T(8,128)S(1)} %get-tuple-element.34), channel_id=1, source_target_pairs={{1,2},{2,1},{5,6},{6,5},{9,10},{10,9},{13,14},{14,13},{17,18},{18,... | collective-permute-start | bytes 491528 | tf_op jit(solution)/shard_map/ppermute | solution.py:391
  49.4 5.0 %collective-permute-done.7.warp_b = f32[2,2,40,256]{3,2,1,0:T(8,128)S(1)} collective-permute-done((f32[2,2,40,256]{3,2,1,0:T(8,128)S(1)}, f32[2,2,40,256]{3,2,1,0:T(8,128)S(1)}, u32[]{:S(2)}, u32[]{:S(2)}) %collective-permute-start.7) | collective-permute-done | bytes 163872 | tf_op jit(solution)/shard_map/ppermute | solution.py:391
  54.4 0.0 collective-permute-done.8.chip
  54.4 0.0 collective-permute-done.9.diag
  54.4 0.0 collective-permute-done.1.vel_a
  54.4 0.0 collective-permute-done.2.vel_b
  54.4 8.6 %shard_map.43 = (f32[2,3,10,40,256]{4,3,2,1,0:T(8,128)}, f32[3,10,40,256]{3,2,1,0:T(8,128)}, f32[2,12,40,256]{3,2,1,0:T(8,128)S(1)}, f32[2,14,40,256]{3,2,1,0:T(8,128)S(1)}) custom-call(f32[3,8,64,256]{3,2,1,0:T(8,128)} %bitcast.4, f32[3,8,40,256]{3,2,1,0:T(8,128)S(1)} %collective-permute-done.other.vel_other, ...), custom_call_target="tpu_custom_call" | custom-call | bytes 11485184 | tf_op jit(solution)/shard_map/pallas_call | solution.py:25
  63.0 0.1 collective-permute-start.10
  63.1 3.1 %collective-permute-done.10.beside = f32[3,10,40,256]{3,2,1,0:T(8,128)S(1)} collective-permute-done((f32[3,10,40,256]{3,2,1,0:T(8,128)}, f32[3,10,40,256]{3,2,1,0:T(8,128)S(1)}, u32[]{:S(2)}, u32[]{:S(2)}) %collective-permute-start.10) | collective-permute-done | bytes 1228832 | tf_op jit(solution)/shard_map/ppermute | solution.py:396
  66.2 6.1 %shard_map.44 = (f32[2,3,8,32,256]{4,3,2,1,0:T(8,128)S(1)}, f32[3,8,32,256]{3,2,1,0:T(8,128)S(1)}) custom-call(f32[2,3,10,40,256]{4,3,2,1,0:T(8,128)} %get-tuple-element.37.vel, f32[3,10,40,256]{3,2,1,0:T(8,128)S(1)} %collective-permute-done.10.beside, f32[2,12,40,256]{3,2,1,0:T(8,128)S(1)} %get-tuple-element.39.warps, ...), custom_call_target="tpu_custom_call" | custom-call | bytes 8175616 | tf_op jit(solution)/shard_map/pallas_call | solution.py:25
  72.3 0.2 collective-permute-start.11
  72.5 2.1 %collective-permute-done.11.beside = f32[3,8,32,256]{3,2,1,0:T(8,128)S(1)} collective-permute-done((f32[3,8,32,256]{3,2,1,0:T(8,128)S(1)}, f32[3,8,32,256]{3,2,1,0:T(8,128)S(1)}, u32[]{:S(2)}, u32[]{:S(2)}) %collective-permute-start.11) | collective-permute-done | bytes 786464 | tf_op jit(solution)/shard_map/ppermute | solution.py:396
  74.7 0.1 shard_map.45
  74.8 0.6 collective-permute-start.12
  75.4 19.0 %collective-permute-done.12.other = f32[3,8,32,256]{3,2,1,0:T(8,128)S(1)} collective-permute-done((f32[3,8,32,256]{3,2,1,0:T(8,128)S(1)}, f32[3,8,32,256]{3,2,1,0:T(8,128)S(1)}, u32[]{:S(2)}, u32[]{:S(2)}) %collective-permute-start.12) | collective-permute-done | bytes 786464 | tf_op jit(solution)/shard_map/ppermute | solution.py:396
  94.4 1.2 %shard_map.46 = f32[3,8,64,256]{3,2,1,0:T(8,128)} custom-call(f32[2,3,8,32,256]{4,3,2,1,0:T(8,128)S(1)} %get-tuple-element.41.vel, f32[3,8,32,256]{3,2,1,0:T(8,128)S(1)} %collective-permute-done.11.beside, f32[3,8,32,256]{3,2,1,0:T(8,128)S(1)} %collective-permute-done.12.other), custom_call_target="tpu_custom_call" | custom-call | bytes 4718592 | tf_op jit(solution)/shard_map/pallas_call | solution.py:25
  (1 shorter events, 0.0 us)
Async XLA Ops:
  0.0 1.4 %copy-start = (f32[1,3,8,64,256]{4,3,2,1,0:T(8,128)S(1)}, f32[1,3,8,64,256]{4,3,2,1,0:T(8,128)}, u32[]{:S(2)}) copy-start(f32[1,3,8,64,256]{4,3,2,1,0:T(8,128)} %param.5) | copy-start | bytes 4718596
  1.5 28.8 %collective-permute-start = (f32[3,8,40,256]{3,2,1,0:T(8,128)S(1)}, f32[3,8,40,256]{3,2,1,0:T(8,128)S(1)}, u32[]{:S(2)}, u32[]{:S(2)}) collective-permute-start(f32[3,8,40,256]{3,2,1,0:T(8,128)S(1)} %shard_map.37), channel_id=1, source_target_pairs={{0,8},{4,12},{8,0},{12,4},{1,9},{5,13},{9,1},{13,5},{2,10},{6,14},... | collective-permute-start | bytes 2949128 | tf_op jit(solution)/shard_map/ppermute | solution.py:396
  3.1 2.2 %copy-start.2 = (f32[1,16,128,512]{3,2,1,0:T(8,128)S(1)}, f32[1,16,128,512]{3,2,1,0:T(8,128)}, u32[]{:S(2)}) copy-start(f32[1,16,128,512]{3,2,1,0:T(8,128)} %param.3) | copy-start | bytes 12582916
  5.2 14.4 %copy-start.3 = (s32[1,3,8,64,256]{4,3,2,1,0:T(8,128)S(1)}, s32[1,3,8,64,256]{4,3,2,1,0:T(8,128)}, u32[]{:S(2)}) copy-start(s32[1,3,8,64,256]{4,3,2,1,0:T(8,128)} %param.4) | copy-start | bytes 4718596
  8.4 7.8 %collective-permute-start.3 = (f32[4,64,256]{2,1,0:T(8,128)S(1)}, f32[4,64,256]{2,1,0:T(8,128)S(1)}, u32[]{:S(2)}, u32[]{:S(2)}) collective-permute-start(f32[4,64,256]{2,1,0:T(8,128)S(1)} %get-tuple-element.28), channel_id=1, source_target_pairs={{0,1},{1,0},{2,3},{3,2},{4,5},{5,4},{6,7},{7,6},{8,9},{9,8},{10,11... | collective-permute-start | bytes 786440 | tf_op jit(solution)/shard_map/ppermute | solution.py:390
  10.1 9.4 %collective-permute-start.4 = (f32[4,64,256]{2,1,0:T(8,128)S(1)}, f32[4,64,256]{2,1,0:T(8,128)S(1)}, u32[]{:S(2)}, u32[]{:S(2)}) collective-permute-start(f32[4,64,256]{2,1,0:T(8,128)S(1)} %get-tuple-element.29), channel_id=1, source_target_pairs={{1,2},{2,1},{5,6},{6,5},{9,10},{10,9},{13,14},{14,13},{17,18},{18,... | collective-permute-start | bytes 786440 | tf_op jit(solution)/shard_map/ppermute | solution.py:391
  19.4 10.9 %copy-start.1 = (f32[1,3,8,64,256]{4,3,2,1,0:T(8,128)S(1)}, f32[1,3,8,64,256]{4,3,2,1,0:T(8,128)}, u32[]{:S(2)}) copy-start(f32[1,3,8,64,256]{4,3,2,1,0:T(8,128)} %param.5) | copy-start | bytes 4718596
  28.1 10.6 %collective-permute-start.5 = (f32[8,40,256]{2,1,0:T(8,128)S(1)}, f32[8,40,256]{2,1,0:T(8,128)S(1)}, u32[]{:S(2)}, u32[]{:S(2)}) collective-permute-start(f32[8,40,256]{2,1,0:T(8,128)S(1)} %get-tuple-element.32), channel_id=1, source_target_pairs={{0,8},{4,12},{8,0},{12,4},{1,9},{5,13},{9,1},{13,5},{2,10},{6,14},... | collective-permute-start | bytes 983048 | tf_op jit(solution)/shard_map/ppermute | solution.py:396
  28.7 25.7 %collective-permute-start.8 = (f32[14,40,256]{2,1,0:T(8,128)S(1)}, f32[14,40,256]{2,1,0:T(8,128)S(1)}, u32[]{:S(2)}, u32[]{:S(2)}) collective-permute-start(f32[14,40,256]{2,1,0:T(8,128)S(1)} %get-tuple-element.35), channel_id=1, source_target_pairs={{0,4},{4,0},{8,12},{12,8},{1,5},{5,1},{9,13},{13,9},{2,6},{6,2},{1... | collective-permute-start | bytes 1720328 | tf_op jit(solution)/shard_map/ppermute | solution.py:396
  28.7 25.7 %collective-permute-start.9 = (f32[14,40,256]{2,1,0:T(8,128)S(1)}, f32[14,40,256]{2,1,0:T(8,128)S(1)}, u32[]{:S(2)}, u32[]{:S(2)}) collective-permute-start(f32[14,40,256]{2,1,0:T(8,128)S(1)} %get-tuple-element.36), channel_id=1, source_target_pairs={{0,12},{4,8},{8,4},{12,0},{1,13},{5,9},{9,5},{13,1},{2,14},{6,10},... | collective-permute-start | bytes 1720328 | tf_op jit(solution)/shard_map/ppermute | solution.py:396
  30.5 23.9 %collective-permute-start.1 = (f32[2,3,2,40,256]{4,3,2,1,0:T(8,128)S(1)}, f32[2,3,2,40,256]{4,3,2,1,0:T(8,128)S(1)}, u32[]{:S(2)}, u32[]{:S(2)}) collective-permute-start(f32[2,3,2,40,256]{4,3,2,1,0:T(8,128)S(1)} %get-tuple-element.24), channel_id=1, source_target_pairs={{0,1},{1,0},{2,3},{3,2},{4,5},{5,4},{6,7},{7,6},{8,9},{9,8},{10,11... | collective-permute-start | bytes 1474568 | tf_op jit(solution)/shard_map/ppermute | solution.py:390
  30.6 23.8 %collective-permute-start.2 = (f32[2,3,2,40,256]{4,3,2,1,0:T(8,128)S(1)}, f32[2,3,2,40,256]{4,3,2,1,0:T(8,128)S(1)}, u32[]{:S(2)}, u32[]{:S(2)}) collective-permute-start(f32[2,3,2,40,256]{4,3,2,1,0:T(8,128)S(1)} %get-tuple-element.25), channel_id=1, source_target_pairs={{1,2},{2,1},{5,6},{6,5},{9,10},{10,9},{13,14},{14,13},{17,18},{18,... | collective-permute-start | bytes 1474568 | tf_op jit(solution)/shard_map/ppermute | solution.py:391
  38.8 8.4 %collective-permute-start.6 = (f32[2,2,40,256]{3,2,1,0:T(8,128)S(1)}, f32[2,2,40,256]{3,2,1,0:T(8,128)S(1)}, u32[]{:S(2)}, u32[]{:S(2)}) collective-permute-start(f32[2,2,40,256]{3,2,1,0:T(8,128)S(1)} %get-tuple-element.33), channel_id=1, source_target_pairs={{0,1},{1,0},{2,3},{3,2},{4,5},{5,4},{6,7},{7,6},{8,9},{9,8},{10,11... | collective-permute-start | bytes 491528 | tf_op jit(solution)/shard_map/ppermute | solution.py:390
  47.2 7.2 %collective-permute-start.7 = (f32[2,2,40,256]{3,2,1,0:T(8,128)S(1)}, f32[2,2,40,256]{3,2,1,0:T(8,128)S(1)}, u32[]{:S(2)}, u32[]{:S(2)}) collective-permute-start(f32[2,2,40,256]{3,2,1,0:T(8,128)S(1)} %get-tuple-element.34), channel_id=1, source_target_pairs={{1,2},{2,1},{5,6},{6,5},{9,10},{10,9},{13,14},{14,13},{17,18},{18,... | collective-permute-start | bytes 491528 | tf_op jit(solution)/shard_map/ppermute | solution.py:391
  63.0 3.2 %collective-permute-start.10 = (f32[3,10,40,256]{3,2,1,0:T(8,128)}, f32[3,10,40,256]{3,2,1,0:T(8,128)S(1)}, u32[]{:S(2)}, u32[]{:S(2)}) collective-permute-start(f32[3,10,40,256]{3,2,1,0:T(8,128)} %get-tuple-element.38), channel_id=1, source_target_pairs={{0,4},{4,0},{8,12},{12,8},{1,5},{5,1},{9,13},{13,9},{2,6},{6,2},{1... | collective-permute-start | bytes 3686408 | tf_op jit(solution)/shard_map/ppermute | solution.py:396
  72.3 2.4 %collective-permute-start.11 = (f32[3,8,32,256]{3,2,1,0:T(8,128)S(1)}, f32[3,8,32,256]{3,2,1,0:T(8,128)S(1)}, u32[]{:S(2)}, u32[]{:S(2)}) collective-permute-start(f32[3,8,32,256]{3,2,1,0:T(8,128)S(1)} %get-tuple-element.42), channel_id=1, source_target_pairs={{0,4},{4,0},{8,12},{12,8},{1,5},{5,1},{9,13},{13,9},{2,6},{6,2},{1... | collective-permute-start | bytes 2359304 | tf_op jit(solution)/shard_map/ppermute | solution.py:396
  74.8 19.6 %collective-permute-start.12 = (f32[3,8,32,256]{3,2,1,0:T(8,128)S(1)}, f32[3,8,32,256]{3,2,1,0:T(8,128)S(1)}, u32[]{:S(2)}, u32[]{:S(2)}) collective-permute-start(f32[3,8,32,256]{3,2,1,0:T(8,128)S(1)} %shard_map.45), channel_id=1, source_target_pairs={{0,8},{4,12},{8,0},{12,4},{1,9},{5,13},{9,1},{13,5},{2,10},{6,14},... | collective-permute-start | bytes 2359304 | tf_op jit(solution)/shard_map/ppermute | solution.py:396

commit v2 on v1

--- a/solution.py
+++ b/solution.py
@@ -1,5 +1,3 @@
-import functools
-
 import jax
 import jax.numpy as jnp
 from jax import lax
@@ -7,31 +5,28 @@
 from jax.experimental.pallas import tpu as pltpu
 from jax.sharding import PartitionSpec as P
 
+
 ITERS = 2
 RIM = 8
 F32 = jnp.float32
 BF16 = jnp.bfloat16
 
 
-def launch(body, outs, ins, scratch=(), anys=(), grid=None, in_specs=None, out_specs=None, flops=0):
-    vmem = pl.BlockSpec(memory_space=pltpu.VMEM)
-    anym = pl.BlockSpec(memory_space=pl.ANY)
-    if in_specs is None:
-        in_specs = [anym if i in anys else vmem for i in range(len(ins))]
-    if out_specs is None:
-        out_specs = [vmem for _ in outs]
-    moved = sum(4 * x.size for x in ins) + sum(4 * o.size for o in outs)
-    params = dict(grid=grid) if grid is not None else {}
+def launch(body, outs, ins, scratch=(), hbm=(), hbm_out=(), micros=1.0, limit=16, alias={}):
+    spaces = [pltpu.HBM if i in hbm else pltpu.VMEM for i in range(len(ins))]
+    targets = [pl.ANY if i in hbm_out else pltpu.VMEM for i in range(len(outs))]
     return pl.pallas_call(
         body,
         out_shape=outs,
-        in_specs=in_specs,
-        out_specs=out_specs,
+        in_specs=[pl.BlockSpec(memory_space=space) for space in spaces],
+        out_specs=[pl.BlockSpec(memory_space=space) for space in targets],
         scratch_shapes=scratch,
-        compiler_params=pltpu.CompilerParams(vmem_limit_bytes=48 * 2**20),
-        cost_estimate=pl.CostEstimate(flops=flops, bytes_accessed=moved, transcendentals=0),
-        **params,
-    )(*ins)
+        input_output_aliases=alias,
+        compiler_params=pltpu.CompilerParams(vmem_limit_bytes=limit * 2**20),
+        cost_estimate=pl.CostEstimate(
+            flops=0, bytes_accessed=int(micros * 3.3e6), transcendentals=0
+        ),
+    )(*[pltpu.with_memory_space_constraint(v, pltpu.HBM) if i in hbm and i not in alias else v for i, v in enumerate(ins)])
 
 
 def shape(*dims):
@@ -62,64 +57,92 @@
     return jnp.where(keep, moved, 0.0)
 
 
-def halve_kernel(fine, part, edge, buf_a, buf_b, mat, rows, prev):
-    k = pl.program_id(0)
-    last = pl.num_programs(0) - 1
-    deep, tall, wide = fine.shape
-
-    @pl.when(k == 0)
-    def _():
-        i = lax.broadcasted_iota(jnp.int32, mat.shape, 0)
-        j = lax.broadcasted_iota(jnp.int32, mat.shape, 1)
-        d = i - 2 * j
-        inner = (d == 0) | (d == 1)
-        outer = (d == -1) | (d == 2)
-        mat[...] = jnp.where(inner, 0.375, jnp.where(outer, 0.125, 0.0)).astype(BF16)
-
-    f = fine[...].reshape(deep * tall, wide)
-    hi = f.astype(BF16)
-    lo = (f - hi.astype(F32)).astype(BF16)
-    w = mat[...]
-    got = jnp.dot(hi, w, preferred_element_type=F32) + jnp.dot(lo, w, preferred_element_type=F32)
-    half = tall // 2
+def halve_kernel(fine, part, edge, buf_a, buf_b, held, mat, rows, prev, sems):
+    count, tall, wide = fine.shape
+    n, half = count // 2, tall // 2
     cut = rows.shape[2]
-    for c in range(rows.shape[0]):
-        rows[c] = got[:, c * cut : (c + 1) * cut]
-    layers = []
-    for z in range(deep):
-        cols = []
+
+    def fetch(k):
+        pair = pl.ds(2 * k, 2)
+        return pltpu.make_async_copy(fine.at[pair], held.at[pair], sems.at[k])
+
+    for k in range(n):
+        fetch(k).start()
+    i = lax.broadcasted_iota(jnp.int32, mat.shape, 0)
+    j = lax.broadcasted_iota(jnp.int32, mat.shape, 1)
+    d = i - 2 * j
+    inner = (d == 0) | (d == 1)
+    outer = (d == -1) | (d == 2)
+    mat[...] = jnp.where(inner, 0.375, jnp.where(outer, 0.125, 0.0)).astype(BF16)
+
+    def pair(k, carry):
+        fetch(k).wait()
+        f = held[pl.ds(2 * k, 2)].reshape(2 * tall, wide)
+        hi = f.astype(BF16)
+        lo = (f - hi.astype(F32)).astype(BF16)
+        w = mat[...]
+        got = jnp.dot(hi, w, preferred_element_type=F32)
+        got += jnp.dot(lo, w, preferred_element_type=F32)
         for c in range(rows.shape[0]):
-            even = rows[c, pl.ds(z * tall, half, 2), :]
-            odd = rows[c, pl.ds(z * tall + 1, half, 2), :]
-            cols.append(
-                (shift_rows(odd, False) + shift_rows(even, True) + 3.0 * (even + odd)) * (1.0 / 64.0)
-            )
-        layers.append(jnp.concatenate(cols, 1))
-    even, odd = layers
-    mid = 3.0 * (even + odd)
-
-    @pl.when(k == 0)
-    def _():
-        edge[0] = even
-        part[0] = mid
-
-    @pl.when(k > 0)
-    def _():
-        part[k] = mid + prev[...]
-        part[k - 1] += even
-
-    prev[...] = odd
-
-    @pl.when(k == last)
-    def _():
-        edge[1] = odd
-        parity, _, _ = slab_place()
-        n = part.shape[0]
-        for i in range(4):
-            above = odd if i == 3 else part[n - 3 + i]
-            below = edge[0] if i == 0 else part[i - 1]
-            buf_a[i] = jnp.where(parity == 0, above, below)
-            buf_b[i] = jnp.where(parity == 0, below, above)
+            rows[c] = got[:, c * cut : (c + 1) * cut]
+        layers = []
+        for z in range(2):
+            cols = []
+            for c in range(rows.shape[0]):
+                even = rows[c, pl.ds(z * tall, half, 2), :]
+                odd = rows[c, pl.ds(z * tall + 1, half, 2), :]
+                cols.append(
+                    (shift_rows(odd, False) + shift_rows(even, True) + 3.0 * (even + odd))
+                    * (1.0 / 64.0)
+                )
+            layers.append(jnp.concatenate(cols, 1))
+        even, odd = layers
+        mid = 3.0 * (even + odd)
+
+        @pl.when(k == 0)
+        def _():
+            edge[0] = even
+            part[0] = mid
+
+        @pl.when(k > 0)
+        def _():
+            part[k] = mid + prev[...]
+            part[k - 1] += even
+
+        prev[...] = odd
+        return carry
+
+    lax.fori_loop(0, n, pair, 0)
+    edge[1] = prev[...]
+    parity, _, _ = slab_place()
+    for i in range(4):
+        above = edge[1] if i == 3 else part[n - 3 + i]
+        below = edge[0] if i == 0 else part[i - 1]
+        buf_a[i] = jnp.where(parity == 0, above, below)
+        buf_b[i] = jnp.where(parity == 0, below, above)
+
+
+def pack(dst, layer, count, chip, half):
+    low = lax.broadcasted_iota(jnp.int32, (8, dst.shape[1]), 0) < 4
+    mine = low == (chip == 0)
+    main = pl.multiple_of(8 * chip, 8)
+    rim = pl.multiple_of(half * (1 - chip), 8)
+    for i in range(count):
+        dst[pl.ds(i * half, half), :] = layer(i, main, half)
+    for i in range(0, count, 2):
+        a, b = layer(i, rim, 8), layer(i + 1, rim, 8)
+        dst[pl.ds(count * half + 4 * i, 8), :] = jnp.where(mine, a, pltpu.roll(b, 4, 0))
+
+
+def unpack(src, store, count, chip, half):
+    main = pl.multiple_of(8 * chip, 8)
+    rim = pl.multiple_of(half * (1 - chip), 8)
+    for i in range(count):
+        store(i, main, half, src[pl.ds(i * half, half), :])
+    for i in range(0, count, 2):
+        v = src[pl.ds(count * half + 4 * i, 8), :]
+        store(i, rim, 8, v)
+        store(i + 1, rim, 8, pltpu.roll(v, 4, 0))
 
 
 def join_kernel(part, edge, got_a, got_b, ext, near, far):
@@ -145,7 +168,12 @@
     span = near.shape[1]
     step = ext.shape[1] - span
     near[...] = ext[:, pl.ds(pl.multiple_of(x * step, 8), span), :]
-    far[...] = ext[:, pl.ds(pl.multiple_of((1 - x) * step, 8), span), :]
+    there = (1 - x) * step
+
+    def layer(i, start, size):
+        return ext[i + 3, pl.ds(pl.multiple_of(there + start, 8), size), :]
+
+    pack(far, layer, n, 1 - x, ext.shape[1] // 2)
 
 
 def warp_kernel(ext, offs, near, far, wide, full):
@@ -195,25 +223,34 @@
     span = near.shape[1]
     step = tall - span
     near[...] = full[:, pl.ds(pl.multiple_of(x * step, 8), span), :]
-    far[...] = full[:, pl.ds(pl.multiple_of((1 - x) * step, 8), span), :]
-
-
-def cut_kernel(vel, far, sem):
-    x, _ = chip_and_core()
-    span = far.shape[2]
-    step = vel.shape[2] - span
-    copy = pltpu.make_async_copy(
-        vel.at[:, :, pl.ds(pl.multiple_of((1 - x) * step, 8), span), :], far, sem
-    )
+    there = (1 - x) * step
+
+    def layer(i, start, size):
+        return full[i, pl.ds(pl.multiple_of(there + start, 8), size), :]
+
+    pack(far, layer, n, 1 - x, tall // 2)
+
+
+def cut_kernel(vel, far, held, sem):
+    x, _ = chip_and_core()
+    n, tall = vel.shape[1:3]
+    span = held.shape[2]
+    there = pl.multiple_of((1 - x) * (tall - span), 8)
+    copy = pltpu.make_async_copy(vel.at[:, :, pl.ds(there, span), :], held, sem)
     copy.start()
     copy.wait()
 
-
-def rim_velocity_kernel(vel, other, buf_a, buf_b, stage, sem):
+    def layer(i, start, size):
+        return held[i // n, i % n, pl.ds(start, size), :]
+
+    pack(far, layer, 3 * n, 1 - x, tall // 2)
+
+
+def rim_own_kernel(vel, buf_a, buf_b, stage, sem):
     x, _ = chip_and_core()
     parity, _, _ = slab_place()
     n = vel.shape[1]
-    span = other.shape[2]
+    span = stage.shape[3]
     start = pl.multiple_of(x * (vel.shape[2] - span), 8)
     copies = [
         pltpu.make_async_copy(vel.at[:, pl.ds(z, 2), pl.ds(start, span), :], stage.at[j], sem.at[j])
@@ -223,18 +260,45 @@
         copy.start()
     for copy in copies:
         copy.wait()
-    for m in range(2):
-        for comp in range(3):
-            for i in range(2):
-                below = stage[0, comp, i] if m == 0 else other[comp, i]
-                above = stage[1, comp, i] if m == 0 else other[comp, n - 2 + i]
-                buf_a[m, comp, i] = jnp.where(parity == 0, above, below)
-                buf_b[m, comp, i] = jnp.where(parity == 0, below, above)
-
-
-def rim_warp_kernel(near, other, buf_a, buf_b):
+    below, above = stage[0], stage[1]
+    buf_a[...] = jnp.where(parity == 0, above, below)
+    buf_b[...] = jnp.where(parity == 0, below, above)
+
+
+def rim_other_kernel(vel_far, diag_far, buf_a, buf_b, vel_other, diag):
+    x, _ = chip_and_core()
     parity, _, _ = slab_place()
-    n = near.shape[0]
+    n, span = vel_other.shape[1:3]
+    half = span - RIM
+
+    def store_vel(i, start, size, v):
+        vel_other[i // n, i % n, pl.ds(start, size), :] = v
+
+    def store_diag(i, start, size, v):
+        diag[i, pl.ds(start, size), :] = v
+
+    unpack(vel_far, store_vel, 3 * n, x, half)
+    unpack(diag_far, store_diag, n, x, half)
+    for comp in range(3):
+        for i in range(2):
+            below, above = vel_other[comp, i], vel_other[comp, n - 2 + i]
+            buf_a[2 * comp + i] = jnp.where(parity == 0, above, below)
+            buf_b[2 * comp + i] = jnp.where(parity == 0, below, above)
+    for i in range(3):
+        below, above = diag[i], diag[n - 3 + i]
+        buf_a[6 + i] = jnp.where(parity == 0, above, below)
+        buf_b[6 + i] = jnp.where(parity == 0, below, above)
+
+
+def rim_warp_kernel(near, far, buf_a, buf_b, other):
+    x, _ = chip_and_core()
+    parity, _, _ = slab_place()
+    n, span = near.shape[:2]
+
+    def store(i, start, size, v):
+        other[i, pl.ds(start, size), :] = v
+
+    unpack(far, store, n, x, span - RIM)
     for m in range(2):
         ref = near if m == 0 else other
         for i in range(2):
@@ -264,7 +328,7 @@
 
 
 def first_kernel(
-    vel, vel_other, vel_a, vel_b, warp, warp_other, warp_a, warp_b, chip, diag,
+    vel, vel_other, own_a, own_b, rim_a, rim_b, warp, warp_other, warp_a, warp_b, chip, diag,
     out, out_sum, warps, targets, held, moved, stage, sem,
 ):
     x, core = chip_and_core()
@@ -274,7 +338,13 @@
     copy = pltpu.make_async_copy(vel.at[:, :, pl.ds(start, span), :], stage, sem)
     copy.start()
     for i in range(n + 6):
-        a, b = chip[i], diag[i]
+        a = chip[i]
+        if i < 3:
+            b = pick(parity, rim_a[6 + i], rim_b[6 + i], False)
+        elif i < n + 3:
+            b = diag[i - 3]
+        else:
+            b = pick(parity, rim_a[3 + i - n], rim_b[3 + i - n], True)
         targets[0, i] = jnp.where(core == 0, a, b)
         targets[1, i] = jnp.where(core == 0, b, a)
     for m in range(2):
@@ -289,8 +359,9 @@
         ref = stage if m == 0 else vel_other
         for comp in range(3):
             for i in range(2):
-                held[m, comp, i] = pick(parity, vel_a[m, comp, i], vel_b[m, comp, i], False)
-                held[m, comp, n + 2 + i] = pick(parity, vel_a[m, comp, i], vel_b[m, comp, i], True)
+                a, b = (own_a[comp, i], own_b[comp, i]) if m == 0 else (rim_a[2 * comp + i], rim_b[2 * comp + i])
+                held[m, comp, i] = pick(parity, a, b, False)
+                held[m, comp, n + 2 + i] = pick(parity, a, b, True)
             for i in range(n):
                 held[m, comp, i + 2] = ref[comp, i]
     deep = n + 4
@@ -361,19 +432,25 @@
     out[...] = (2.0 * vel[1] + beside[...]) * 0.25
 
 
-def close_kernel(vel, beside, other, out, stage, sem):
+def close_own_kernel(vel, beside, out, stage, sem):
     x, _ = chip_and_core()
     half = stage.shape[2]
-    there = pltpu.make_async_copy(
-        other, out.at[:, :, pl.ds(pl.multiple_of((1 - x) * half, 8), half), :], sem.at[0]
-    )
-    there.start()
     stage[...] = (2.0 * vel[0] + beside[...]) * 0.25
     here = pltpu.make_async_copy(
-        stage, out.at[:, :, pl.ds(pl.multiple_of(x * half, 8), half), :], sem.at[1]
+        stage, out.at[:, :, pl.ds(pl.multiple_of(x * half, 8), half), :], sem
     )
     here.start()
     here.wait()
+
+
+def close_far_kernel(done, home, out, sem):
+    del done
+    x, _ = chip_and_core()
+    half = home.shape[2]
+    there = pltpu.make_async_copy(
+        home, out.at[:, :, pl.ds(pl.multiple_of((1 - x) * half, 8), half), :], sem
+    )
+    there.start()
     there.wait()
 
 
@@ -386,10 +463,9 @@
 
 def swap_slabs(buf_a, buf_b):
     count = lax.axis_size("slab")
-    return (
-        lax.ppermute(buf_a, "slab", swaps(count, 0)),
-        lax.ppermute(buf_b, "slab", swaps(count, 1)),
-    )
+    got_a = lax.ppermute(buf_a, "slab", swaps(count, 0))
+    got_b = lax.ppermute(buf_b, "slab", swaps(count, 1))
+    return got_a, got_b
 
 
 def swap_phases(values, mask):
@@ -397,6 +473,10 @@
 
 
 def ring_of_four(fine_images, offsets, velocity_init):
+    return four_phases(fine_images, offsets, velocity_init)
+
+
+def four_phases(fine_images, offsets, velocity_init):
     fine, offs, vel = fine_images[0], offsets[0], velocity_init[0]
     deep, tall, wide = fine.shape
     n, rows, cols = offs.shape[1:]
@@ -405,52 +485,70 @@
     lanes = 128
     dma = pltpu.SemaphoreType.DMA
 
-    (vel_far,) = launch(cut_kernel, [shape(3, n, span, cols)], [vel], [dma], anys=(0,))
-    vel_other = swap_phases(vel_far, 2)
-
-    full = lambda *dims: pl.BlockSpec(dims, lambda k: (0,) * len(dims))
+    (vel_cut,) = launch(
+        cut_kernel,
+        [shape(3 * n * (half + 4), cols)],
+        [vel],
+        [pltpu.VMEM((3, n, span, cols), F32), dma],
+        hbm=(0,),
+        micros=1.0,
+    )
+    vel_far = swap_phases(vel_cut, 2)
+
     part, edge, buf_a, buf_b = launch(
         halve_kernel,
         [shape(n, rows, cols), shape(2, rows, cols), shape(4, rows, cols), shape(4, rows, cols)],
         [fine],
         [
+            pltpu.VMEM((deep, tall, wide), F32),
             pltpu.VMEM((wide, cols), BF16),
             pltpu.VMEM((cols // lanes, 2 * tall, lanes), F32),
             pltpu.VMEM((rows, cols), F32),
+            dma((n,)),
         ],
-        grid=(n,),
-        in_specs=[pl.BlockSpec((2, tall, wide), lambda k: (k, 0, 0))],
-        out_specs=[full(n, rows, cols), full(2, rows, cols), full(4, rows, cols), full(4, rows, cols)],
+        hbm=(0,),
+        micros=4.0,
     )
     got_a, got_b = swap_slabs(buf_a, buf_b)
+    buf_a, buf_b = launch(
+        rim_own_kernel,
+        [shape(3, 2, span, cols)] * 2,
+        [vel],
+        [pltpu.VMEM((2, 3, 2, span, cols), F32), dma((2,))],
+        hbm=(0,),
+    )
+    own_a, own_b = swap_slabs(buf_a, buf_b)
     ext, near, far = launch(
         join_kernel,
-        [shape(n + 6, rows, cols), shape(n + 6, span, cols), shape(n + 6, span, cols)],
+        [shape(n + 6, rows, cols), shape(n + 6, span, cols), shape(n * (half + 4), cols)],
         [part, edge, got_a, got_b],
     )
     chip = swap_phases(near, 1)
-    diag = swap_phases(far, 3)
-
-    warp, warp_far = launch(
+    diag_far = swap_phases(far, 3)
+
+    warp, warp_cut = launch(
         warp_kernel,
-        [shape(n, span, cols), shape(n, span, cols)],
+        [shape(n, span, cols), shape(n * (half + 4), cols)],
         [ext, offs],
         [
             pltpu.VMEM((5, cols // lanes, n + 4, rows + 16, lanes), F32),
             pltpu.VMEM((n, rows, cols), F32),
         ],
-    )
-    warp_other = swap_phases(warp_far, 2)
-
-    buf_a, buf_b = launch(
-        rim_velocity_kernel,
-        [shape(2, 3, 2, span, cols)] * 2,
-        [vel, vel_other],
-        [pltpu.VMEM((2, 3, 2, span, cols), F32), dma((2,))],
-        anys=(0,),
-    )
-    vel_a, vel_b = swap_slabs(buf_a, buf_b)
-    buf_a, buf_b = launch(rim_warp_kernel, [shape(2, 2, span, cols)] * 2, [warp, warp_other])
+        micros=8.5,
+    )
+    warp_far = swap_phases(warp_cut, 2)
+
+    buf_a, buf_b, vel_other, diag = launch(
+        rim_other_kernel,
+        [shape(9, span, cols)] * 2 + [shape(3, n, span, cols), shape(n, span, cols)],
+        [vel_far, diag_far],
+    )
+    rim_a, rim_b = swap_slabs(buf_a, buf_b)
+    buf_a, buf_b, warp_other = launch(
+        rim_warp_kernel,
+        [shape(2, 2, span, cols)] * 2 + [shape(n, span, cols)],
+        [warp, warp_far],
+    )
     warp_a, warp_b = swap_slabs(buf_a, buf_b)
 
     state, own_sum, warps, targets = launch(
@@ -461,14 +559,15 @@
             shape(2, n + 4, span, cols),
             shape(2, n + 6, span, cols),
         ],
-        [vel, vel_other, vel_a, vel_b, warp, warp_other, warp_a, warp_b, chip, diag],
+        [vel, vel_other, own_a, own_b, rim_a, rim_b, warp, warp_other, warp_a, warp_b, chip, diag],
         [
             pltpu.VMEM((2, 3, n + 4, span, cols), F32),
             pltpu.VMEM((2, 3, n + 4, span, cols), F32),
             pltpu.VMEM((3, n, span, cols), F32),
             dma,
         ],
-        anys=(0,),
+        hbm=(0,),
+        micros=5.0,
     )
     beside = swap_phases(own_sum, 1)
     state, own_sum = launch(
@@ -476,16 +575,26 @@
         [shape(2, 3, n, half, cols), shape(3, n, half, cols)],
         [state, beside, warps, targets],
         [pltpu.VMEM((2, 3, n + 2, span, cols), F32)],
+        micros=4.0,
     )
     beside = swap_phases(own_sum, 1)
     (away,) = launch(send_kernel, [shape(3, n, half, cols)], [state, beside])
     home = swap_phases(away, 2)
     (velocity,) = launch(
-        close_kernel,
+        close_own_kernel,
         [shape(3, n, rows, cols)],
-        [state, beside, home],
-        [pltpu.VMEM((3, n, half, cols), F32), dma((2,))],
-        out_specs=[pl.BlockSpec(memory_space=pl.ANY)],
+        [state, beside],
+        [pltpu.VMEM((3, n, half, cols), F32), dma],
+        hbm_out=(0,),
+    )
+    (velocity,) = launch(
+        close_far_kernel,
+        [shape(3, n, rows, cols)],
+        [velocity, home],
+        [dma],
+        hbm=(0,),
+        hbm_out=(0,),
+        alias={0: 0},
     )
     return velocity[None]
 
@@ -624,7 +733,7 @@
     smooth_rows = smooth_matrix(height)
     smooth_columns = smooth_matrix(breadth)
     velocity = velocity_init
-    for iteration in range(ITERS):
+    for _ in range(ITERS):
         warped = (
             warped_base
             + velocity[:, 0] * grad_z
@@ -650,8 +759,9 @@
         P(("case", "phase"), None, "slab", None, None),
         P(("case", "phase"), None, "slab", None, None),
     )
+    four = mesh.shape["phase"] == 4
     return jax.shard_map(
-        ring_of_four if mesh.shape["phase"] == 4 else shards,
+        ring_of_four if four else shards,
         mesh=mesh,
         in_specs=placed,
         out_specs=P(("case", "phase"), None, "slab", None, None),

time: 95.9 us -> 89.5 us (0.933)
  waiting for transfers between devices: 51.1 us -> 44.1 us
  starting transfers between devices: 12.7 us -> 16.4 us
  local copies, waits for them, and re-layouts: 3.6 us -> 0.01 us
    ppermute x7, waiting for transfers between devices: 30.3 us -> 26 us  [swap_phases(): lax.ppermute(values, 'phase', [(i, i ^ mask) for i in range(lax.axis_size...]
    unnamed x8 -> x2, local copies, waits for them, and re-layouts: 3.6 us -> 0.01 us
    ppermute x6 -> x8, starting transfers between devices: 8.08 us -> 11.3 us  [the longest x4 9.04 us: swap_slabs(): got_b = lax.ppermute(buf_b, 'slab', swaps(count, 1))]
    ppermute x6 -> x8, waiting for transfers between devices: 20.8 us -> 18 us  [the longest x4 11.1 us: swap_slabs(): got_a = lax.ppermute(buf_a, 'slab', swaps(count, 0))]
    pallas_call x10 -> x12, Pallas kernels: 28 us -> 28.5 us  [launch(): pl.pallas_call(body, out_shape=outs, in_specs=[pl.BlockSpec(memory_space=...]
  transfers between devices with their start and end apart: 13 -> 15, of which waited for: 8 -> 9; matrix products, arithmetic and copies ran while one was open for 0% -> 0% of each run, Pallas kernels for 13% -> 17%
where the time goes in v2:
time: 89.5 us; the launch traced here: 89.2 us
  waiting for transfers between devices  44.1 us (49%)
  Pallas kernels  28.5 us (32%)
  starting transfers between devices  16.4 us (18%)
    pallas_call x12, Pallas kernels, launch(): pl.pallas_call(body, out_shape=outs, in_specs=[pl.BlockSpec(memory_space=...  28.5 us
    ppermute x7, waiting for transfers between devices, swap_phases(): lax.ppermute(values, 'phase', [(i, i ^ mask) for i in range(lax.axis_size...  26 us
    ppermute x4, waiting for transfers between devices, swap_slabs(): got_a = lax.ppermute(buf_a, 'slab', swaps(count, 0))  11.1 us
    ppermute x4, starting transfers between devices, swap_slabs(): got_b = lax.ppermute(buf_b, 'slab', swaps(count, 1))  9.04 us
    ppermute x4, waiting for transfers between devices, swap_slabs(): got_b = lax.ppermute(buf_b, 'slab', swaps(count, 1))  6.99 us
    ppermute x7, starting transfers between devices, swap_phases(): lax.ppermute(values, 'phase', [(i, i ^ mask) for i in range(lax.axis_size...  5.09 us
    ppermute x4, starting transfers between devices, swap_slabs(): got_a = lax.ppermute(buf_a, 'slab', swaps(count, 0))  2.28 us
  transfers between devices with their start and end apart: 15, of which 9 were waited for; matrix products, arithmetic and copies ran while one was open for 0% of the time, Pallas kernels for 17%

profile of v2, /device:TPU:16, one launch (start us, length us, event | category | flops | bytes accessed | tf_op | source)
XLA Modules:
  0.0 89.2 jit_solution(3685302372305625202)
XLA Ops:
  0.0 1.3 %shard_map.37 = f32[864,256]{1,0:T(8,128)S(1)} custom-call(f32[3,8,64,256]{3,2,1,0:T(8,128)} %bitcast.5), custom_call_target="tpu_custom_call" | custom-call | bytes 3300000 | tf_op jit(solution)/shard_map/pallas_call | solution.py:18
  1.3 1.6 %collective-permute-start = (f32[864,256]{1,0:T(8,128)S(1)}, f32[864,256]{1,0:T(8,128)S(1)}, u32[]{:S(2)}, u32[]{:S(2)}) collective-permute-start(f32[864,256]{1,0:T(8,128)S(1)} %shard_map.37), channel_id=1, source_target_pairs={{0,8},{4,12},{8,0},{12,4},{1,9},{5,13},{9,1},{13,5},{2,10},{6,14},... | collective-permute-start | bytes 2654216 | tf_op jit(solution)/shard_map/ppermute | solution.py:472
  2.8 0.0 copy-start
  2.8 4.2 %shard_map.38 = (f32[8,64,256]{2,1,0:T(8,128)S(1)}, f32[2,64,256]{2,1,0:T(8,128)S(1)}, f32[4,64,256]{2,1,0:T(8,128)S(1)}, f32[4,64,256]{2,1,0:T(8,128)S(1)}) custom-call(f32[16,128,512]{2,1,0:T(8,128)} %bitcast.8), custom_call_target="tpu_custom_call" | custom-call | bytes 13200000 | tf_op jit(solution)/shard_map/pallas_call | solution.py:18
  7.0 1.6 %collective-permute-start.1 = (f32[4,64,256]{2,1,0:T(8,128)S(1)}, f32[4,64,256]{2,1,0:T(8,128)S(1)}, u32[]{:S(2)}, u32[]{:S(2)}) collective-permute-start(f32[4,64,256]{2,1,0:T(8,128)S(1)} %get-tuple-element.31), channel_id=1, source_target_pairs={{0,1},{1,0},{2,3},{3,2},{4,5},{5,4},{6,7},{7,6},{8,9},{9,8},{10,11... | collective-permute-start | bytes 786440 | tf_op jit(solution)/shard_map/ppermute | solution.py:466
  8.7 1.9 %collective-permute-start.2 = (f32[4,64,256]{2,1,0:T(8,128)S(1)}, f32[4,64,256]{2,1,0:T(8,128)S(1)}, u32[]{:S(2)}, u32[]{:S(2)}) collective-permute-start(f32[4,64,256]{2,1,0:T(8,128)S(1)} %get-tuple-element.32), channel_id=1, source_target_pairs={{1,2},{2,1},{5,6},{6,5},{9,10},{10,9},{13,14},{14,13},{17,18},{18,... | collective-permute-start | bytes 786440 | tf_op jit(solution)/shard_map/ppermute | solution.py:467
  10.6 4.3 %collective-permute-done.1.got_a = f32[4,64,256]{2,1,0:T(8,128)S(1)} collective-permute-done((f32[4,64,256]{2,1,0:T(8,128)S(1)}, f32[4,64,256]{2,1,0:T(8,128)S(1)}, u32[]{:S(2)}, u32[]{:S(2)}) %collective-permute-start.1) | collective-permute-done | bytes 262176 | tf_op jit(solution)/shard_map/ppermute | solution.py:466
  14.8 3.2 %collective-permute-done.2.got_b = f32[4,64,256]{2,1,0:T(8,128)S(1)} collective-permute-done((f32[4,64,256]{2,1,0:T(8,128)S(1)}, f32[4,64,256]{2,1,0:T(8,128)S(1)}, u32[]{:S(2)}, u32[]{:S(2)}) %collective-permute-start.2) | collective-permute-done | bytes 262176 | tf_op jit(solution)/shard_map/ppermute | solution.py:467
  18.0 0.2 shard_map.39
  18.2 0.1 collective-permute-start.3
  18.3 0.0 copy-done
  18.3 8.5 %shard_map.42 = (f32[8,40,256]{2,1,0:T(8,128)S(1)}, f32[288,256]{1,0:T(8,128)S(1)}) custom-call(f32[14,64,256]{2,1,0:T(8,128)S(1)} %get-tuple-element.39.ext, s32[3,8,64,256]{3,2,1,0:T(8,128)S(1)} %bitcast.4), custom_call_target="tpu_custom_call" | custom-call | bytes 28050000 | tf_op jit(solution)/shard_map/pallas_call | solution.py:18
  26.8 0.6 collective-permute-start.8
  27.4 1.3 %collective-permute-start.11 = (f32[14,40,256]{2,1,0:T(8,128)S(1)}, f32[14,40,256]{2,1,0:T(8,128)S(1)}, u32[]{:S(2)}, u32[]{:S(2)}) collective-permute-start(f32[14,40,256]{2,1,0:T(8,128)S(1)} %get-tuple-element.45), channel_id=1, source_target_pairs={{0,4},{4,0},{8,12},{12,8},{1,5},{5,1},{9,13},{13,9},{2,6},{6,2},{1... | collective-permute-start | bytes 1720328 | tf_op jit(solution)/shard_map/ppermute | solution.py:472
  28.7 1.1 %shard_map.41 = (f32[3,2,40,256]{3,2,1,0:T(8,128)S(1)}, f32[3,2,40,256]{3,2,1,0:T(8,128)S(1)}) custom-call(f32[3,8,64,256]{3,2,1,0:T(8,128)} %bitcast.6), custom_call_target="tpu_custom_call" | custom-call | bytes 3300000 | tf_op jit(solution)/shard_map/pallas_call | solution.py:18
  29.8 0.1 collective-permute-start.4
  29.9 0.0 collective-permute-done.3.diag_far
  29.9 2.2 %collective-permute-start.5 = (f32[3,2,40,256]{3,2,1,0:T(8,128)S(1)}, f32[3,2,40,256]{3,2,1,0:T(8,128)S(1)}, u32[]{:S(2)}, u32[]{:S(2)}) collective-permute-start(f32[3,2,40,256]{3,2,1,0:T(8,128)S(1)} %get-tuple-element.36), channel_id=1, source_target_pairs={{1,2},{2,1},{5,6},{6,5},{9,10},{10,9},{13,14},{14,13},{17,18},{18,... | collective-permute-start | bytes 737288 | tf_op jit(solution)/shard_map/ppermute | solution.py:467
  32.1 0.0 collective-permute-done.vel_far
  32.1 0.2 shard_map.40
  32.3 0.5 collective-permute-start.6
  32.8 3.6 %collective-permute-done.8.far = f32[288,256]{1,0:T(8,128)S(1)} collective-permute-done((f32[288,256]{1,0:T(8,128)S(1)}, f32[288,256]{1,0:T(8,128)S(1)}, u32[]{:S(2)}, u32[]{:S(2)}) %collective-permute-start.8) | collective-permute-done | bytes 294944 | tf_op jit(solution)/shard_map/ppermute | solution.py:472
  36.4 2.2 %collective-permute-start.7 = (f32[9,40,256]{2,1,0:T(8,128)S(1)}, f32[9,40,256]{2,1,0:T(8,128)S(1)}, u32[]{:S(2)}, u32[]{:S(2)}) collective-permute-start(f32[9,40,256]{2,1,0:T(8,128)S(1)} %get-tuple-element.38), channel_id=1, source_target_pairs={{1,2},{2,1},{5,6},{6,5},{9,10},{10,9},{13,14},{14,13},{17,18},{18,... | collective-permute-start | bytes 1105928 | tf_op jit(solution)/shard_map/ppermute | solution.py:467
  38.6 0.1 shard_map.43
  38.7 0.0 collective-permute-done.4.own_a
  38.7 0.0 collective-permute-start.9
  38.7 0.9 %collective-permute-done.5.own_b = f32[3,2,40,256]{3,2,1,0:T(8,128)S(1)} collective-permute-done((f32[3,2,40,256]{3,2,1,0:T(8,128)S(1)}, f32[3,2,40,256]{3,2,1,0:T(8,128)S(1)}, u32[]{:S(2)}, u32[]{:S(2)}) %collective-permute-start.5) | collective-permute-done | bytes 245792 | tf_op jit(solution)/shard_map/ppermute | solution.py:467
  39.7 2.7 %collective-permute-start.10 = (f32[2,2,40,256]{3,2,1,0:T(8,128)S(1)}, f32[2,2,40,256]{3,2,1,0:T(8,128)S(1)}, u32[]{:S(2)}, u32[]{:S(2)}) collective-permute-start(f32[2,2,40,256]{3,2,1,0:T(8,128)S(1)} %get-tuple-element.44), channel_id=1, source_target_pairs={{1,2},{2,1},{5,6},{6,5},{9,10},{10,9},{13,14},{14,13},{17,18},{18,... | collective-permute-start | bytes 491528 | tf_op jit(solution)/shard_map/ppermute | solution.py:467
  42.4 6.7 %collective-permute-done.9.warp_a = f32[2,2,40,256]{3,2,1,0:T(8,128)S(1)} collective-permute-done((f32[2,2,40,256]{3,2,1,0:T(8,128)S(1)}, f32[2,2,40,256]{3,2,1,0:T(8,128)S(1)}, u32[]{:S(2)}, u32[]{:S(2)}) %collective-permute-start.9) | collective-permute-done | bytes 163872 | tf_op jit(solution)/shard_map/ppermute | solution.py:466
  49.1 2.9 %collective-permute-done.10.warp_b = f32[2,2,40,256]{3,2,1,0:T(8,128)S(1)} collective-permute-done((f32[2,2,40,256]{3,2,1,0:T(8,128)S(1)}, f32[2,2,40,256]{3,2,1,0:T(8,128)S(1)}, u32[]{:S(2)}, u32[]{:S(2)}) %collective-permute-start.10) | collective-permute-done | bytes 163872 | tf_op jit(solution)/shard_map/ppermute | solution.py:467
  52.0 0.0 collective-permute-done.11.chip
  52.0 0.0 collective-permute-done.6.rim_a
  52.1 0.0 collective-permute-done.7.rim_b
  52.1 6.8 %shard_map.44 = (f32[2,3,10,40,256]{4,3,2,1,0:T(8,128)S(1)}, f32[3,10,40,256]{3,2,1,0:T(8,128)S(1)}, f32[2,12,40,256]{3,2,1,0:T(8,128)S(1)}, f32[2,14,40,256]{3,2,1,0:T(8,128)S(1)}) custom-call(f32[3,8,64,256]{3,2,1,0:T(8,128)} %bitcast.7, f32[3,8,40,256]{3,2,1,0:T(8,128)S(1)} %get-tuple-element.34.vel_other, ...), custom_call_target="tpu_custom_call" | custom-call | bytes 16500000 | tf_op jit(solution)/shard_map/pallas_call | solution.py:18
  58.8 0.1 collective-permute-start.12
  58.9 2.9 %collective-permute-done.12.beside = f32[3,10,40,256]{3,2,1,0:T(8,128)S(1)} collective-permute-done((f32[3,10,40,256]{3,2,1,0:T(8,128)S(1)}, f32[3,10,40,256]{3,2,1,0:T(8,128)S(1)}, u32[]{:S(2)}, u32[]{:S(2)}) %collective-permute-start.12) | collective-permute-done | bytes 1228832 | tf_op jit(solution)/shard_map/ppermute | solution.py:472
  61.8 4.4 %shard_map.45 = (f32[2,3,8,32,256]{4,3,2,1,0:T(8,128)S(1)}, f32[3,8,32,256]{3,2,1,0:T(8,128)S(1)}) custom-call(f32[2,3,10,40,256]{4,3,2,1,0:T(8,128)S(1)} %get-tuple-element.47.vel, f32[3,10,40,256]{3,2,1,0:T(8,128)S(1)} %collective-permute-done.12.beside, f32[2,12,40,256]{3,2,1,0:T(8,128)S(1)} %get-tuple-element.49.warps, ...), custom_call_target="tpu_custom_call" | custom-call | bytes 13200000 | tf_op jit(solution)/shard_map/pallas_call | solution.py:18
  66.2 0.2 collective-permute-start.13
  66.4 2.1 %collective-permute-done.13.beside = f32[3,8,32,256]{3,2,1,0:T(8,128)S(1)} collective-permute-done((f32[3,8,32,256]{3,2,1,0:T(8,128)S(1)}, f32[3,8,32,256]{3,2,1,0:T(8,128)S(1)}, u32[]{:S(2)}, u32[]{:S(2)}) %collective-permute-start.13) | collective-permute-done | bytes 786464 | tf_op jit(solution)/shard_map/ppermute | solution.py:472
  68.6 0.1 shard_map.47
  68.6 1.3 %collective-permute-start.14 = (f32[3,8,32,256]{3,2,1,0:T(8,128)S(1)}, f32[3,8,32,256]{3,2,1,0:T(8,128)S(1)}, u32[]{:S(2)}, u32[]{:S(2)}) collective-permute-start(f32[3,8,32,256]{3,2,1,0:T(8,128)S(1)} %shard_map.47), channel_id=1, source_target_pairs={{0,8},{4,12},{8,0},{12,4},{1,9},{5,13},{9,1},{13,5},{2,10},{6,14},... | collective-permute-start | bytes 2359304 | tf_op jit(solution)/shard_map/ppermute | solution.py:472
  69.9 1.0 %shard_map.46.done = f32[3,8,64,256]{3,2,1,0:T(8,128)} custom-call(f32[2,3,8,32,256]{4,3,2,1,0:T(8,128)S(1)} %get-tuple-element.51.vel, f32[3,8,32,256]{3,2,1,0:T(8,128)S(1)} %collective-permute-done.13.beside), custom_call_target="tpu_custom_call" | custom-call | bytes 3300000 | tf_op jit(solution)/shard_map/pallas_call | solution.py:18
  70.9 17.4 %collective-permute-done.14.home = f32[3,8,32,256]{3,2,1,0:T(8,128)S(1)} collective-permute-done((f32[3,8,32,256]{3,2,1,0:T(8,128)S(1)}, f32[3,8,32,256]{3,2,1,0:T(8,128)S(1)}, u32[]{:S(2)}, u32[]{:S(2)}) %collective-permute-start.14) | collective-permute-done | bytes 786464 | tf_op jit(solution)/shard_map/ppermute | solution.py:472
  88.3 0.9 shard_map.48
Async XLA Ops:
  1.3 30.8 %collective-permute-start = (f32[864,256]{1,0:T(8,128)S(1)}, f32[864,256]{1,0:T(8,128)S(1)}, u32[]{:S(2)}, u32[]{:S(2)}) collective-permute-start(f32[864,256]{1,0:T(8,128)S(1)} %shard_map.37), channel_id=1, source_target_pairs={{0,8},{4,12},{8,0},{12,4},{1,9},{5,13},{9,1},{13,5},{2,10},{6,14},... | collective-permute-start | bytes 2654216 | tf_op jit(solution)/shard_map/ppermute | solution.py:472
  2.8 15.4 %copy-start = (s32[1,3,8,64,256]{4,3,2,1,0:T(8,128)S(1)}, s32[1,3,8,64,256]{4,3,2,1,0:T(8,128)}, u32[]{:S(2)}) copy-start(s32[1,3,8,64,256]{4,3,2,1,0:T(8,128)} %param.4) | copy-start | bytes 4718596
  7.0 7.8 %collective-permute-start.1 = (f32[4,64,256]{2,1,0:T(8,128)S(1)}, f32[4,64,256]{2,1,0:T(8,128)S(1)}, u32[]{:S(2)}, u32[]{:S(2)}) collective-permute-start(f32[4,64,256]{2,1,0:T(8,128)S(1)} %get-tuple-element.31), channel_id=1, source_target_pairs={{0,1},{1,0},{2,3},{3,2},{4,5},{5,4},{6,7},{7,6},{8,9},{9,8},{10,11... | collective-permute-start | bytes 786440 | tf_op jit(solution)/shard_map/ppermute | solution.py:466
  8.7 9.4 %collective-permute-start.2 = (f32[4,64,256]{2,1,0:T(8,128)S(1)}, f32[4,64,256]{2,1,0:T(8,128)S(1)}, u32[]{:S(2)}, u32[]{:S(2)}) collective-permute-start(f32[4,64,256]{2,1,0:T(8,128)S(1)} %get-tuple-element.32), channel_id=1, source_target_pairs={{1,2},{2,1},{5,6},{6,5},{9,10},{10,9},{13,14},{14,13},{17,18},{18,... | collective-permute-start | bytes 786440 | tf_op jit(solution)/shard_map/ppermute | solution.py:467
  18.2 11.7 %collective-permute-start.3 = (f32[288,256]{1,0:T(8,128)S(1)}, f32[288,256]{1,0:T(8,128)S(1)}, u32[]{:S(2)}, u32[]{:S(2)}) collective-permute-start(f32[288,256]{1,0:T(8,128)S(1)} %get-tuple-element.33), channel_id=1, source_target_pairs={{0,12},{4,8},{8,4},{12,0},{1,13},{5,9},{9,5},{13,1},{2,14},{6,10},... | collective-permute-start | bytes 884744 | tf_op jit(solution)/shard_map/ppermute | solution.py:472
  26.8 9.6 %collective-permute-start.8 = (f32[288,256]{1,0:T(8,128)S(1)}, f32[288,256]{1,0:T(8,128)S(1)}, u32[]{:S(2)}, u32[]{:S(2)}) collective-permute-start(f32[288,256]{1,0:T(8,128)S(1)} %get-tuple-element.41), channel_id=1, source_target_pairs={{0,8},{4,12},{8,0},{12,4},{1,9},{5,13},{9,1},{13,5},{2,10},{6,14},... | collective-permute-start | bytes 884744 | tf_op jit(solution)/shard_map/ppermute | solution.py:472
  27.4 24.7 %collective-permute-start.11 = (f32[14,40,256]{2,1,0:T(8,128)S(1)}, f32[14,40,256]{2,1,0:T(8,128)S(1)}, u32[]{:S(2)}, u32[]{:S(2)}) collective-permute-start(f32[14,40,256]{2,1,0:T(8,128)S(1)} %get-tuple-element.45), channel_id=1, source_target_pairs={{0,4},{4,0},{8,12},{12,8},{1,5},{5,1},{9,13},{13,9},{2,6},{6,2},{1... | collective-permute-start | bytes 1720328 | tf_op jit(solution)/shard_map/ppermute | solution.py:472
  29.8 8.9 %collective-permute-start.4 = (f32[3,2,40,256]{3,2,1,0:T(8,128)S(1)}, f32[3,2,40,256]{3,2,1,0:T(8,128)S(1)}, u32[]{:S(2)}, u32[]{:S(2)}) collective-permute-start(f32[3,2,40,256]{3,2,1,0:T(8,128)S(1)} %get-tuple-element.35), channel_id=1, source_target_pairs={{0,1},{1,0},{2,3},{3,2},{4,5},{5,4},{6,7},{7,6},{8,9},{9,8},{10,11... | collective-permute-start | bytes 737288 | tf_op jit(solution)/shard_map/ppermute | solution.py:466
  29.9 9.8 %collective-permute-start.5 = (f32[3,2,40,256]{3,2,1,0:T(8,128)S(1)}, f32[3,2,40,256]{3,2,1,0:T(8,128)S(1)}, u32[]{:S(2)}, u32[]{:S(2)}) collective-permute-start(f32[3,2,40,256]{3,2,1,0:T(8,128)S(1)} %get-tuple-element.36), channel_id=1, source_target_pairs={{1,2},{2,1},{5,6},{6,5},{9,10},{10,9},{13,14},{14,13},{17,18},{18,... | collective-permute-start | bytes 737288 | tf_op jit(solution)/shard_map/ppermute | solution.py:467
  32.3 19.8 %collective-permute-start.6 = (f32[9,40,256]{2,1,0:T(8,128)S(1)}, f32[9,40,256]{2,1,0:T(8,128)S(1)}, u32[]{:S(2)}, u32[]{:S(2)}) collective-permute-start(f32[9,40,256]{2,1,0:T(8,128)S(1)} %get-tuple-element.37), channel_id=1, source_target_pairs={{0,1},{1,0},{2,3},{3,2},{4,5},{5,4},{6,7},{7,6},{8,9},{9,8},{10,11... | collective-permute-start | bytes 1105928 | tf_op jit(solution)/shard_map/ppermute | solution.py:466
  36.4 15.7 %collective-permute-start.7 = (f32[9,40,256]{2,1,0:T(8,128)S(1)}, f32[9,40,256]{2,1,0:T(8,128)S(1)}, u32[]{:S(2)}, u32[]{:S(2)}) collective-permute-start(f32[9,40,256]{2,1,0:T(8,128)S(1)} %get-tuple-element.38), channel_id=1, source_target_pairs={{1,2},{2,1},{5,6},{6,5},{9,10},{10,9},{13,14},{14,13},{17,18},{18,... | collective-permute-start | bytes 1105928 | tf_op jit(solution)/shard_map/ppermute | solution.py:467
  38.7 10.4 %collective-permute-start.9 = (f32[2,2,40,256]{3,2,1,0:T(8,128)S(1)}, f32[2,2,40,256]{3,2,1,0:T(8,128)S(1)}, u32[]{:S(2)}, u32[]{:S(2)}) collective-permute-start(f32[2,2,40,256]{3,2,1,0:T(8,128)S(1)} %get-tuple-element.43), channel_id=1, source_target_pairs={{0,1},{1,0},{2,3},{3,2},{4,5},{5,4},{6,7},{7,6},{8,9},{9,8},{10,11... | collective-permute-start | bytes 491528 | tf_op jit(solution)/shard_map/ppermute | solution.py:466
  39.7 12.4 %collective-permute-start.10 = (f32[2,2,40,256]{3,2,1,0:T(8,128)S(1)}, f32[2,2,40,256]{3,2,1,0:T(8,128)S(1)}, u32[]{:S(2)}, u32[]{:S(2)}) collective-permute-start(f32[2,2,40,256]{3,2,1,0:T(8,128)S(1)} %get-tuple-element.44), channel_id=1, source_target_pairs={{1,2},{2,1},{5,6},{6,5},{9,10},{10,9},{13,14},{14,13},{17,18},{18,... | collective-permute-start | bytes 491528 | tf_op jit(solution)/shard_map/ppermute | solution.py:467
  58.8 3.0 %collective-permute-start.12 = (f32[3,10,40,256]{3,2,1,0:T(8,128)S(1)}, f32[3,10,40,256]{3,2,1,0:T(8,128)S(1)}, u32[]{:S(2)}, u32[]{:S(2)}) collective-permute-start(f32[3,10,40,256]{3,2,1,0:T(8,128)S(1)} %get-tuple-element.48), channel_id=1, source_target_pairs={{0,4},{4,0},{8,12},{12,8},{1,5},{5,1},{9,13},{13,9},{2,6},{6,2},{1... | collective-permute-start | bytes 3686408 | tf_op jit(solution)/shard_map/ppermute | solution.py:472
  66.2 2.4 %collective-permute-start.13 = (f32[3,8,32,256]{3,2,1,0:T(8,128)S(1)}, f32[3,8,32,256]{3,2,1,0:T(8,128)S(1)}, u32[]{:S(2)}, u32[]{:S(2)}) collective-permute-start(f32[3,8,32,256]{3,2,1,0:T(8,128)S(1)} %get-tuple-element.52), channel_id=1, source_target_pairs={{0,4},{4,0},{8,12},{12,8},{1,5},{5,1},{9,13},{13,9},{2,6},{6,2},{1... | collective-permute-start | bytes 2359304 | tf_op jit(solution)/shard_map/ppermute | solution.py:472
  68.6 19.6 %collective-permute-start.14 = (f32[3,8,32,256]{3,2,1,0:T(8,128)S(1)}, f32[3,8,32,256]{3,2,1,0:T(8,128)S(1)}, u32[]{:S(2)}, u32[]{:S(2)}) collective-permute-start(f32[3,8,32,256]{3,2,1,0:T(8,128)S(1)} %shard_map.47), channel_id=1, source_target_pairs={{0,8},{4,12},{8,0},{12,4},{1,9},{5,13},{9,1},{13,5},{2,10},{6,14},... | collective-permute-start | bytes 2359304 | tf_op jit(solution)/shard_map/ppermute | solution.py:472

commit v3 on v2

--- a/solution.py
+++ b/solution.py
@@ -171,9 +171,9 @@
     there = (1 - x) * step
 
     def layer(i, start, size):
-        return ext[i + 3, pl.ds(pl.multiple_of(there + start, 8), size), :]
-
-    pack(far, layer, n, 1 - x, ext.shape[1] // 2)
+        return ext[i + 2, pl.ds(pl.multiple_of(there + start, 8), size), :]
+
+    pack(far, layer, n + 2, 1 - x, ext.shape[1] // 2)
 
 
 def warp_kernel(ext, offs, near, far, wide, full):
@@ -278,14 +278,14 @@
         diag[i, pl.ds(start, size), :] = v
 
     unpack(vel_far, store_vel, 3 * n, x, half)
-    unpack(diag_far, store_diag, n, x, half)
+    unpack(diag_far, store_diag, n + 2, x, half)
     for comp in range(3):
         for i in range(2):
             below, above = vel_other[comp, i], vel_other[comp, n - 2 + i]
             buf_a[2 * comp + i] = jnp.where(parity == 0, above, below)
             buf_b[2 * comp + i] = jnp.where(parity == 0, below, above)
-    for i in range(3):
-        below, above = diag[i], diag[n - 3 + i]
+    for i in range(2):
+        below, above = diag[2 + i], diag[n - 2 + i]
         buf_a[6 + i] = jnp.where(parity == 0, above, below)
         buf_b[6 + i] = jnp.where(parity == 0, below, above)
 
@@ -319,7 +319,8 @@
     mismatch = warped + velocity[0] * gz + velocity[1] * gy + velocity[2] * gx - here
     denominator = (gz * gz + gy * gy + gx * gx) + mismatch * mismatch + 1.0
     ratio = mismatch / denominator
-    return [jnp.where(valid, v - ratio * g, 0.0) for v, g in zip(velocity, (gz, gy, gx))]
+    after = [v - ratio * g for v, g in zip(velocity, (gz, gy, gx))]
+    return after if valid is None else [jnp.where(valid, v, 0.0) for v in after]
 
 
 def smooth_plane(v):
@@ -327,131 +328,227 @@
     return (shift_lanes(v, -1) + 2.0 * v + shift_lanes(v, 1)) * 0.25
 
 
-def first_kernel(
-    vel, vel_other, own_a, own_b, rim_a, rim_b, warp, warp_other, warp_a, warp_b, chip, diag,
-    out, out_sum, warps, targets, held, moved, stage, sem,
+def blur(parts, rows=None):
+    low, here, high = parts
+    v = smooth_plane((low + 2.0 * here + high) * 0.25)
+    if rows is None:
+        return v
+    x, half = rows
+    return jnp.where(x == 0, v[:half], v[v.shape[0] - half :])
+
+
+def first_mid_kernel(
+    vel, vel_other, warp, warp_other, chip, diag, moved, out, out_sum, targets
 ):
     x, core = chip_and_core()
-    parity, has_below, has_above = slab_place()
     n, span = vel_other.shape[1], vel_other.shape[2]
     start = pl.multiple_of(x * (vel.shape[2] - span), 8)
-    copy = pltpu.make_async_copy(vel.at[:, :, pl.ds(start, span), :], stage, sem)
-    copy.start()
-    for i in range(n + 6):
-        a = chip[i]
-        if i < 3:
-            b = pick(parity, rim_a[6 + i], rim_b[6 + i], False)
-        elif i < n + 3:
-            b = diag[i - 3]
-        else:
-            b = pick(parity, rim_a[3 + i - n], rim_b[3 + i - n], True)
+    for i in range(n + 2):
+        a, b = chip[i + 2], diag[i]
         targets[0, i] = jnp.where(core == 0, a, b)
         targets[1, i] = jnp.where(core == 0, b, a)
+
+    def step(i, carry):
+        for m in range(2):
+            if m == 0:
+                v = [vel[comp, i, pl.ds(start, span), :] for comp in range(3)]
+            else:
+                v = [vel_other[comp, i] for comp in range(3)]
+            base = warp[i] if m == 0 else warp_other[i]
+            v = update(v, base, targets[m, i], targets[m, i + 1], targets[m, i + 2], None)
+            for comp in range(3):
+                moved[m, comp, i] = v[comp]
+        return carry
+
+    lax.fori_loop(0, n, step, 0)
+
+    def smooth(i, carry):
+        for comp in range(3):
+            both = [blur([moved[m, comp, i + k] for k in range(3)]) for m in range(2)]
+            for m in range(2):
+                out[m, comp, i] = both[m]
+            out_sum[comp, i] = both[0] + both[1]
+        return carry
+
+    lax.fori_loop(0, n - 2, smooth, 0)
+
+
+def first_rim_kernel(
+    own_a, own_b, rim_a, rim_b, warp_a, warp_b, chip, diag, mid,
+    out, out_sum, targets, held, base, moved,
+):
+    _, core = chip_and_core()
+    parity, has_below, has_above = slab_place()
+    n = mid.shape[2]
+    for k in range(5):
+        low = pick(parity, rim_a[6 + k], rim_b[6 + k], False) if k < 2 else diag[k - 2]
+        high = pick(parity, rim_a[3 + k], rim_b[3 + k], True) if k > 2 else diag[n - 1 + k]
+        for side, b in enumerate((low, high)):
+            a = chip[(n + 1) * side + k]
+            targets[side, 0, k] = jnp.where(core == 0, a, b)
+            targets[side, 1, k] = jnp.where(core == 0, b, a)
     for m in range(2):
-        ref = warp if m == 0 else warp_other
-        for i in range(2):
-            warps[m, i] = pick(parity, warp_a[m, i], warp_b[m, i], False)
-            warps[m, n + 2 + i] = pick(parity, warp_a[m, i], warp_b[m, i], True)
-        for i in range(n):
-            warps[m, i + 2] = ref[i]
-    copy.wait()
-    for m in range(2):
-        ref = stage if m == 0 else vel_other
-        for comp in range(3):
-            for i in range(2):
-                a, b = (own_a[comp, i], own_b[comp, i]) if m == 0 else (rim_a[2 * comp + i], rim_b[2 * comp + i])
-                held[m, comp, i] = pick(parity, a, b, False)
-                held[m, comp, n + 2 + i] = pick(parity, a, b, True)
-            for i in range(n):
-                held[m, comp, i + 2] = ref[comp, i]
-    deep = n + 4
+        for side in range(2):
+            for r in range(2):
+                e = 2 * side + r
+                base[m, e] = pick(parity, warp_a[m, r], warp_b[m, r], side == 1)
+                for comp in range(3):
+                    if m == 0:
+                        a, b = own_a[comp, r], own_b[comp, r]
+                    else:
+                        a, b = rim_a[2 * comp + r], rim_b[2 * comp + r]
+                    held[m, comp, e] = pick(parity, a, b, side == 1)
+                    moved[side, m, comp, r + 2 * (1 - side)] = mid[m, comp, (n - 2) * side + r]
 
     def step(j, carry):
-        m, i = j // deep, j % deep
-        valid = (has_below | (i >= 2)) & (has_above | (i < n + 2))
+        m, e = j // 4, j % 4
+        side, r = e // 2, e % 2
+        at = side + r
         v = update(
-            [held[m, comp, i] for comp in range(3)], warps[m, i],
-            targets[m, i], targets[m, i + 1], targets[m, i + 2], valid,
+            [held[m, comp, e] for comp in range(3)], base[m, e],
+            targets[side, m, at], targets[side, m, at + 1], targets[side, m, at + 2],
+            jnp.where(side == 0, has_below, has_above),
         )
         for comp in range(3):
-            moved[m, comp, i] = v[comp]
-        return carry
-
-    lax.fori_loop(0, 2 * deep, step, 0)
-
-    def blur(i, carry):
-        valid = (has_below | (i >= 1)) & (has_above | (i < n + 1))
+            moved[side, m, comp, e] = v[comp]
+        return carry
+
+    lax.fori_loop(0, 8, step, 0)
+
+    def smooth(e, carry):
+        side, r = e // 2, e % 2
+        valid = (side == r) & jnp.where(side == 0, has_below, has_above) | (side != r)
         for comp in range(3):
-            total = None
+            both = [blur([moved[side, m, comp, r + k] for k in range(3)]) for m in range(2)]
             for m in range(2):
-                v = (moved[m, comp, i] + 2.0 * moved[m, comp, i + 1] + moved[m, comp, i + 2]) * 0.25
-                v = jnp.where(valid, smooth_plane(v), 0.0)
-                out[m, comp, i] = v
-                total = v if total is None else total + v
-            out_sum[comp, i] = total
-        return carry
-
-    lax.fori_loop(0, n + 2, blur, 0)
-
-
-def second_kernel(vel, beside, warps, targets, out, out_sum, moved):
-    x, _ = chip_and_core()
-    _, has_below, has_above = slab_place()
-    n, half = out.shape[2], out.shape[3]
-    deep = n + 2
+                both[m] = jnp.where(valid, both[m], 0.0)
+                out[m, comp, e] = both[m]
+            out_sum[comp, e] = both[0] + both[1]
+        return carry
+
+    lax.fori_loop(0, 4, smooth, 0)
+
+
+def second_mid_kernel(vel, beside, warp, warp_other, targets, moved, out, out_sum):
+    x, _ = chip_and_core()
+    inner, half = vel.shape[2], out.shape[3]
+
+    def step(i, carry):
+        for m in range(2):
+            v = [(2.0 * vel[m, comp, i] + beside[comp, i]) * 0.25 for comp in range(3)]
+            base = warp[i + 1] if m == 0 else warp_other[i + 1]
+            v = update(v, base, targets[m, i + 1], targets[m, i + 2], targets[m, i + 3], None)
+            for comp in range(3):
+                moved[m, comp, i] = v[comp]
+        return carry
+
+    lax.fori_loop(0, inner, step, 0)
+
+    def smooth(i, carry):
+        for comp in range(3):
+            both = [blur([moved[m, comp, i + k] for k in range(3)], (x, half)) for m in range(2)]
+            for m in range(2):
+                out[m, comp, i] = both[m]
+            out_sum[comp, i] = both[0] + both[1]
+        return carry
+
+    lax.fori_loop(0, inner - 2, smooth, 0)
+
+
+def second_rim_kernel(
+    vel, beside, warp, warp_other, warp_a, warp_b, mid, targets, out, out_sum, base, moved
+):
+    x, _ = chip_and_core()
+    parity, has_below, has_above = slab_place()
+    inner, half = mid.shape[2], out.shape[3]
+    n = inner + 2
+    for m in range(2):
+        own = warp if m == 0 else warp_other
+        base[m, 0] = pick(parity, warp_a[m, 1], warp_b[m, 1], False)
+        base[m, 1] = own[0]
+        base[m, 2] = own[n - 1]
+        base[m, 3] = pick(parity, warp_a[m, 0], warp_b[m, 0], True)
+        for comp in range(3):
+            for r in range(2):
+                moved[0, m, comp, 2 + r] = mid[m, comp, r]
+                moved[1, m, comp, r] = mid[m, comp, inner - 2 + r]
 
     def step(j, carry):
-        m, i = j // deep, j % deep
-        valid = (has_below | (i >= 1)) & (has_above | (i < n + 1))
+        m, e = j // 4, j % 4
+        side, r = e // 2, e % 2
+        at = 1 - side + r
+        valid = (side == r) & jnp.where(side == 0, has_below, has_above) | (side != r)
         v = update(
-            [(2.0 * vel[m, comp, i] + beside[comp, i]) * 0.25 for comp in range(3)], warps[m, i + 1],
-            targets[m, i + 1], targets[m, i + 2], targets[m, i + 3], valid,
+            [(2.0 * vel[m, comp, e] + beside[comp, e]) * 0.25 for comp in range(3)], base[m, e],
+            targets[side, m, at], targets[side, m, at + 1], targets[side, m, at + 2], valid,
         )
         for comp in range(3):
-            moved[m, comp, i] = v[comp]
-        return carry
-
-    lax.fori_loop(0, 2 * deep, step, 0)
-
-    def blur(i, carry):
+            moved[side, m, comp, e] = v[comp]
+        return carry
+
+    lax.fori_loop(0, 8, step, 0)
+
+    def smooth(e, carry):
+        side, r = e // 2, e % 2
         for comp in range(3):
-            total = None
+            both = [
+                blur([moved[side, m, comp, r + k] for k in range(3)], (x, half)) for m in range(2)
+            ]
             for m in range(2):
-                v = (moved[m, comp, i] + 2.0 * moved[m, comp, i + 1] + moved[m, comp, i + 2]) * 0.25
-                v = smooth_plane(v)
-                v = jnp.where(x == 0, v[:half], v[v.shape[0] - half :])
-                out[m, comp, i] = v
-                total = v if total is None else total + v
-            out_sum[comp, i] = total
-        return carry
-
-    lax.fori_loop(0, n, blur, 0)
+                out[m, comp, e] = both[m]
+            out_sum[comp, e] = both[0] + both[1]
+        return carry
+
+    lax.fori_loop(0, 4, smooth, 0)
 
 
 def send_kernel(vel, beside, out):
     out[...] = (2.0 * vel[1] + beside[...]) * 0.25
 
 
-def close_own_kernel(vel, beside, out, stage, sem):
-    x, _ = chip_and_core()
-    half = stage.shape[2]
-    stage[...] = (2.0 * vel[0] + beside[...]) * 0.25
-    here = pltpu.make_async_copy(
-        stage, out.at[:, :, pl.ds(pl.multiple_of(x * half, 8), half), :], sem
-    )
-    here.start()
-    here.wait()
-
-
-def close_far_kernel(done, home, out, sem):
+def close_own_kernel(mid, mid_beside, rim, rim_beside, out, stage_mid, stage_rim, sem):
+    x, _ = chip_and_core()
+    half = stage_mid.shape[2]
+    rows = pl.ds(pl.multiple_of(x * half, 8), half)
+    n = out.shape[1]
+    stage_mid[...] = (2.0 * mid[0] + mid_beside[...]) * 0.25
+    stage_rim[...] = (2.0 * rim[0] + rim_beside[...]) * 0.25
+    copies = [
+        pltpu.make_async_copy(stage_mid, out.at[:, pl.ds(2, n - 4), rows, :], sem.at[0]),
+        pltpu.make_async_copy(stage_rim.at[:, pl.ds(0, 2)], out.at[:, pl.ds(0, 2), rows, :], sem.at[1]),
+        pltpu.make_async_copy(stage_rim.at[:, pl.ds(2, 2)], out.at[:, pl.ds(n - 2, 2), rows, :], sem.at[2]),
+    ]
+    for copy in copies:
+        copy.start()
+    for copy in copies:
+        copy.wait()
+
+
+def close_mid_kernel(done, home, out, sem):
     del done
     x, _ = chip_and_core()
     half = home.shape[2]
-    there = pltpu.make_async_copy(
-        home, out.at[:, :, pl.ds(pl.multiple_of((1 - x) * half, 8), half), :], sem
-    )
-    there.start()
-    there.wait()
+    rows = pl.ds(pl.multiple_of((1 - x) * half, 8), half)
+    copy = pltpu.make_async_copy(home, out.at[:, pl.ds(2, out.shape[1] - 4), rows, :], sem)
+    copy.start()
+    copy.wait()
+
+
+def close_rim_kernel(done, home, out, sem):
+    del done
+    x, _ = chip_and_core()
+    half = home.shape[2]
+    rows = pl.ds(pl.multiple_of((1 - x) * half, 8), half)
+    copies = [
+        pltpu.make_async_copy(
+            home.at[:, pl.ds(2 * k, 2)], out.at[:, pl.ds(z, 2), rows, :], sem.at[k]
+        )
+        for k, z in enumerate((0, out.shape[1] - 2))
+    ]
+    for copy in copies:
+        copy.start()
+    for copy in copies:
+        copy.wait()
 
 
 def swaps(count, first):
@@ -520,7 +617,7 @@
     own_a, own_b = swap_slabs(buf_a, buf_b)
     ext, near, far = launch(
         join_kernel,
-        [shape(n + 6, rows, cols), shape(n + 6, span, cols), shape(n * (half + 4), cols)],
+        [shape(n + 6, rows, cols), shape(n + 6, span, cols), shape((n + 2) * (half + 4), cols)],
         [part, edge, got_a, got_b],
     )
     chip = swap_phases(near, 1)
@@ -540,7 +637,7 @@
 
     buf_a, buf_b, vel_other, diag = launch(
         rim_other_kernel,
-        [shape(9, span, cols)] * 2 + [shape(3, n, span, cols), shape(n, span, cols)],
+        [shape(8, span, cols)] * 2 + [shape(3, n, span, cols), shape(n + 2, span, cols)],
         [vel_far, diag_far],
     )
     rim_a, rim_b = swap_slabs(buf_a, buf_b)
@@ -551,51 +648,77 @@
     )
     warp_a, warp_b = swap_slabs(buf_a, buf_b)
 
-    state, own_sum, warps, targets = launch(
-        first_kernel,
+    moved, mid, mid_sum, targets = launch(
+        first_mid_kernel,
         [
-            shape(2, 3, n + 2, span, cols),
-            shape(3, n + 2, span, cols),
-            shape(2, n + 4, span, cols),
-            shape(2, n + 6, span, cols),
+            shape(2, 3, n, span, cols),
+            shape(2, 3, n - 2, span, cols),
+            shape(3, n - 2, span, cols),
+            shape(2, n + 2, span, cols),
         ],
-        [vel, vel_other, own_a, own_b, rim_a, rim_b, warp, warp_other, warp_a, warp_b, chip, diag],
+        [vel, vel_other, warp, warp_other, chip, diag],
+        micros=3.3,
+    )
+    mid_beside = swap_phases(mid_sum, 1)
+    rim, rim_sum, ends = launch(
+        first_rim_kernel,
+        [shape(2, 3, 4, span, cols), shape(3, 4, span, cols), shape(2, 2, 5, span, cols)],
+        [own_a, own_b, rim_a, rim_b, warp_a, warp_b, chip, diag, moved],
         [
-            pltpu.VMEM((2, 3, n + 4, span, cols), F32),
-            pltpu.VMEM((2, 3, n + 4, span, cols), F32),
-            pltpu.VMEM((3, n, span, cols), F32),
-            dma,
+            pltpu.VMEM((2, 3, 4, span, cols), F32),
+            pltpu.VMEM((2, 4, span, cols), F32),
+            pltpu.VMEM((2, 2, 3, 4, span, cols), F32),
         ],
-        hbm=(0,),
-        micros=5.0,
-    )
-    beside = swap_phases(own_sum, 1)
-    state, own_sum = launch(
-        second_kernel,
-        [shape(2, 3, n, half, cols), shape(3, n, half, cols)],
-        [state, beside, warps, targets],
-        [pltpu.VMEM((2, 3, n + 2, span, cols), F32)],
-        micros=4.0,
-    )
-    beside = swap_phases(own_sum, 1)
-    (away,) = launch(send_kernel, [shape(3, n, half, cols)], [state, beside])
-    home = swap_phases(away, 2)
+        micros=2.0,
+    )
+    rim_beside = swap_phases(rim_sum, 1)
+    moved, mid, mid_sum = launch(
+        second_mid_kernel,
+        [
+            shape(2, 3, n - 2, span, cols),
+            shape(2, 3, n - 4, half, cols),
+            shape(3, n - 4, half, cols),
+        ],
+        [mid, mid_beside, warp, warp_other, targets],
+        micros=2.5,
+    )
+    mid_beside = swap_phases(mid_sum, 1)
+    rim, rim_sum = launch(
+        second_rim_kernel,
+        [shape(2, 3, 4, half, cols), shape(3, 4, half, cols)],
+        [rim, rim_beside, warp, warp_other, warp_a, warp_b, moved, ends],
+        [
+            pltpu.VMEM((2, 4, span, cols), F32),
+            pltpu.VMEM((2, 2, 3, 4, span, cols), F32),
+        ],
+        micros=2.0,
+    )
+    rim_beside = swap_phases(rim_sum, 1)
+    (away,) = launch(send_kernel, [shape(3, n - 4, half, cols)], [mid, mid_beside])
+    mid_home = swap_phases(away, 2)
+    (away,) = launch(send_kernel, [shape(3, 4, half, cols)], [rim, rim_beside])
+    rim_home = swap_phases(away, 2)
     (velocity,) = launch(
         close_own_kernel,
         [shape(3, n, rows, cols)],
-        [state, beside],
-        [pltpu.VMEM((3, n, half, cols), F32), dma],
+        [mid, mid_beside, rim, rim_beside],
+        [
+            pltpu.VMEM((3, n - 4, half, cols), F32),
+            pltpu.VMEM((3, 4, half, cols), F32),
+            dma((3,)),
+        ],
         hbm_out=(0,),
     )
-    (velocity,) = launch(
-        close_far_kernel,
-        [shape(3, n, rows, cols)],
-        [velocity, home],
-        [dma],
-        hbm=(0,),
-        hbm_out=(0,),
-        alias={0: 0},
-    )
+    for kernel, home, sems in ((close_mid_kernel, mid_home, dma), (close_rim_kernel, rim_home, dma((2,)))):
+        (velocity,) = launch(
+            kernel,
+            [shape(3, n, rows, cols)],
+            [velocity, home],
+            [sems],
+            hbm=(0,),
+            hbm_out=(0,),
+            alias={0: 0},
+        )
     return velocity[None]
 
 

time: 89.5 us -> 79.6 us (0.89)
  the two profiles are of different devices: /device:TPU:16 before, /device:TPU:0 now
where the time goes in v3:
time: 79.6 us; the launch traced here: 78.8 us
  Pallas kernels  26.7 us (34%)
  starting transfers between devices  25.9 us (33%)
  waiting for transfers between devices  25.9 us (33%)
    pallas_call x16, Pallas kernels, launch(): pl.pallas_call(body, out_shape=outs, in_specs=[pl.BlockSpec(memory_space=...  26.7 us
    ppermute x10, waiting for transfers between devices, swap_phases(): lax.ppermute(values, 'phase', [(i, i ^ mask) for i in range(lax.axis_size...  16.3 us
    ppermute x4, starting transfers between devices, swap_slabs(): got_a = lax.ppermute(buf_a, 'slab', swaps(count, 0))  14.1 us
    ppermute x4, waiting for transfers between devices, swap_slabs(): got_a = lax.ppermute(buf_a, 'slab', swaps(count, 0))  9.64 us
    ppermute x10, starting transfers between devices, swap_phases(): lax.ppermute(values, 'phase', [(i, i ^ mask) for i in range(lax.axis_size...  9.2 us
    ppermute x4, starting transfers between devices, swap_slabs(): got_b = lax.ppermute(buf_b, 'slab', swaps(count, 1))  2.66 us
  transfers between devices with their start and end apart: 18, of which 6 were waited for; matrix products, arithmetic and copies ran while one was open for 0% of the time, Pallas kernels for 31%

profile of v3, /device:TPU:0, one launch (start us, length us, event | category | flops | bytes accessed | tf_op | source)
XLA Modules:
  0.0 78.8 jit_solution(11804616189469947705)
XLA Ops:
  0.0 1.3 %shard_map.37 = f32[864,256]{1,0:T(8,128)S(1)} custom-call(f32[3,8,64,256]{3,2,1,0:T(8,128)} %bitcast.4), custom_call_target="tpu_custom_call" | custom-call | bytes 3300000 | tf_op jit(solution)/shard_map/pallas_call | solution.py:18
  1.3 3.0 %collective-permute-start = (f32[864,256]{1,0:T(8,128)S(1)}, f32[864,256]{1,0:T(8,128)S(1)}, u32[]{:S(2)}, u32[]{:S(2)}) collective-permute-start(f32[864,256]{1,0:T(8,128)S(1)} %shard_map.37), channel_id=1, source_target_pairs={{0,8},{4,12},{8,0},{12,4},{1,9},{5,13},{9,1},{13,5},{2,10},{6,14},... | collective-permute-start | bytes 2654216 | tf_op jit(solution)/shard_map/ppermute | solution.py:569
  4.3 0.0 copy-start.1
  4.3 4.2 %shard_map.38 = (f32[8,64,256]{2,1,0:T(8,128)S(1)}, f32[2,64,256]{2,1,0:T(8,128)S(1)}, f32[4,64,256]{2,1,0:T(8,128)S(1)}, f32[4,64,256]{2,1,0:T(8,128)S(1)}) custom-call(f32[16,128,512]{2,1,0:T(8,128)} %bitcast.8), custom_call_target="tpu_custom_call" | custom-call | bytes 13200000 | tf_op jit(solution)/shard_map/pallas_call | solution.py:18
  8.5 1.6 %collective-permute-start.1 = (f32[4,64,256]{2,1,0:T(8,128)S(1)}, f32[4,64,256]{2,1,0:T(8,128)S(1)}, u32[]{:S(2)}, u32[]{:S(2)}) collective-permute-start(f32[4,64,256]{2,1,0:T(8,128)S(1)} %get-tuple-element.37), channel_id=1, source_target_pairs={{0,1},{1,0},{2,3},{3,2},{4,5},{5,4},{6,7},{7,6},{8,9},{9,8},{10,11... | collective-permute-start | bytes 786440 | tf_op jit(solution)/shard_map/ppermute | solution.py:563
  10.1 0.7 collective-permute-start.2
  10.8 5.5 %collective-permute-done.1.got_a = f32[4,64,256]{2,1,0:T(8,128)S(1)} collective-permute-done((f32[4,64,256]{2,1,0:T(8,128)S(1)}, f32[4,64,256]{2,1,0:T(8,128)S(1)}, u32[]{:S(2)}, u32[]{:S(2)}) %collective-permute-start.1) | collective-permute-done | bytes 262176 | tf_op jit(solution)/shard_map/ppermute | solution.py:563
  16.3 0.0 collective-permute-done.2.got_b
  16.3 0.2 shard_map.39
  16.5 0.1 collective-permute-start.5
  16.6 0.5 collective-permute-start.3
  17.0 0.0 copy-done.1
  17.0 8.5 %shard_map.41 = (f32[8,40,256]{2,1,0:T(8,128)S(1)}, f32[288,256]{1,0:T(8,128)S(1)}) custom-call(f32[14,64,256]{2,1,0:T(8,128)S(1)} %get-tuple-element.41.ext, s32[3,8,64,256]{3,2,1,0:T(8,128)S(1)} %bitcast.7), custom_call_target="tpu_custom_call" | custom-call | bytes 28050000 | tf_op jit(solution)/shard_map/pallas_call | solution.py:18
  25.6 0.0 copy-start
  25.6 1.7 %collective-permute-start.4 = (f32[288,256]{1,0:T(8,128)S(1)}, f32[288,256]{1,0:T(8,128)S(1)}, u32[]{:S(2)}, u32[]{:S(2)}) collective-permute-start(f32[288,256]{1,0:T(8,128)S(1)} %get-tuple-element.43), channel_id=1, source_target_pairs={{0,8},{4,12},{8,0},{12,4},{1,9},{5,13},{9,1},{13,5},{2,10},{6,14},... | collective-permute-start | bytes 884744 | tf_op jit(solution)/shard_map/ppermute | solution.py:569
  27.3 1.1 %shard_map.45 = (f32[3,2,40,256]{3,2,1,0:T(8,128)S(1)}, f32[3,2,40,256]{3,2,1,0:T(8,128)S(1)}) custom-call(f32[3,8,64,256]{3,2,1,0:T(8,128)} %bitcast.5), custom_call_target="tpu_custom_call" | custom-call | bytes 3300000 | tf_op jit(solution)/shard_map/pallas_call | solution.py:18
  28.4 4.7 %collective-permute-start.8 = (f32[3,2,40,256]{3,2,1,0:T(8,128)S(1)}, f32[3,2,40,256]{3,2,1,0:T(8,128)S(1)}, u32[]{:S(2)}, u32[]{:S(2)}) collective-permute-start(f32[3,2,40,256]{3,2,1,0:T(8,128)S(1)} %get-tuple-element.52), channel_id=1, source_target_pairs={{0,1},{1,0},{2,3},{3,2},{4,5},{5,4},{6,7},{7,6},{8,9},{9,8},{10,11... | collective-permute-start | bytes 737288 | tf_op jit(solution)/shard_map/ppermute | solution.py:563
  33.1 0.0 collective-permute-done.3.diag_far
  33.1 0.7 collective-permute-start.9
  33.7 0.0 collective-permute-done.vel_far
  33.8 0.2 shard_map.40
  33.9 3.1 %collective-permute-start.10 = (f32[8,40,256]{2,1,0:T(8,128)S(1)}, f32[8,40,256]{2,1,0:T(8,128)S(1)}, u32[]{:S(2)}, u32[]{:S(2)}) collective-permute-start(f32[8,40,256]{2,1,0:T(8,128)S(1)} %get-tuple-element.54), channel_id=1, source_target_pairs={{0,1},{1,0},{2,3},{3,2},{4,5},{5,4},{6,7},{7,6},{8,9},{9,8},{10,11... | collective-permute-start | bytes 983048 | tf_op jit(solution)/shard_map/ppermute | solution.py:563
  37.0 1.2 %collective-permute-done.4.far = f32[288,256]{1,0:T(8,128)S(1)} collective-permute-done((f32[288,256]{1,0:T(8,128)S(1)}, f32[288,256]{1,0:T(8,128)S(1)}, u32[]{:S(2)}, u32[]{:S(2)}) %collective-permute-start.4) | collective-permute-done | bytes 294944 | tf_op jit(solution)/shard_map/ppermute | solution.py:569
  38.2 0.7 collective-permute-start.11
  38.9 0.1 shard_map.42
  38.9 0.0 collective-permute-done.5.chip
  38.9 0.0 copy-done
  38.9 2.6 %shard_map.43 = (f32[2,3,8,40,256]{4,3,2,1,0:T(8,128)S(1)}, f32[2,3,6,40,256]{4,3,2,1,0:T(8,128)S(1)}, f32[3,6,40,256]{3,2,1,0:T(8,128)S(1)}, f32[2,10,40,256]{3,2,1,0:T(8,128)S(1)}) custom-call(f32[3,8,64,256]{3,2,1,0:T(8,128)S(1)} %bitcast.6, f32[3,8,40,256]{3,2,1,0:T(8,128)S(1)} %get-tuple-element.40.vel_other, ...), custom_call_target="tpu_custom_call" | custom-call | bytes 10890000 | tf_op jit(solution)/shard_map/pallas_call | solution.py:18
  41.5 0.1 collective-permute-start.6
  41.6 0.0 collective-permute-done.8.own_a
  41.6 4.7 %collective-permute-start.12 = (f32[2,2,40,256]{3,2,1,0:T(8,128)S(1)}, f32[2,2,40,256]{3,2,1,0:T(8,128)S(1)}, u32[]{:S(2)}, u32[]{:S(2)}) collective-permute-start(f32[2,2,40,256]{3,2,1,0:T(8,128)S(1)} %get-tuple-element.56), channel_id=1, source_target_pairs={{0,1},{1,0},{2,3},{3,2},{4,5},{5,4},{6,7},{7,6},{8,9},{9,8},{10,11... | collective-permute-start | bytes 491528 | tf_op jit(solution)/shard_map/ppermute | solution.py:563
  46.3 0.0 collective-permute-done.9.own_b
  46.3 0.7 collective-permute-start.13
  47.0 4.1 %collective-permute-done.12.warp_a = f32[2,2,40,256]{3,2,1,0:T(8,128)S(1)} collective-permute-done((f32[2,2,40,256]{3,2,1,0:T(8,128)S(1)}, f32[2,2,40,256]{3,2,1,0:T(8,128)S(1)}, u32[]{:S(2)}, u32[]{:S(2)}) %collective-permute-start.12) | collective-permute-done | bytes 163872 | tf_op jit(solution)/shard_map/ppermute | solution.py:563
  51.1 0.0 collective-permute-done.13.warp_b
  51.1 0.0 collective-permute-done.10.rim_a
  51.1 0.0 collective-permute-done.11.rim_b
  51.1 2.2 %shard_map.46 = (f32[2,3,4,40,256]{4,3,2,1,0:T(8,128)S(1)}, f32[3,4,40,256]{3,2,1,0:T(8,128)S(1)}, f32[2,2,5,40,256]{4,3,2,1,0:T(8,128)S(1)}) custom-call(f32[3,2,40,256]{3,2,1,0:T(8,128)S(1)} %collective-permute-done.8.own_a, f32[3,2,40,256]{3,2,1,0:T(8,128)S(1)} %collective-permute-done.9.own_b, f32[8,40,256]{2,1,0:T(8,128)S(1)} %collective-permute-done.10.rim_a, ...), custom_call_target="tpu_custom_call" | custom-call | bytes 6600000 | tf_op jit(solution)/shard_map/pallas_call | solution.py:18
  53.3 0.1 collective-permute-start.14
  53.4 0.0 collective-permute-done.6.beside
  53.4 1.8 %shard_map.44 = (f32[2,3,6,40,256]{4,3,2,1,0:T(8,128)S(1)}, f32[2,3,4,32,256]{4,3,2,1,0:T(8,128)S(1)}, f32[3,4,32,256]{3,2,1,0:T(8,128)S(1)}) custom-call(f32[2,3,6,40,256]{4,3,2,1,0:T(8,128)S(1)} %get-tuple-element.47.vel, f32[3,6,40,256]{3,2,1,0:T(8,128)S(1)} %collective-permute-done.6.beside, f32[8,40,256]{2,1,0:T(8,128)S(1)} %get-tuple-element.42.near.warp, ...), custom_call_target="tpu_custom_call" | custom-call | bytes 8250000 | tf_op jit(solution)/shard_map/pallas_call | solution.py:18
  55.2 0.5 collective-permute-start.7
  55.8 0.0 collective-permute-done.14.beside
  55.8 2.1 %shard_map.47 = (f32[2,3,4,32,256]{4,3,2,1,0:T(8,128)S(1)}, f32[3,4,32,256]{3,2,1,0:T(8,128)S(1)}) custom-call(f32[2,3,4,40,256]{4,3,2,1,0:T(8,128)S(1)} %get-tuple-element.59.vel, f32[3,4,40,256]{3,2,1,0:T(8,128)S(1)} %collective-permute-done.14.beside, f32[8,40,256]{2,1,0:T(8,128)S(1)} %get-tuple-element.42.near.warp, ...), custom_call_target="tpu_custom_call" | custom-call | bytes 6600000 | tf_op jit(solution)/shard_map/pallas_call | solution.py:18
  57.9 0.1 collective-permute-start.15
  58.0 0.0 collective-permute-done.7.mid_beside.beside
  58.0 1.6 %collective-permute-start.16 = (f32[3,4,32,256]{3,2,1,0:T(8,128)S(1)}, f32[3,4,32,256]{3,2,1,0:T(8,128)S(1)}, u32[]{:S(2)}, u32[]{:S(2)}) collective-permute-start(f32[3,4,32,256]{3,2,1,0:T(8,128)S(1)} %shard_map.49), channel_id=1, source_target_pairs={{0,8},{4,12},{8,0},{12,4},{1,9},{5,13},{9,1},{13,5},{2,10},{6,14},... | collective-permute-start | bytes 1179656 | tf_op jit(solution)/shard_map/ppermute | solution.py:569
  59.6 0.1 collective-permute-done.15.rim_beside.beside
  59.7 1.6 %collective-permute-start.17 = (f32[3,4,32,256]{3,2,1,0:T(8,128)S(1)}, f32[3,4,32,256]{3,2,1,0:T(8,128)S(1)}, u32[]{:S(2)}, u32[]{:S(2)}) collective-permute-start(f32[3,4,32,256]{3,2,1,0:T(8,128)S(1)} %shard_map.51), channel_id=1, source_target_pairs={{0,8},{4,12},{8,0},{12,4},{1,9},{5,13},{9,1},{13,5},{2,10},{6,14},... | collective-permute-start | bytes 1179656 | tf_op jit(solution)/shard_map/ppermute | solution.py:569
  61.3 1.0 %shard_map.48.done = f32[3,8,64,256]{3,2,1,0:T(8,128)} custom-call(f32[2,3,4,32,256]{4,3,2,1,0:T(8,128)S(1)} %get-tuple-element.50.mid.vel, f32[3,4,32,256]{3,2,1,0:T(8,128)S(1)} %collective-permute-done.7.mid_beside.beside, f32[2,3,4,32,256]{4,3,2,1,0:T(8,128)S(1)} %get-tuple-element.63.rim.vel, f32[3,4,32,256]{3,2,1,0:T(8,128)S(1)} %collective-permute-done.15.rim_beside.beside), custom_call_target="tpu_custom_call" | custom-call | bytes 3300000 | tf_op jit(solution)/shard_map/pallas_call | solution.py:18
  62.3 7.8 %collective-permute-done.16.home = f32[3,4,32,256]{3,2,1,0:T(8,128)S(1)} collective-permute-done((f32[3,4,32,256]{3,2,1,0:T(8,128)S(1)}, f32[3,4,32,256]{3,2,1,0:T(8,128)S(1)}, u32[]{:S(2)}, u32[]{:S(2)}) %collective-permute-start.16) | collective-permute-done | bytes 393248 | tf_op jit(solution)/shard_map/ppermute | solution.py:569
  70.1 0.8 shard_map.50.done
  70.8 7.2 %collective-permute-done.17.home = f32[3,4,32,256]{3,2,1,0:T(8,128)S(1)} collective-permute-done((f32[3,4,32,256]{3,2,1,0:T(8,128)S(1)}, f32[3,4,32,256]{3,2,1,0:T(8,128)S(1)}, u32[]{:S(2)}, u32[]{:S(2)}) %collective-permute-start.17) | collective-permute-done | bytes 393248 | tf_op jit(solution)/shard_map/ppermute | solution.py:569
  78.0 0.8 shard_map.52
  (2 shorter events, 0.1 us)
Async XLA Ops:
  1.3 32.5 %collective-permute-start = (f32[864,256]{1,0:T(8,128)S(1)}, f32[864,256]{1,0:T(8,128)S(1)}, u32[]{:S(2)}, u32[]{:S(2)}) collective-permute-start(f32[864,256]{1,0:T(8,128)S(1)} %shard_map.37), channel_id=1, source_target_pairs={{0,8},{4,12},{8,0},{12,4},{1,9},{5,13},{9,1},{13,5},{2,10},{6,14},... | collective-permute-start | bytes 2654216 | tf_op jit(solution)/shard_map/ppermute | solution.py:569
  4.3 12.7 %copy-start.1 = (s32[1,3,8,64,256]{4,3,2,1,0:T(8,128)S(1)}, s32[1,3,8,64,256]{4,3,2,1,0:T(8,128)}, u32[]{:S(2)}) copy-start(s32[1,3,8,64,256]{4,3,2,1,0:T(8,128)} %param.4) | copy-start | bytes 4718596
  8.5 7.8 %collective-permute-start.1 = (f32[4,64,256]{2,1,0:T(8,128)S(1)}, f32[4,64,256]{2,1,0:T(8,128)S(1)}, u32[]{:S(2)}, u32[]{:S(2)}) collective-permute-start(f32[4,64,256]{2,1,0:T(8,128)S(1)} %get-tuple-element.37), channel_id=1, source_target_pairs={{0,1},{1,0},{2,3},{3,2},{4,5},{5,4},{6,7},{7,6},{8,9},{9,8},{10,11... | collective-permute-start | bytes 786440 | tf_op jit(solution)/shard_map/ppermute | solution.py:563
  10.1 6.2 %collective-permute-start.2 = (f32[4,64,256]{2,1,0:T(8,128)S(1)}, f32[4,64,256]{2,1,0:T(8,128)S(1)}, u32[]{:S(2)}, u32[]{:S(2)}) collective-permute-start(f32[4,64,256]{2,1,0:T(8,128)S(1)} %get-tuple-element.38), channel_id=1, source_target_pairs={{1,2},{2,1},{5,6},{6,5},{9,10},{10,9},{13,14},{14,13},{17,18},{18,... | collective-permute-start | bytes 786440 | tf_op jit(solution)/shard_map/ppermute | solution.py:564
  16.5 22.4 %collective-permute-start.5 = (f32[14,40,256]{2,1,0:T(8,128)S(1)}, f32[14,40,256]{2,1,0:T(8,128)S(1)}, u32[]{:S(2)}, u32[]{:S(2)}) collective-permute-start(f32[14,40,256]{2,1,0:T(8,128)S(1)} %get-tuple-element.45), channel_id=1, source_target_pairs={{0,4},{4,0},{8,12},{12,8},{1,5},{5,1},{9,13},{13,9},{2,6},{6,2},{1... | collective-permute-start | bytes 1720328 | tf_op jit(solution)/shard_map/ppermute | solution.py:569
  16.6 16.5 %collective-permute-start.3 = (f32[360,256]{1,0:T(8,128)S(1)}, f32[360,256]{1,0:T(8,128)S(1)}, u32[]{:S(2)}, u32[]{:S(2)}) collective-permute-start(f32[360,256]{1,0:T(8,128)S(1)} %get-tuple-element.39), channel_id=1, source_target_pairs={{0,12},{4,8},{8,4},{12,0},{1,13},{5,9},{9,5},{13,1},{2,14},{6,10},... | collective-permute-start | bytes 1105928 | tf_op jit(solution)/shard_map/ppermute | solution.py:569
  25.6 13.4 %copy-start = (f32[1,3,8,64,256]{4,3,2,1,0:T(8,128)S(1)}, f32[1,3,8,64,256]{4,3,2,1,0:T(8,128)}, u32[]{:S(2)}) copy-start(f32[1,3,8,64,256]{4,3,2,1,0:T(8,128)} %param.5) | copy-start | bytes 4718596
  25.6 12.6 %collective-permute-start.4 = (f32[288,256]{1,0:T(8,128)S(1)}, f32[288,256]{1,0:T(8,128)S(1)}, u32[]{:S(2)}, u32[]{:S(2)}) collective-permute-start(f32[288,256]{1,0:T(8,128)S(1)} %get-tuple-element.43), channel_id=1, source_target_pairs={{0,8},{4,12},{8,0},{12,4},{1,9},{5,13},{9,1},{13,5},{2,10},{6,14},... | collective-permute-start | bytes 884744 | tf_op jit(solution)/shard_map/ppermute | solution.py:569
  28.4 13.2 %collective-permute-start.8 = (f32[3,2,40,256]{3,2,1,0:T(8,128)S(1)}, f32[3,2,40,256]{3,2,1,0:T(8,128)S(1)}, u32[]{:S(2)}, u32[]{:S(2)}) collective-permute-start(f32[3,2,40,256]{3,2,1,0:T(8,128)S(1)} %get-tuple-element.52), channel_id=1, source_target_pairs={{0,1},{1,0},{2,3},{3,2},{4,5},{5,4},{6,7},{7,6},{8,9},{9,8},{10,11... | collective-permute-start | bytes 737288 | tf_op jit(solution)/shard_map/ppermute | solution.py:563
  33.1 13.3 %collective-permute-start.9 = (f32[3,2,40,256]{3,2,1,0:T(8,128)S(1)}, f32[3,2,40,256]{3,2,1,0:T(8,128)S(1)}, u32[]{:S(2)}, u32[]{:S(2)}) collective-permute-start(f32[3,2,40,256]{3,2,1,0:T(8,128)S(1)} %get-tuple-element.53), channel_id=1, source_target_pairs={{1,2},{2,1},{5,6},{6,5},{9,10},{10,9},{13,14},{14,13},{17,18},{18,... | collective-permute-start | bytes 737288 | tf_op jit(solution)/shard_map/ppermute | solution.py:564
  33.9 17.2 %collective-permute-start.10 = (f32[8,40,256]{2,1,0:T(8,128)S(1)}, f32[8,40,256]{2,1,0:T(8,128)S(1)}, u32[]{:S(2)}, u32[]{:S(2)}) collective-permute-start(f32[8,40,256]{2,1,0:T(8,128)S(1)} %get-tuple-element.54), channel_id=1, source_target_pairs={{0,1},{1,0},{2,3},{3,2},{4,5},{5,4},{6,7},{7,6},{8,9},{9,8},{10,11... | collective-permute-start | bytes 983048 | tf_op jit(solution)/shard_map/ppermute | solution.py:563
  38.2 12.9 %collective-permute-start.11 = (f32[8,40,256]{2,1,0:T(8,128)S(1)}, f32[8,40,256]{2,1,0:T(8,128)S(1)}, u32[]{:S(2)}, u32[]{:S(2)}) collective-permute-start(f32[8,40,256]{2,1,0:T(8,128)S(1)} %get-tuple-element.55), channel_id=1, source_target_pairs={{1,2},{2,1},{5,6},{6,5},{9,10},{10,9},{13,14},{14,13},{17,18},{18,... | collective-permute-start | bytes 983048 | tf_op jit(solution)/shard_map/ppermute | solution.py:564
  41.5 11.9 %collective-permute-start.6 = (f32[3,6,40,256]{3,2,1,0:T(8,128)S(1)}, f32[3,6,40,256]{3,2,1,0:T(8,128)S(1)}, u32[]{:S(2)}, u32[]{:S(2)}) collective-permute-start(f32[3,6,40,256]{3,2,1,0:T(8,128)S(1)} %get-tuple-element.48), channel_id=1, source_target_pairs={{0,4},{4,0},{8,12},{12,8},{1,5},{5,1},{9,13},{13,9},{2,6},{6,2},{1... | collective-permute-start | bytes 2211848 | tf_op jit(solution)/shard_map/ppermute | solution.py:569
  41.6 9.5 %collective-permute-start.12 = (f32[2,2,40,256]{3,2,1,0:T(8,128)S(1)}, f32[2,2,40,256]{3,2,1,0:T(8,128)S(1)}, u32[]{:S(2)}, u32[]{:S(2)}) collective-permute-start(f32[2,2,40,256]{3,2,1,0:T(8,128)S(1)} %get-tuple-element.56), channel_id=1, source_target_pairs={{0,1},{1,0},{2,3},{3,2},{4,5},{5,4},{6,7},{7,6},{8,9},{9,8},{10,11... | collective-permute-start | bytes 491528 | tf_op jit(solution)/shard_map/ppermute | solution.py:563
  46.3 4.8 %collective-permute-start.13 = (f32[2,2,40,256]{3,2,1,0:T(8,128)S(1)}, f32[2,2,40,256]{3,2,1,0:T(8,128)S(1)}, u32[]{:S(2)}, u32[]{:S(2)}) collective-permute-start(f32[2,2,40,256]{3,2,1,0:T(8,128)S(1)} %get-tuple-element.57), channel_id=1, source_target_pairs={{1,2},{2,1},{5,6},{6,5},{9,10},{10,9},{13,14},{14,13},{17,18},{18,... | collective-permute-start | bytes 491528 | tf_op jit(solution)/shard_map/ppermute | solution.py:564
  53.3 2.5 %collective-permute-start.14 = (f32[3,4,40,256]{3,2,1,0:T(8,128)S(1)}, f32[3,4,40,256]{3,2,1,0:T(8,128)S(1)}, u32[]{:S(2)}, u32[]{:S(2)}) collective-permute-start(f32[3,4,40,256]{3,2,1,0:T(8,128)S(1)} %get-tuple-element.60), channel_id=1, source_target_pairs={{0,4},{4,0},{8,12},{12,8},{1,5},{5,1},{9,13},{13,9},{2,6},{6,2},{1... | collective-permute-start | bytes 1474568 | tf_op jit(solution)/shard_map/ppermute | solution.py:569
  55.2 2.7 %collective-permute-start.7 = (f32[3,4,32,256]{3,2,1,0:T(8,128)S(1)}, f32[3,4,32,256]{3,2,1,0:T(8,128)S(1)}, u32[]{:S(2)}, u32[]{:S(2)}) collective-permute-start(f32[3,4,32,256]{3,2,1,0:T(8,128)S(1)} %get-tuple-element.51), channel_id=1, source_target_pairs={{0,4},{4,0},{8,12},{12,8},{1,5},{5,1},{9,13},{13,9},{2,6},{6,2},{1... | collective-permute-start | bytes 1179656 | tf_op jit(solution)/shard_map/ppermute | solution.py:569
  57.9 1.8 %collective-permute-start.15 = (f32[3,4,32,256]{3,2,1,0:T(8,128)S(1)}, f32[3,4,32,256]{3,2,1,0:T(8,128)S(1)}, u32[]{:S(2)}, u32[]{:S(2)}) collective-permute-start(f32[3,4,32,256]{3,2,1,0:T(8,128)S(1)} %get-tuple-element.64), channel_id=1, source_target_pairs={{0,4},{4,0},{8,12},{12,8},{1,5},{5,1},{9,13},{13,9},{2,6},{6,2},{1... | collective-permute-start | bytes 1179656 | tf_op jit(solution)/shard_map/ppermute | solution.py:569
  58.0 12.1 %collective-permute-start.16 = (f32[3,4,32,256]{3,2,1,0:T(8,128)S(1)}, f32[3,4,32,256]{3,2,1,0:T(8,128)S(1)}, u32[]{:S(2)}, u32[]{:S(2)}) collective-permute-start(f32[3,4,32,256]{3,2,1,0:T(8,128)S(1)} %shard_map.49), channel_id=1, source_target_pairs={{0,8},{4,12},{8,0},{12,4},{1,9},{5,13},{9,1},{13,5},{2,10},{6,14},... | collective-permute-start | bytes 1179656 | tf_op jit(solution)/shard_map/ppermute | solution.py:569
  59.7 18.3 %collective-permute-start.17 = (f32[3,4,32,256]{3,2,1,0:T(8,128)S(1)}, f32[3,4,32,256]{3,2,1,0:T(8,128)S(1)}, u32[]{:S(2)}, u32[]{:S(2)}) collective-permute-start(f32[3,4,32,256]{3,2,1,0:T(8,128)S(1)} %shard_map.51), channel_id=1, source_target_pairs={{0,8},{4,12},{8,0},{12,4},{1,9},{5,13},{9,1},{13,5},{2,10},{6,14},... | collective-permute-start | bytes 1179656 | tf_op jit(solution)/shard_map/ppermute | solution.py:569

commit v4 on v3

--- a/solution.py
+++ b/solution.py
@@ -50,11 +50,17 @@
 
 
 def shift_lanes(a, step):
-    width = a.shape[1]
-    lane = lax.broadcasted_iota(jnp.int32, a.shape, 1)
-    moved = pltpu.roll(a, (-step) % width, 1)
-    keep = lane < width - step if step > 0 else lane >= -step
-    return jnp.where(keep, moved, 0.0)
+    lanes = 128
+    count = a.shape[1] // lanes
+    lane = lax.broadcasted_iota(jnp.int32, (a.shape[0], lanes), 1)
+    turned = [pltpu.roll(a[:, c * lanes : (c + 1) * lanes], (-step) % lanes, 1) for c in range(count)]
+    edge = lane >= lanes - step if step > 0 else lane < -step
+    ahead = 1 if step > 0 else -1
+    cols = []
+    for c in range(count):
+        beyond = turned[c + ahead] if 0 <= c + ahead < count else 0.0
+        cols.append(jnp.where(edge, beyond, turned[c]))
+    return jnp.concatenate(cols, 1)
 
 
 def halve_kernel(fine, part, edge, buf_a, buf_b, held, mat, rows, prev, sems):
@@ -122,27 +128,36 @@
         buf_b[i] = jnp.where(parity == 0, below, above)
 
 
-def pack(dst, layer, count, chip, half):
-    low = lax.broadcasted_iota(jnp.int32, (8, dst.shape[1]), 0) < 4
-    mine = low == (chip == 0)
+def slots(keep, chip, cols):
+    group = 8 // keep
+    slot = lax.broadcasted_iota(jnp.int32, (8, cols), 0) // keep
+    return jnp.where(chip == 0, slot, (slot + 1) % group)
+
+
+def pack(dst, layer, count, chip, half, keep):
+    which = slots(keep, chip, dst.shape[1])
     main = pl.multiple_of(8 * chip, 8)
     rim = pl.multiple_of(half * (1 - chip), 8)
+    group = 8 // keep
     for i in range(count):
         dst[pl.ds(i * half, half), :] = layer(i, main, half)
-    for i in range(0, count, 2):
-        a, b = layer(i, rim, 8), layer(i + 1, rim, 8)
-        dst[pl.ds(count * half + 4 * i, 8), :] = jnp.where(mine, a, pltpu.roll(b, 4, 0))
-
-
-def unpack(src, store, count, chip, half):
+    for i in range(0, count, group):
+        tile = layer(i, rim, 8)
+        for g in range(1, group):
+            tile = jnp.where(which == g, pltpu.roll(layer(i + g, rim, 8), keep * g, 0), tile)
+        dst[pl.ds(count * half + keep * i, 8), :] = tile
+
+
+def unpack(src, store, count, chip, half, keep):
     main = pl.multiple_of(8 * chip, 8)
     rim = pl.multiple_of(half * (1 - chip), 8)
+    group = 8 // keep
     for i in range(count):
         store(i, main, half, src[pl.ds(i * half, half), :])
-    for i in range(0, count, 2):
-        v = src[pl.ds(count * half + 4 * i, 8), :]
-        store(i, rim, 8, v)
-        store(i + 1, rim, 8, pltpu.roll(v, 4, 0))
+    for i in range(0, count, group):
+        v = src[pl.ds(count * half + keep * i, 8), :]
+        for g in range(group):
+            store(i + g, rim, 8, v if g == 0 else pltpu.roll(v, 8 - keep * g, 0))
 
 
 def join_kernel(part, edge, got_a, got_b, ext, near, far):
@@ -173,7 +188,7 @@
     def layer(i, start, size):
         return ext[i + 2, pl.ds(pl.multiple_of(there + start, 8), size), :]
 
-    pack(far, layer, n + 2, 1 - x, ext.shape[1] // 2)
+    pack(far, layer, n + 2, 1 - x, ext.shape[1] // 2, 4)
 
 
 def warp_kernel(ext, offs, near, far, wide, full):
@@ -184,33 +199,38 @@
 
     def fill(z, carry):
         v = ext[z + 1]
-        for s in range(5):
-            moved = v if s == 2 else shift_lanes(v, s - 2)
+        whole = [v if k == 0 else shift_lanes(v, k) for k in range(-2, 3)]
+        for k in range(5):
+            moved = whole[0] if k == 0 else whole[k] - whole[k - 1]
             for c in range(columns):
-                wide[s, c, z, pl.ds(0, 8), :] = blank
-                wide[s, c, z, pl.ds(8, tall), :] = moved[:, c * lanes : (c + 1) * lanes]
-                wide[s, c, z, pl.ds(8 + tall, 8), :] = blank
+                wide[k, c, z, pl.ds(0, 8), :] = blank
+                wide[k, c, z, pl.ds(8, tall), :] = moved[:, c * lanes : (c + 1) * lanes]
+                wide[k, c, z, pl.ds(8 + tall, 8), :] = blank
         return carry
 
     lax.fori_loop(0, depth, fill, 0)
 
+    def shares(comp, z, y, c):
+        h = offs[comp, z, pl.ds(y, 8), pl.ds(c * lanes, lanes)].astype(F32) * 0.5
+        return [jnp.minimum(jnp.maximum(h - k, 0.0), 1.0) for k in range(-2, 2)]
+
     def weights(comp, z, y, c):
-        h = offs[comp, z, pl.ds(y, 8), pl.ds(c * lanes, lanes)].astype(F32) * 0.5
-        return [jnp.maximum(1.0 - jnp.abs(h - (s - 2.0)), 0.0) for s in range(5)]
+        s = shares(comp, z, y, c)
+        return [1.0 - s[0], s[0] - s[1], s[1] - s[2], s[2] - s[3], s[3]]
 
     def tile(i, carry):
         z = i // (tall // 8)
         y = pl.multiple_of((i % (tall // 8)) * 8, 8)
         for c in range(columns):
-            wz, wy, wx = (weights(m, z, y, c) for m in range(3))
+            wz, wy = weights(0, z, y, c), weights(1, z, y, c)
+            sx = shares(2, z, y, c)
             total = None
             for a in range(5):
                 plane = None
                 for b in range(5):
-                    line = None
-                    for s in range(5):
-                        term = wx[s] * wide[s, c, z + a, pl.ds(y + 6 + b, 8), :]
-                        line = term if line is None else line + term
+                    line = wide[0, c, z + a, pl.ds(y + 6 + b, 8), :]
+                    for k in range(4):
+                        line += sx[k] * wide[k + 1, c, z + a, pl.ds(y + 6 + b, 8), :]
                     line = wy[b] * line
                     plane = line if plane is None else plane + line
                 plane = wz[a] * plane
@@ -228,7 +248,7 @@
     def layer(i, start, size):
         return full[i, pl.ds(pl.multiple_of(there + start, 8), size), :]
 
-    pack(far, layer, n, 1 - x, tall // 2)
+    pack(far, layer, n, 1 - x, tall // 2, 2)
 
 
 def cut_kernel(vel, far, held, sem):
@@ -243,7 +263,7 @@
     def layer(i, start, size):
         return held[i // n, i % n, pl.ds(start, size), :]
 
-    pack(far, layer, 3 * n, 1 - x, tall // 2)
+    pack(far, layer, 3 * n, 1 - x, tall // 2, 2)
 
 
 def rim_own_kernel(vel, buf_a, buf_b, stage, sem):
@@ -277,8 +297,8 @@
     def store_diag(i, start, size, v):
         diag[i, pl.ds(start, size), :] = v
 
-    unpack(vel_far, store_vel, 3 * n, x, half)
-    unpack(diag_far, store_diag, n + 2, x, half)
+    unpack(vel_far, store_vel, 3 * n, x, half, 2)
+    unpack(diag_far, store_diag, n + 2, x, half, 4)
     for comp in range(3):
         for i in range(2):
             below, above = vel_other[comp, i], vel_other[comp, n - 2 + i]
@@ -298,7 +318,7 @@
     def store(i, start, size, v):
         other[i, pl.ds(start, size), :] = v
 
-    unpack(far, store, n, x, span - RIM)
+    unpack(far, store, n, x, span - RIM, 2)
     for m in range(2):
         ref = near if m == 0 else other
         for i in range(2):
@@ -324,24 +344,22 @@
 
 
 def smooth_plane(v):
-    v = (shift_rows(v, False) + 2.0 * v + shift_rows(v, True)) * 0.25
-    return (shift_lanes(v, -1) + 2.0 * v + shift_lanes(v, 1)) * 0.25
+    v = shift_rows(v, False) + (v + v) + shift_rows(v, True)
+    return shift_lanes(v, -1) + (v + v) + shift_lanes(v, 1)
 
 
 def blur(parts, rows=None):
     low, here, high = parts
-    v = smooth_plane((low + 2.0 * here + high) * 0.25)
+    v = smooth_plane((low + (here + here) + high) * (1.0 / 64.0))
     if rows is None:
         return v
     x, half = rows
     return jnp.where(x == 0, v[:half], v[v.shape[0] - half :])
 
 
-def first_mid_kernel(
-    vel, vel_other, warp, warp_other, chip, diag, moved, out, out_sum, targets
-):
+def first_own_kernel(vel, warp, chip, diag, moved, targets):
     x, core = chip_and_core()
-    n, span = vel_other.shape[1], vel_other.shape[2]
+    n, span = warp.shape[:2]
     start = pl.multiple_of(x * (vel.shape[2] - span), 8)
     for i in range(n + 2):
         a, b = chip[i + 2], diag[i]
@@ -349,22 +367,30 @@
         targets[1, i] = jnp.where(core == 0, b, a)
 
     def step(i, carry):
-        for m in range(2):
-            if m == 0:
-                v = [vel[comp, i, pl.ds(start, span), :] for comp in range(3)]
-            else:
-                v = [vel_other[comp, i] for comp in range(3)]
-            base = warp[i] if m == 0 else warp_other[i]
-            v = update(v, base, targets[m, i], targets[m, i + 1], targets[m, i + 2], None)
-            for comp in range(3):
-                moved[m, comp, i] = v[comp]
+        v = [vel[comp, i, pl.ds(start, span), :] for comp in range(3)]
+        v = update(v, warp[i], targets[0, i], targets[0, i + 1], targets[0, i + 2], None)
+        for comp in range(3):
+            moved[comp, i] = v[comp]
+        return carry
+
+    lax.fori_loop(0, n, step, 0)
+
+
+def first_mid_kernel(vel_other, warp_other, moved_own, targets, moved, out, out_sum):
+    n = vel_other.shape[1]
+
+    def step(i, carry):
+        v = [vel_other[comp, i] for comp in range(3)]
+        v = update(v, warp_other[i], targets[1, i], targets[1, i + 1], targets[1, i + 2], None)
+        for comp in range(3):
+            moved[comp, i] = v[comp]
         return carry
 
     lax.fori_loop(0, n, step, 0)
 
     def smooth(i, carry):
         for comp in range(3):
-            both = [blur([moved[m, comp, i + k] for k in range(3)]) for m in range(2)]
+            both = [blur([ref[comp, i + k] for k in range(3)]) for ref in (moved_own, moved)]
             for m in range(2):
                 out[m, comp, i] = both[m]
             out_sum[comp, i] = both[0] + both[1]
@@ -374,12 +400,12 @@
 
 
 def first_rim_kernel(
-    own_a, own_b, rim_a, rim_b, warp_a, warp_b, chip, diag, mid,
+    own_a, own_b, rim_a, rim_b, warp_a, warp_b, chip, diag, mid_own, mid_other,
     out, out_sum, targets, held, base, moved,
 ):
     _, core = chip_and_core()
     parity, has_below, has_above = slab_place()
-    n = mid.shape[2]
+    n = mid_own.shape[1]
     for k in range(5):
         low = pick(parity, rim_a[6 + k], rim_b[6 + k], False) if k < 2 else diag[k - 2]
         high = pick(parity, rim_a[3 + k], rim_b[3 + k], True) if k > 2 else diag[n - 1 + k]
@@ -398,7 +424,8 @@
                     else:
                         a, b = rim_a[2 * comp + r], rim_b[2 * comp + r]
                     held[m, comp, e] = pick(parity, a, b, side == 1)
-                    moved[side, m, comp, r + 2 * (1 - side)] = mid[m, comp, (n - 2) * side + r]
+                    mid = mid_own if m == 0 else mid_other
+                    moved[side, m, comp, r + 2 * (1 - side)] = mid[comp, (n - 2) * side + r]
 
     def step(j, carry):
         m, e = j // 4, j % 4
@@ -584,7 +611,7 @@
 
     (vel_cut,) = launch(
         cut_kernel,
-        [shape(3 * n * (half + 4), cols)],
+        [shape(3 * n * (half + 2), cols)],
         [vel],
         [pltpu.VMEM((3, n, span, cols), F32), dma],
         hbm=(0,),
@@ -625,7 +652,7 @@
 
     warp, warp_cut = launch(
         warp_kernel,
-        [shape(n, span, cols), shape(n * (half + 4), cols)],
+        [shape(n, span, cols), shape(n * (half + 2), cols)],
         [ext, offs],
         [
             pltpu.VMEM((5, cols // lanes, n + 4, rows + 16, lanes), F32),
@@ -648,22 +675,23 @@
     )
     warp_a, warp_b = swap_slabs(buf_a, buf_b)
 
-    moved, mid, mid_sum, targets = launch(
+    moved_own, targets = launch(
+        first_own_kernel,
+        [shape(3, n, span, cols), shape(2, n + 2, span, cols)],
+        [vel, warp, chip, diag],
+        micros=1.5,
+    )
+    moved, mid, mid_sum = launch(
         first_mid_kernel,
-        [
-            shape(2, 3, n, span, cols),
-            shape(2, 3, n - 2, span, cols),
-            shape(3, n - 2, span, cols),
-            shape(2, n + 2, span, cols),
-        ],
-        [vel, vel_other, warp, warp_other, chip, diag],
-        micros=3.3,
+        [shape(3, n, span, cols), shape(2, 3, n - 2, span, cols), shape(3, n - 2, span, cols)],
+        [vel_other, warp_other, moved_own, targets],
+        micros=2.0,
     )
     mid_beside = swap_phases(mid_sum, 1)
     rim, rim_sum, ends = launch(
         first_rim_kernel,
         [shape(2, 3, 4, span, cols), shape(3, 4, span, cols), shape(2, 2, 5, span, cols)],
-        [own_a, own_b, rim_a, rim_b, warp_a, warp_b, chip, diag, moved],
+        [own_a, own_b, rim_a, rim_b, warp_a, warp_b, chip, diag, moved_own, moved],
         [
             pltpu.VMEM((2, 3, 4, span, cols), F32),
             pltpu.VMEM((2, 4, span, cols), F32),

time: 79.6 us -> 78.6 us (0.987)
    pallas_call x16 -> x17, Pallas kernels: 26.7 us -> 26.4 us  [launch(): pl.pallas_call(body, out_shape=outs, in_specs=[pl.BlockSpec(memory_space=...]
where the time goes in v4:
time: 78.6 us; the launch traced here: 77.8 us
  Pallas kernels  26.4 us (34%)
  starting transfers between devices  25.9 us (33%)
  waiting for transfers between devices  25.2 us (32%)
    pallas_call x17, Pallas kernels, launch(): pl.pallas_call(body, out_shape=outs, in_specs=[pl.BlockSpec(memory_space=...  26.4 us
    ppermute x10, waiting for transfers between devices, swap_phases(): lax.ppermute(values, 'phase', [(i, i ^ mask) for i in range(lax.axis_size...  15.6 us
    ppermute x4, starting transfers between devices, swap_slabs(): got_a = lax.ppermute(buf_a, 'slab', swaps(count, 0))  14.1 us
    ppermute x4, waiting for transfers between devices, swap_slabs(): got_a = lax.ppermute(buf_a, 'slab', swaps(count, 0))  9.64 us
    ppermute x10, starting transfers between devices, swap_phases(): lax.ppermute(values, 'phase', [(i, i ^ mask) for i in range(lax.axis_size...  9.19 us
    ppermute x4, starting transfers between devices, swap_slabs(): got_b = lax.ppermute(buf_b, 'slab', swaps(count, 1))  2.66 us
  transfers between devices with their start and end apart: 18, of which 6 were waited for; matrix products, arithmetic and copies ran while one was open for 0% of the time, Pallas kernels for 31%

profile of v4, /device:TPU:0, one launch (start us, length us, event | category | flops | bytes accessed | tf_op | source)
XLA Modules:
  0.0 77.8 jit_solution(6920461709645552193)
XLA Ops:
  0.0 1.3 %shard_map.37 = f32[816,256]{1,0:T(8,128)S(1)} custom-call(f32[3,8,64,256]{3,2,1,0:T(8,128)} %bitcast.4), custom_call_target="tpu_custom_call" | custom-call | bytes 3300000 | tf_op jit(solution)/shard_map/pallas_call | solution.py:18
  1.3 3.0 %collective-permute-start = (f32[816,256]{1,0:T(8,128)S(1)}, f32[816,256]{1,0:T(8,128)S(1)}, u32[]{:S(2)}, u32[]{:S(2)}) collective-permute-start(f32[816,256]{1,0:T(8,128)S(1)} %shard_map.37), channel_id=1, source_target_pairs={{0,8},{4,12},{8,0},{12,4},{1,9},{5,13},{9,1},{13,5},{2,10},{6,14},... | collective-permute-start | bytes 2506760 | tf_op jit(solution)/shard_map/ppermute | solution.py:596
  4.3 0.0 copy-start.1
  4.3 4.2 %shard_map.38 = (f32[8,64,256]{2,1,0:T(8,128)S(1)}, f32[2,64,256]{2,1,0:T(8,128)S(1)}, f32[4,64,256]{2,1,0:T(8,128)S(1)}, f32[4,64,256]{2,1,0:T(8,128)S(1)}) custom-call(f32[16,128,512]{2,1,0:T(8,128)} %bitcast.8), custom_call_target="tpu_custom_call" | custom-call | bytes 13200000 | tf_op jit(solution)/shard_map/pallas_call | solution.py:18
  8.5 1.6 %collective-permute-start.1 = (f32[4,64,256]{2,1,0:T(8,128)S(1)}, f32[4,64,256]{2,1,0:T(8,128)S(1)}, u32[]{:S(2)}, u32[]{:S(2)}) collective-permute-start(f32[4,64,256]{2,1,0:T(8,128)S(1)} %get-tuple-element.38), channel_id=1, source_target_pairs={{0,1},{1,0},{2,3},{3,2},{4,5},{5,4},{6,7},{7,6},{8,9},{9,8},{10,11... | collective-permute-start | bytes 786440 | tf_op jit(solution)/shard_map/ppermute | solution.py:590
  10.1 0.7 collective-permute-start.2
  10.8 5.5 %collective-permute-done.1.got_a = f32[4,64,256]{2,1,0:T(8,128)S(1)} collective-permute-done((f32[4,64,256]{2,1,0:T(8,128)S(1)}, f32[4,64,256]{2,1,0:T(8,128)S(1)}, u32[]{:S(2)}, u32[]{:S(2)}) %collective-permute-start.1) | collective-permute-done | bytes 262176 | tf_op jit(solution)/shard_map/ppermute | solution.py:590
  16.3 0.0 collective-permute-done.2.got_b
  16.3 0.2 shard_map.39
  16.5 0.1 collective-permute-start.5
  16.6 0.5 collective-permute-start.3
  17.0 0.0 copy-done.1
  17.0 7.8 %shard_map.41 = (f32[8,40,256]{2,1,0:T(8,128)S(1)}, f32[272,256]{1,0:T(8,128)S(1)}) custom-call(f32[14,64,256]{2,1,0:T(8,128)S(1)} %get-tuple-element.42.ext, s32[3,8,64,256]{3,2,1,0:T(8,128)S(1)} %bitcast.7), custom_call_target="tpu_custom_call" | custom-call | bytes 28050000 | tf_op jit(solution)/shard_map/pallas_call | solution.py:18
  24.8 0.0 copy-start
  24.9 1.7 %collective-permute-start.4 = (f32[272,256]{1,0:T(8,128)S(1)}, f32[272,256]{1,0:T(8,128)S(1)}, u32[]{:S(2)}, u32[]{:S(2)}) collective-permute-start(f32[272,256]{1,0:T(8,128)S(1)} %get-tuple-element.44), channel_id=1, source_target_pairs={{0,8},{4,12},{8,0},{12,4},{1,9},{5,13},{9,1},{13,5},{2,10},{6,14},... | collective-permute-start | bytes 835592 | tf_op jit(solution)/shard_map/ppermute | solution.py:596
  26.6 1.1 %shard_map.46 = (f32[3,2,40,256]{3,2,1,0:T(8,128)S(1)}, f32[3,2,40,256]{3,2,1,0:T(8,128)S(1)}) custom-call(f32[3,8,64,256]{3,2,1,0:T(8,128)} %bitcast.5), custom_call_target="tpu_custom_call" | custom-call | bytes 3300000 | tf_op jit(solution)/shard_map/pallas_call | solution.py:18
  27.7 4.7 %collective-permute-start.8 = (f32[3,2,40,256]{3,2,1,0:T(8,128)S(1)}, f32[3,2,40,256]{3,2,1,0:T(8,128)S(1)}, u32[]{:S(2)}, u32[]{:S(2)}) collective-permute-start(f32[3,2,40,256]{3,2,1,0:T(8,128)S(1)} %get-tuple-element.54), channel_id=1, source_target_pairs={{0,1},{1,0},{2,3},{3,2},{4,5},{5,4},{6,7},{7,6},{8,9},{9,8},{10,11... | collective-permute-start | bytes 737288 | tf_op jit(solution)/shard_map/ppermute | solution.py:590
  32.4 0.0 collective-permute-done.3.diag_far
  32.4 0.7 collective-permute-start.9
  33.0 0.0 collective-permute-done.vel_far
  33.0 0.2 shard_map.40
  33.2 3.1 %collective-permute-start.10 = (f32[8,40,256]{2,1,0:T(8,128)S(1)}, f32[8,40,256]{2,1,0:T(8,128)S(1)}, u32[]{:S(2)}, u32[]{:S(2)}) collective-permute-start(f32[8,40,256]{2,1,0:T(8,128)S(1)} %get-tuple-element.56), channel_id=1, source_target_pairs={{0,1},{1,0},{2,3},{3,2},{4,5},{5,4},{6,7},{7,6},{8,9},{9,8},{10,11... | collective-permute-start | bytes 983048 | tf_op jit(solution)/shard_map/ppermute | solution.py:590
  36.3 0.5 collective-permute-done.4.far
  36.8 0.7 collective-permute-start.11
  37.5 0.1 shard_map.42
  37.5 0.0 collective-permute-done.5.chip
  37.5 0.0 copy-done
  37.5 1.0 %shard_map.43 = (f32[3,8,40,256]{3,2,1,0:T(8,128)S(1)}, f32[2,10,40,256]{3,2,1,0:T(8,128)S(1)}) custom-call(f32[3,8,64,256]{3,2,1,0:T(8,128)S(1)} %bitcast.6, f32[8,40,256]{2,1,0:T(8,128)S(1)} %get-tuple-element.43.near.warp, f32[14,40,256]{2,1,0:T(8,128)S(1)} %collective-permute-done.5.chip, f32[10,40,256]{2,1,0:T(8,128)S(1)} %get-tuple-element.47.diag), custom_call_target="tpu_custom_call" | custom-call | bytes 4950000 | tf_op jit(solution)/shard_map/pallas_call | solution.py:18
  38.6 2.2 %shard_map.44 = (f32[3,8,40,256]{3,2,1,0:T(8,128)S(1)}, f32[2,3,6,40,256]{4,3,2,1,0:T(8,128)S(1)}, f32[3,6,40,256]{3,2,1,0:T(8,128)S(1)}) custom-call(f32[3,8,40,256]{3,2,1,0:T(8,128)S(1)} %get-tuple-element.41.vel_other, f32[8,40,256]{2,1,0:T(8,128)S(1)} %get-tuple-element.45.warp_other, f32[3,8,40,256]{3,2,1,0:T(8,128)S(1)} %get-tuple-element.48.moved_own.mid_own, ...), custom_call_target="tpu_custom_call" | custom-call | bytes 6600000 | tf_op jit(solution)/shard_map/pallas_call | solution.py:18
  40.8 0.1 collective-permute-start.6
  40.8 0.0 collective-permute-done.8.own_a
  40.8 4.7 %collective-permute-start.12 = (f32[2,2,40,256]{3,2,1,0:T(8,128)S(1)}, f32[2,2,40,256]{3,2,1,0:T(8,128)S(1)}, u32[]{:S(2)}, u32[]{:S(2)}) collective-permute-start(f32[2,2,40,256]{3,2,1,0:T(8,128)S(1)} %get-tuple-element.58), channel_id=1, source_target_pairs={{0,1},{1,0},{2,3},{3,2},{4,5},{5,4},{6,7},{7,6},{8,9},{9,8},{10,11... | collective-permute-start | bytes 491528 | tf_op jit(solution)/shard_map/ppermute | solution.py:590
  45.5 0.0 collective-permute-done.9.own_b
  45.5 0.7 collective-permute-start.13
  46.2 4.1 %collective-permute-done.12.warp_a = f32[2,2,40,256]{3,2,1,0:T(8,128)S(1)} collective-permute-done((f32[2,2,40,256]{3,2,1,0:T(8,128)S(1)}, f32[2,2,40,256]{3,2,1,0:T(8,128)S(1)}, u32[]{:S(2)}, u32[]{:S(2)}) %collective-permute-start.12) | collective-permute-done | bytes 163872 | tf_op jit(solution)/shard_map/ppermute | solution.py:590
  50.3 0.0 collective-permute-done.13.warp_b
  50.3 0.0 collective-permute-done.10.rim_a
  50.3 0.0 collective-permute-done.11.rim_b
  50.3 2.1 %shard_map.47 = (f32[2,3,4,40,256]{4,3,2,1,0:T(8,128)S(1)}, f32[3,4,40,256]{3,2,1,0:T(8,128)S(1)}, f32[2,2,5,40,256]{4,3,2,1,0:T(8,128)S(1)}) custom-call(f32[3,2,40,256]{3,2,1,0:T(8,128)S(1)} %collective-permute-done.8.own_a, f32[3,2,40,256]{3,2,1,0:T(8,128)S(1)} %collective-permute-done.9.own_b, f32[8,40,256]{2,1,0:T(8,128)S(1)} %collective-permute-done.10.rim_a, ...), custom_call_target="tpu_custom_call" | custom-call | bytes 6600000 | tf_op jit(solution)/shard_map/pallas_call | solution.py:18
  52.5 0.1 collective-permute-start.14
  52.5 0.0 collective-permute-done.6.beside
  52.6 1.8 %shard_map.45 = (f32[2,3,6,40,256]{4,3,2,1,0:T(8,128)S(1)}, f32[2,3,4,32,256]{4,3,2,1,0:T(8,128)S(1)}, f32[3,4,32,256]{3,2,1,0:T(8,128)S(1)}) custom-call(f32[2,3,6,40,256]{4,3,2,1,0:T(8,128)S(1)} %get-tuple-element.50.vel, f32[3,6,40,256]{3,2,1,0:T(8,128)S(1)} %collective-permute-done.6.beside, f32[8,40,256]{2,1,0:T(8,128)S(1)} %get-tuple-element.43.near.warp, ...), custom_call_target="tpu_custom_call" | custom-call | bytes 8250000 | tf_op jit(solution)/shard_map/pallas_call | solution.py:18
  54.3 0.5 collective-permute-start.7
  54.9 0.0 collective-permute-done.14.beside
  54.9 2.0 %shard_map.48 = (f32[2,3,4,32,256]{4,3,2,1,0:T(8,128)S(1)}, f32[3,4,32,256]{3,2,1,0:T(8,128)S(1)}) custom-call(f32[2,3,4,40,256]{4,3,2,1,0:T(8,128)S(1)} %get-tuple-element.61.vel, f32[3,4,40,256]{3,2,1,0:T(8,128)S(1)} %collective-permute-done.14.beside, f32[8,40,256]{2,1,0:T(8,128)S(1)} %get-tuple-element.43.near.warp, ...), custom_call_target="tpu_custom_call" | custom-call | bytes 6600000 | tf_op jit(solution)/shard_map/pallas_call | solution.py:18
  56.9 0.1 collective-permute-start.15
  57.0 0.0 collective-permute-done.7.mid_beside.beside
  57.0 1.6 %collective-permute-start.16 = (f32[3,4,32,256]{3,2,1,0:T(8,128)S(1)}, f32[3,4,32,256]{3,2,1,0:T(8,128)S(1)}, u32[]{:S(2)}, u32[]{:S(2)}) collective-permute-start(f32[3,4,32,256]{3,2,1,0:T(8,128)S(1)} %shard_map.50), channel_id=1, source_target_pairs={{0,8},{4,12},{8,0},{12,4},{1,9},{5,13},{9,1},{13,5},{2,10},{6,14},... | collective-permute-start | bytes 1179656 | tf_op jit(solution)/shard_map/ppermute | solution.py:596
  58.6 0.1 collective-permute-done.15.rim_beside.beside
  58.7 1.6 %collective-permute-start.17 = (f32[3,4,32,256]{3,2,1,0:T(8,128)S(1)}, f32[3,4,32,256]{3,2,1,0:T(8,128)S(1)}, u32[]{:S(2)}, u32[]{:S(2)}) collective-permute-start(f32[3,4,32,256]{3,2,1,0:T(8,128)S(1)} %shard_map.52), channel_id=1, source_target_pairs={{0,8},{4,12},{8,0},{12,4},{1,9},{5,13},{9,1},{13,5},{2,10},{6,14},... | collective-permute-start | bytes 1179656 | tf_op jit(solution)/shard_map/ppermute | solution.py:596
  60.3 1.0 %shard_map.49.done = f32[3,8,64,256]{3,2,1,0:T(8,128)} custom-call(f32[2,3,4,32,256]{4,3,2,1,0:T(8,128)S(1)} %get-tuple-element.52.mid.vel, f32[3,4,32,256]{3,2,1,0:T(8,128)S(1)} %collective-permute-done.7.mid_beside.beside, f32[2,3,4,32,256]{4,3,2,1,0:T(8,128)S(1)} %get-tuple-element.65.rim.vel, f32[3,4,32,256]{3,2,1,0:T(8,128)S(1)} %collective-permute-done.15.rim_beside.beside), custom_call_target="tpu_custom_call" | custom-call | bytes 3300000 | tf_op jit(solution)/shard_map/pallas_call | solution.py:18
  61.3 7.8 %collective-permute-done.16.home = f32[3,4,32,256]{3,2,1,0:T(8,128)S(1)} collective-permute-done((f32[3,4,32,256]{3,2,1,0:T(8,128)S(1)}, f32[3,4,32,256]{3,2,1,0:T(8,128)S(1)}, u32[]{:S(2)}, u32[]{:S(2)}) %collective-permute-start.16) | collective-permute-done | bytes 393248 | tf_op jit(solution)/shard_map/ppermute | solution.py:596
  69.1 0.8 shard_map.51.done
  69.8 7.2 %collective-permute-done.17.home = f32[3,4,32,256]{3,2,1,0:T(8,128)S(1)} collective-permute-done((f32[3,4,32,256]{3,2,1,0:T(8,128)S(1)}, f32[3,4,32,256]{3,2,1,0:T(8,128)S(1)}, u32[]{:S(2)}, u32[]{:S(2)}) %collective-permute-start.17) | collective-permute-done | bytes 393248 | tf_op jit(solution)/shard_map/ppermute | solution.py:596
  77.0 0.8 shard_map.53
  (2 shorter events, 0.1 us)
Async XLA Ops:
  1.3 31.8 %collective-permute-start = (f32[816,256]{1,0:T(8,128)S(1)}, f32[816,256]{1,0:T(8,128)S(1)}, u32[]{:S(2)}, u32[]{:S(2)}) collective-permute-start(f32[816,256]{1,0:T(8,128)S(1)} %shard_map.37), channel_id=1, source_target_pairs={{0,8},{4,12},{8,0},{12,4},{1,9},{5,13},{9,1},{13,5},{2,10},{6,14},... | collective-permute-start | bytes 2506760 | tf_op jit(solution)/shard_map/ppermute | solution.py:596
  4.3 12.7 %copy-start.1 = (s32[1,3,8,64,256]{4,3,2,1,0:T(8,128)S(1)}, s32[1,3,8,64,256]{4,3,2,1,0:T(8,128)}, u32[]{:S(2)}) copy-start(s32[1,3,8,64,256]{4,3,2,1,0:T(8,128)} %param.4) | copy-start | bytes 4718596
  8.5 7.8 %collective-permute-start.1 = (f32[4,64,256]{2,1,0:T(8,128)S(1)}, f32[4,64,256]{2,1,0:T(8,128)S(1)}, u32[]{:S(2)}, u32[]{:S(2)}) collective-permute-start(f32[4,64,256]{2,1,0:T(8,128)S(1)} %get-tuple-element.38), channel_id=1, source_target_pairs={{0,1},{1,0},{2,3},{3,2},{4,5},{5,4},{6,7},{7,6},{8,9},{9,8},{10,11... | collective-permute-start | bytes 786440 | tf_op jit(solution)/shard_map/ppermute | solution.py:590
  10.1 6.2 %collective-permute-start.2 = (f32[4,64,256]{2,1,0:T(8,128)S(1)}, f32[4,64,256]{2,1,0:T(8,128)S(1)}, u32[]{:S(2)}, u32[]{:S(2)}) collective-permute-start(f32[4,64,256]{2,1,0:T(8,128)S(1)} %get-tuple-element.39), channel_id=1, source_target_pairs={{1,2},{2,1},{5,6},{6,5},{9,10},{10,9},{13,14},{14,13},{17,18},{18,... | collective-permute-start | bytes 786440 | tf_op jit(solution)/shard_map/ppermute | solution.py:591
  16.5 21.0 %collective-permute-start.5 = (f32[14,40,256]{2,1,0:T(8,128)S(1)}, f32[14,40,256]{2,1,0:T(8,128)S(1)}, u32[]{:S(2)}, u32[]{:S(2)}) collective-permute-start(f32[14,40,256]{2,1,0:T(8,128)S(1)} %get-tuple-element.46), channel_id=1, source_target_pairs={{0,4},{4,0},{8,12},{12,8},{1,5},{5,1},{9,13},{13,9},{2,6},{6,2},{1... | collective-permute-start | bytes 1720328 | tf_op jit(solution)/shard_map/ppermute | solution.py:596
  16.6 15.8 %collective-permute-start.3 = (f32[360,256]{1,0:T(8,128)S(1)}, f32[360,256]{1,0:T(8,128)S(1)}, u32[]{:S(2)}, u32[]{:S(2)}) collective-permute-start(f32[360,256]{1,0:T(8,128)S(1)} %get-tuple-element.40), channel_id=1, source_target_pairs={{0,12},{4,8},{8,4},{12,0},{1,13},{5,9},{9,5},{13,1},{2,14},{6,10},... | collective-permute-start | bytes 1105928 | tf_op jit(solution)/shard_map/ppermute | solution.py:596
  24.8 12.7 %copy-start = (f32[1,3,8,64,256]{4,3,2,1,0:T(8,128)S(1)}, f32[1,3,8,64,256]{4,3,2,1,0:T(8,128)}, u32[]{:S(2)}) copy-start(f32[1,3,8,64,256]{4,3,2,1,0:T(8,128)} %param.5) | copy-start | bytes 4718596
  24.9 11.9 %collective-permute-start.4 = (f32[272,256]{1,0:T(8,128)S(1)}, f32[272,256]{1,0:T(8,128)S(1)}, u32[]{:S(2)}, u32[]{:S(2)}) collective-permute-start(f32[272,256]{1,0:T(8,128)S(1)} %get-tuple-element.44), channel_id=1, source_target_pairs={{0,8},{4,12},{8,0},{12,4},{1,9},{5,13},{9,1},{13,5},{2,10},{6,14},... | collective-permute-start | bytes 835592 | tf_op jit(solution)/shard_map/ppermute | solution.py:596
  27.7 13.1 %collective-permute-start.8 = (f32[3,2,40,256]{3,2,1,0:T(8,128)S(1)}, f32[3,2,40,256]{3,2,1,0:T(8,128)S(1)}, u32[]{:S(2)}, u32[]{:S(2)}) collective-permute-start(f32[3,2,40,256]{3,2,1,0:T(8,128)S(1)} %get-tuple-element.54), channel_id=1, source_target_pairs={{0,1},{1,0},{2,3},{3,2},{4,5},{5,4},{6,7},{7,6},{8,9},{9,8},{10,11... | collective-permute-start | bytes 737288 | tf_op jit(solution)/shard_map/ppermute | solution.py:590
  32.4 13.2 %collective-permute-start.9 = (f32[3,2,40,256]{3,2,1,0:T(8,128)S(1)}, f32[3,2,40,256]{3,2,1,0:T(8,128)S(1)}, u32[]{:S(2)}, u32[]{:S(2)}) collective-permute-start(f32[3,2,40,256]{3,2,1,0:T(8,128)S(1)} %get-tuple-element.55), channel_id=1, source_target_pairs={{1,2},{2,1},{5,6},{6,5},{9,10},{10,9},{13,14},{14,13},{17,18},{18,... | collective-permute-start | bytes 737288 | tf_op jit(solution)/shard_map/ppermute | solution.py:591
  33.2 17.1 %collective-permute-start.10 = (f32[8,40,256]{2,1,0:T(8,128)S(1)}, f32[8,40,256]{2,1,0:T(8,128)S(1)}, u32[]{:S(2)}, u32[]{:S(2)}) collective-permute-start(f32[8,40,256]{2,1,0:T(8,128)S(1)} %get-tuple-element.56), channel_id=1, source_target_pairs={{0,1},{1,0},{2,3},{3,2},{4,5},{5,4},{6,7},{7,6},{8,9},{9,8},{10,11... | collective-permute-start | bytes 983048 | tf_op jit(solution)/shard_map/ppermute | solution.py:590
  36.8 13.6 %collective-permute-start.11 = (f32[8,40,256]{2,1,0:T(8,128)S(1)}, f32[8,40,256]{2,1,0:T(8,128)S(1)}, u32[]{:S(2)}, u32[]{:S(2)}) collective-permute-start(f32[8,40,256]{2,1,0:T(8,128)S(1)} %get-tuple-element.57), channel_id=1, source_target_pairs={{1,2},{2,1},{5,6},{6,5},{9,10},{10,9},{13,14},{14,13},{17,18},{18,... | collective-permute-start | bytes 983048 | tf_op jit(solution)/shard_map/ppermute | solution.py:591
  40.8 11.8 %collective-permute-start.6 = (f32[3,6,40,256]{3,2,1,0:T(8,128)S(1)}, f32[3,6,40,256]{3,2,1,0:T(8,128)S(1)}, u32[]{:S(2)}, u32[]{:S(2)}) collective-permute-start(f32[3,6,40,256]{3,2,1,0:T(8,128)S(1)} %get-tuple-element.51), channel_id=1, source_target_pairs={{0,4},{4,0},{8,12},{12,8},{1,5},{5,1},{9,13},{13,9},{2,6},{6,2},{1... | collective-permute-start | bytes 2211848 | tf_op jit(solution)/shard_map/ppermute | solution.py:596
  40.8 9.5 %collective-permute-start.12 = (f32[2,2,40,256]{3,2,1,0:T(8,128)S(1)}, f32[2,2,40,256]{3,2,1,0:T(8,128)S(1)}, u32[]{:S(2)}, u32[]{:S(2)}) collective-permute-start(f32[2,2,40,256]{3,2,1,0:T(8,128)S(1)} %get-tuple-element.58), channel_id=1, source_target_pairs={{0,1},{1,0},{2,3},{3,2},{4,5},{5,4},{6,7},{7,6},{8,9},{9,8},{10,11... | collective-permute-start | bytes 491528 | tf_op jit(solution)/shard_map/ppermute | solution.py:590
  45.5 4.8 %collective-permute-start.13 = (f32[2,2,40,256]{3,2,1,0:T(8,128)S(1)}, f32[2,2,40,256]{3,2,1,0:T(8,128)S(1)}, u32[]{:S(2)}, u32[]{:S(2)}) collective-permute-start(f32[2,2,40,256]{3,2,1,0:T(8,128)S(1)} %get-tuple-element.59), channel_id=1, source_target_pairs={{1,2},{2,1},{5,6},{6,5},{9,10},{10,9},{13,14},{14,13},{17,18},{18,... | collective-permute-start | bytes 491528 | tf_op jit(solution)/shard_map/ppermute | solution.py:591
  52.5 2.4 %collective-permute-start.14 = (f32[3,4,40,256]{3,2,1,0:T(8,128)S(1)}, f32[3,4,40,256]{3,2,1,0:T(8,128)S(1)}, u32[]{:S(2)}, u32[]{:S(2)}) collective-permute-start(f32[3,4,40,256]{3,2,1,0:T(8,128)S(1)} %get-tuple-element.62), channel_id=1, source_target_pairs={{0,4},{4,0},{8,12},{12,8},{1,5},{5,1},{9,13},{13,9},{2,6},{6,2},{1... | collective-permute-start | bytes 1474568 | tf_op jit(solution)/shard_map/ppermute | solution.py:596
  54.3 2.7 %collective-permute-start.7 = (f32[3,4,32,256]{3,2,1,0:T(8,128)S(1)}, f32[3,4,32,256]{3,2,1,0:T(8,128)S(1)}, u32[]{:S(2)}, u32[]{:S(2)}) collective-permute-start(f32[3,4,32,256]{3,2,1,0:T(8,128)S(1)} %get-tuple-element.53), channel_id=1, source_target_pairs={{0,4},{4,0},{8,12},{12,8},{1,5},{5,1},{9,13},{13,9},{2,6},{6,2},{1... | collective-permute-start | bytes 1179656 | tf_op jit(solution)/shard_map/ppermute | solution.py:596
  56.9 1.8 %collective-permute-start.15 = (f32[3,4,32,256]{3,2,1,0:T(8,128)S(1)}, f32[3,4,32,256]{3,2,1,0:T(8,128)S(1)}, u32[]{:S(2)}, u32[]{:S(2)}) collective-permute-start(f32[3,4,32,256]{3,2,1,0:T(8,128)S(1)} %get-tuple-element.66), channel_id=1, source_target_pairs={{0,4},{4,0},{8,12},{12,8},{1,5},{5,1},{9,13},{13,9},{2,6},{6,2},{1... | collective-permute-start | bytes 1179656 | tf_op jit(solution)/shard_map/ppermute | solution.py:596
  57.0 12.1 %collective-permute-start.16 = (f32[3,4,32,256]{3,2,1,0:T(8,128)S(1)}, f32[3,4,32,256]{3,2,1,0:T(8,128)S(1)}, u32[]{:S(2)}, u32[]{:S(2)}) collective-permute-start(f32[3,4,32,256]{3,2,1,0:T(8,128)S(1)} %shard_map.50), channel_id=1, source_target_pairs={{0,8},{4,12},{8,0},{12,4},{1,9},{5,13},{9,1},{13,5},{2,10},{6,14},... | collective-permute-start | bytes 1179656 | tf_op jit(solution)/shard_map/ppermute | solution.py:596
  58.7 18.3 %collective-permute-start.17 = (f32[3,4,32,256]{3,2,1,0:T(8,128)S(1)}, f32[3,4,32,256]{3,2,1,0:T(8,128)S(1)}, u32[]{:S(2)}, u32[]{:S(2)}) collective-permute-start(f32[3,4,32,256]{3,2,1,0:T(8,128)S(1)} %shard_map.52), channel_id=1, source_target_pairs={{0,8},{4,12},{8,0},{12,4},{1,9},{5,13},{9,1},{13,5},{2,10},{6,14},... | collective-permute-start | bytes 1179656 | tf_op jit(solution)/shard_map/ppermute | solution.py:596
